TPU v7x, 32 devices: a whole 2x2x4 slice. The times are simulated.
32 devices in a mesh: groups: 2 (over y), ctx: 4 (over z), fsdp: 4 (over x, core).
Axes of the slice: x: 2, y: 2, z: 4, core: 2. Of those that a mesh axis runs over, the one named last changes fastest.
Arguments:
- patches: bfloat16 [8, 1024, 1024], P(('groups', 'fsdp'), 'ctx'), parts along dimension 0, may hold values from -6 to 6
- segment_ids: int32 [8, 1024], P(('groups', 'fsdp'), 'ctx'), parts along dimension 0, may hold values from 0 to 15, never falling along the last dimension, each value on 1 to 768 neighbouring positions
- patch_rows: int32 [8, 1024], P(('groups', 'fsdp'), 'ctx'), parts along dimension 0, may hold values from 0 to 63
- patch_cols: int32 [8, 1024], P(('groups', 'fsdp'), 'ctx'), parts along dimension 0, may hold values from 0 to 63
- row_table: bfloat16 [64, 1024], replicated, may hold values from -3 to 3
- col_table: bfloat16 [64, 1024], replicated, may hold values from -3 to 3
- norm_gain: float32 [1024], replicated, may hold values from 0.1 to 1.9
- qkv_weight: bfloat16 [1024, 3072], P('fsdp'), may hold values from -5 to 5
- out_weight: bfloat16 [1024, 1024], P(None, 'fsdp'), may hold values from -0.1875 to 0.1875
Outputs:
- encoded: bfloat16 [8, 1024, 1024], P(('groups', 'fsdp'), 'ctx'), parts along dimension 0
There are 2 independent parts, one for each index of `groups`. A program takes and returns all parts, laid end to end along the dimension named above; an argument that names none is the same for every part. Nothing has to cross between parts.
All inputs are finite; a program needn't handle non-finite values.
Results may differ from a plain program's by a relative error of at most 0.0044.
The roundings to bfloat16 on the way count: a program that leaves them out, or rounds other values in their place, can miss the bound.
Values may be sent and summed in bfloat16 or wider, within the bound.
No kernel may reach another device: no remote copies, remote signals or barrier semaphores. Data moves between devices by JAX's collectives and lax.ppermute only.
A program may use at most 64 MiB of HBM per device.

v0:
```python
import functools

import jax
import jax.numpy as jnp
from jax import lax
from jax.experimental import pallas as pl
from jax.experimental.pallas import tpu as pltpu
from jax.sharding import PartitionSpec as P


HEADS = 16
floor_score = -1e30
epsilon = 1e-06
VM = pl.BlockSpec(memory_space=pltpu.VMEM)
SM = pl.BlockSpec(memory_space=pltpu.SMEM)
PAD = 16


def call(kernel, outs, args, specs, flops, scratch=()):
    moved = sum(a.size * a.dtype.itemsize for a in (*args, *outs))
    return pl.pallas_call(
        kernel,
        out_shape=outs,
        in_specs=specs,
        out_specs=[VM] * len(outs),
        scratch_shapes=scratch,
        cost_estimate=pl.CostEstimate(flops=flops, bytes_accessed=moved, transcendentals=0),
    )(*args)


def embed_kernel(patches, rows, cols, segs, row_table, col_table, gain, embedded, block):
    length, grid = patches.shape[0], row_table.shape[0]
    level = lax.broadcasted_iota(jnp.int32, (grid, length), 0)
    row_hot = jnp.where(rows[...] == level, 1.0, 0.0).T.astype(jnp.bfloat16)
    col_hot = jnp.where(cols[...] == level, 1.0, 0.0).T.astype(jnp.bfloat16)
    x = (
        patches[...].astype(jnp.float32)
        + jnp.dot(row_hot, row_table[...], preferred_element_type=jnp.float32)
        + jnp.dot(col_hot, col_table[...], preferred_element_type=jnp.float32)
    )
    embedded[...] = x
    centered = x - jnp.mean(x, axis=-1, keepdims=True)
    variance = jnp.mean(centered * centered, axis=-1, keepdims=True)
    block[:length, :] = (centered * lax.rsqrt(variance + epsilon) * gain[...]).astype(jnp.bfloat16)
    block[length:, :] = jnp.zeros((PAD, block.shape[1]), jnp.bfloat16)
    block[length:, :length] = jnp.broadcast_to(
        segs[...].astype(jnp.float32), (PAD, length)
    ).astype(jnp.bfloat16)


def qkv_kernel(slots, pieces, tile, scale, order, *refs):
    blocks, weights, outs = refs[:slots], refs[slots : slots + pieces], refs[slots + pieces :]
    q_outs, kv_out = outs[:-1], outs[-1]
    length = blocks[0].shape[0] - PAD
    depth, width = weights[0].shape
    third = width // 3

    for slot in range(slots):
        rows = pl.ds(slot * length, length)
        for first in range(0, width, tile):
            total = None
            for piece in range(pieces):
                lanes = pl.ds(pl.multiple_of(order[piece] * depth, depth), depth)
                part = jnp.dot(
                    blocks[slot][:length, lanes],
                    weights[piece][:, first : first + tile],
                    preferred_element_type=jnp.float32,
                )
                total = part if total is None else total + part
            total = total.astype(jnp.bfloat16)
            if first < third:
                q_outs[slot][:, first : first + tile] = total * jnp.bfloat16(scale)
            else:
                kv_out[rows, first - third : first - third + tile] = total
    kv_out[slots * length :, :] = jnp.zeros((PAD, 2 * third), jnp.bfloat16)
    for slot in range(slots):
        kv_out[pl.ds(slots * length + slot, 1), :length] = blocks[slot][length : length + 1, :length]


def attend_kernel(slots, slot, length, head, q, near, far, out, hot, gate):
    half = slots * length
    third = q.shape[1]
    level = lax.broadcasted_iota(jnp.int32, (128, length), 0).astype(jnp.float32)
    for side, keys in enumerate((near, far)):
        labels = keys[half:, :length].astype(jnp.float32)
        for j in range(slots):
            match = labels[j : j + 1, :] == level
            gate[pl.ds(side * half + j * length, length), :] = (
                jnp.where(match, 0.0, floor_score).T.astype(jnp.bfloat16)
            )
            if side == 0 and j == slot:
                hot[...] = jnp.where(match, 1.0, 0.0).T.astype(jnp.bfloat16)
    lane = lax.broadcasted_iota(jnp.int32, (length, 2 * head), 1)
    nt = (((1,), (1,)), ((), ()))
    ones = jnp.ones((half, 2 * head), jnp.bfloat16)

    def pair(index, carry):
        lanes = pl.ds(pl.multiple_of(index * 2 * head, 2 * head), 2 * head)
        values = pl.ds(pl.multiple_of(third + index * 2 * head, 2 * head), 2 * head)
        both = q[:, lanes]
        mixed = []
        for low in (True, False):
            mask = (lane < head) if low else (lane >= head)
            one = jnp.concatenate([jnp.where(mask, both, jnp.zeros_like(both)), hot[...]], axis=1)
            scores = [
                lax.dot_general(
                    one,
                    jnp.concatenate([keys[:half, lanes], gate[pl.ds(side * half, half), :]], axis=1),
                    nt,
                    preferred_element_type=jnp.float32,
                )
                for side, keys in enumerate((near, far))
            ]
            highest = jnp.maximum(
                jnp.max(scores[0], axis=-1, keepdims=True), jnp.max(scores[1], axis=-1, keepdims=True)
            )
            product = sum(
                jnp.dot(
                    jnp.exp(s - highest).astype(jnp.bfloat16),
                    jnp.concatenate([keys[:half, values], ones], axis=1),
                    preferred_element_type=jnp.float32,
                )
                for s, keys in zip(scores, (near, far))
            )
            mixed.append(product[:, : 2 * head] / product[:, 2 * head :])
        out[:, lanes] = jnp.where(lane < head, mixed[0], mixed[1]).astype(jnp.bfloat16)
        return carry

    lax.fori_loop(0, third // (2 * head), pair, 0)


def out_kernel(slots, pieces, places, order, embedded, *refs):
    contexts, weights, out, context = refs[:slots], refs[slots : slots + pieces], refs[-2], refs[-1]
    width = contexts[0].shape[1]
    for slot in range(slots):
        lanes = pl.ds(pl.multiple_of(places[slot] * width, width), width)
        context[:, lanes] = contexts[slot][...]
    span = weights[0].shape[1]
    for piece in range(pieces):
        lanes = pl.ds(pl.multiple_of(order[piece] * span, span), span)
        out[:, lanes] = (
            embedded[:, lanes]
            + jnp.dot(context[...], weights[piece][...], preferred_element_type=jnp.float32)
        ).astype(jnp.bfloat16)


def body(
    patches, segment_ids, patch_rows, patch_cols, row_table, col_table, norm_gain, qkv_weight, out_weight
):
    n, lanes = lax.axis_size("ctx"), lax.axis_size("fsdp")
    half, chips = n // 2, lanes // 2
    z, f = lax.axis_index("ctx"), lax.axis_index("fsdp")
    length, model = patches.shape[1:]
    head = model // HEADS
    group = model // half
    place = z % half

    def spread(j):
        pairs = []
        for a in range(n):
            for b in range(lanes):
                core = b % 2
                to_core = core if a // half == core else 1 - core
                to = core * half + (a % half + j) % half
                pairs.append((a * lanes + b, to * lanes + b - core + to_core))
        return pairs

    def along(value, by):
        return lax.ppermute(value, "fsdp", [(i, (i + 2 * by) % lanes) for i in range(lanes)])

    def partner(value):
        return lax.ppermute(value, "fsdp", [(i, i ^ 1) for i in range(lanes)])

    def gather(piece):
        own = [piece] + [along(piece, by) for by in range(1, chips)]
        return own + [partner(p) for p in own]

    sources = [2 * ((f // 2 - by) % chips) + f % 2 for by in range(chips)]
    order = jnp.stack(sources + [s ^ 1 for s in sources]).astype(jnp.int32)
    depth = qkv_weight.shape[0]
    share = jnp.concatenate(
        [
            lax.dynamic_slice(qkv_weight, (0, part * model + place * group), (depth, group))
            for part in range(3)
        ],
        axis=1,
    )
    weights = gather(share)

    shape = jax.ShapeDtypeStruct
    embedded, block = call(
        embed_kernel,
        [shape((length, model), jnp.float32), shape((length + PAD, model), jnp.bfloat16)],
        (
            patches[0],
            patch_rows,
            patch_cols,
            segment_ids,
            row_table,
            col_table,
            norm_gain.reshape(1, model),
        ),
        [VM] * 7,
        4 * length * row_table.shape[0] * model,
    )
    blocks = []
    for j in range(half):
        blocks.append(lax.ppermute(block, ("ctx", "fsdp"), spread(j)))
    *queries, kv = call(
        functools.partial(qkv_kernel, half, lanes, min(group, 256), 1.0 / head**0.5),
        [
            *[shape((length, group), jnp.bfloat16)] * half,
            shape((half * length + PAD, 2 * group), jnp.bfloat16),
        ],
        (order, *blocks, *weights),
        [SM] + [VM] * (half + lanes),
        2 * half * length * model * 3 * group,
    )
    other = partner(kv)
    out_weights = gather(out_weight)
    contexts = []
    for j in range(half):
        (context,) = call(
            functools.partial(attend_kernel, half, j, length, head),
            [shape((length, group), jnp.bfloat16)],
            (queries[j], kv, other),
            [VM] * 3,
            8 * length * half * length * 2 * group,
            scratch=[
                pltpu.VMEM((length, 128), jnp.bfloat16),
                pltpu.VMEM((2 * half * length, 128), jnp.bfloat16),
            ],
        )
        back = [(b, a) for a, b in spread(j)]
        contexts.append(lax.ppermute(context, ("ctx", "fsdp"), back))
    places = jnp.stack([(place + j) % half for j in range(half)]).astype(jnp.int32)
    (encoded,) = call(
        functools.partial(out_kernel, half, lanes),
        [shape((length, model), jnp.bfloat16)],
        (places, order, embedded, *contexts, *out_weights),
        [SM, SM] + [VM] * (1 + half + lanes),
        2 * length * model * model,
        scratch=[pltpu.VMEM((length, model), jnp.bfloat16)],
    )
    return encoded[None]


def solution(mesh):
    return jax.shard_map(
        body,
        mesh=mesh,
        in_specs=(
            P(("groups", "fsdp"), "ctx", None),
            P(("groups", "fsdp"), "ctx"),
            P(("groups", "fsdp"), "ctx"),
            P(("groups", "fsdp"), "ctx"),
            P(),
            P(),
            P(),
            P("fsdp", None),
            P(None, "fsdp"),
        ),
        out_specs=P(("groups", "fsdp"), "ctx", None),
        check_vma=False,
    )
```

profile of v0, /device:TPU:1, one launch (start us, length us, event | category | flops | bytes accessed | tf_op | source)
XLA Modules:
  0.0 107.2 jit_solution(14833338810959631202)
XLA Ops:
  0.0 1.2 %constant_dynamic-slice_fusion.2 = (bf16[256,512]{1,0:T(8,128)(2,1)S(1)}, bf16[256,512]{1,0:T(8,128)(2,1)S(1)}, bf16[256,512]{1,0:T(8,128)(2,1)S(1)}) fusion(bf16[256,3072]{1,0:T(8,128)(2,1)} %param.16, s32[]{:T(128)S(6)} %select_n.50, s32[]{:T(128)S(6)} %select_n.52, s32[]{:T(128)S(6)} %select_n.51), kind=kLoop, calls=%fused_computation.3 | loop fusion | bytes 1572876 | tf_op jit(solution)/shard_map/dynamic_slice | solution.py:183
  1.2 0.1 pad_maximum_fusion.refs_2_
  1.2 0.0 copy-start
  1.2 2.1 %collective-permute-start.2 = (bf16[256,1536]{1,0:T(8,128)(2,1)S(1)}, bf16[256,1536]{1,0:T(8,128)(2,1)S(1)}, u32[]{:S(2)}, u32[]{:S(2)}) collective-permute-start(bf16[256,1536]{1,0:T(8,128)(2,1)S(1)} %pad_maximum_fusion.refs_2_), channel_id=1, source_target_pairs={{0,2},{1,3},{2,0},{3,1},{4,6},{5,7},{6,4},{7,5},{8,10},{9,11},{10,... | collective-permute-start | bytes 2359304 | tf_op jit(solution)/shard_map/ppermute | solution.py:169
  3.3 1.0 collective-permute-start.3
  4.3 16.3 %collective-permute-done.2.refs_3_ = bf16[256,1536]{1,0:T(8,128)(2,1)S(1)} collective-permute-done((bf16[256,1536]{1,0:T(8,128)(2,1)S(1)}, bf16[256,1536]{1,0:T(8,128)(2,1)S(1)}, u32[]{:S(2)}, u32[]{:S(2)}) %collective-permute-start.2) | collective-permute-done | bytes 786464 | tf_op jit(solution)/shard_map/ppermute | solution.py:169
  20.6 0.0 copy-start.8
  20.6 1.3 %collective-permute-start.4 = (bf16[256,1536]{1,0:T(8,128)(2,1)S(1)}, bf16[256,1536]{1,0:T(8,128)(2,1)}, u32[]{:S(2)}, u32[]{:S(2)}) collective-permute-start(bf16[256,1536]{1,0:T(8,128)(2,1)S(1)} %collective-permute-done.2.refs_3_), channel_id=1, source_target_pairs={{0,1},{1,0},{2,3},{3,2},{4,5},{5,4},{6,7},{7,6},{8,9},{9,8},{10,11... | collective-permute-start | bytes 2359304 | tf_op jit(solution)/shard_map/ppermute | solution.py:172
  21.8 2.8 %shard_map.91 = (f32[256,1024]{1,0:T(8,128)}, bf16[272,1024]{1,0:T(8,128)(2,1)}) custom-call(bf16[256,1024]{1,0:T(8,128)(2,1)} %bitcast.9, s32[1,256]{1,0:T(1,128)} %rows.1, s32[1,256]{1,0:T(1,128)} %cols.1, s32[1,256]{1,0:T(1,128)} %segs.1, bf16[64,1024]{1,0:T(8,128)(2,1)} %row_table.1, bf16[64,1024]{1,0:T(8,128)(2,1)} %col_table.1, f32[1,1024]{1,0:T(1,128)} %bitcast.10), custom_call_target="tpu_custom_call" | custom-call | flops 67108864 | bytes 2399232 | tf_op jit(solution)/shard_map/pallas_call | solution.py:21
  24.7 4.6 %collective-permute-start = (bf16[272,1024]{1,0:T(8,128)(2,1)}, bf16[272,1024]{1,0:T(8,128)(2,1)S(1)}, u32[]{:S(2)}, u32[]{:S(2)}) collective-permute-start(bf16[272,1024]{1,0:T(8,128)(2,1)} %get-tuple-element.11), channel_id=1, source_target_pairs={{0,0},{1,8},{2,2},{3,10},{4,4},{5,12},{6,6},{7,14},{8,1},{9,9},{10... | collective-permute-start | bytes 1671176 | tf_op jit(solution)/shard_map/ppermute | solution.py:208
  29.3 1.2 %collective-permute-start.1 = (bf16[272,1024]{1,0:T(8,128)(2,1)}, bf16[272,1024]{1,0:T(8,128)(2,1)}, u32[]{:S(2)}, u32[]{:S(2)}) collective-permute-start(bf16[272,1024]{1,0:T(8,128)(2,1)} %get-tuple-element.11), channel_id=1, source_target_pairs={{0,4},{1,12},{2,6},{3,14},{4,0},{5,8},{6,2},{7,10},{8,5},{9,13},{1... | collective-permute-start | bytes 1671176 | tf_op jit(solution)/shard_map/ppermute | solution.py:208
  30.5 0.7 pad_add_fusion.1.order
  31.2 0.0 copy-start.1
  31.2 10.4 %collective-permute-done.refs_0_ = bf16[272,1024]{1,0:T(8,128)(2,1)S(1)} collective-permute-done((bf16[272,1024]{1,0:T(8,128)(2,1)}, bf16[272,1024]{1,0:T(8,128)(2,1)S(1)}, u32[]{:S(2)}, u32[]{:S(2)}) %collective-permute-start) | collective-permute-done | bytes 557088 | tf_op jit(solution)/shard_map/ppermute | solution.py:208
  41.6 0.0 copy-start.10
  41.6 7.8 %collective-permute-done.1.refs_1_ = bf16[272,1024]{1,0:T(8,128)(2,1)} collective-permute-done((bf16[272,1024]{1,0:T(8,128)(2,1)}, bf16[272,1024]{1,0:T(8,128)(2,1)}, u32[]{:S(2)}, u32[]{:S(2)}) %collective-permute-start.1) | collective-permute-done | bytes 557088 | tf_op jit(solution)/shard_map/ppermute | solution.py:208
  49.4 0.0 collective-permute-done.3.refs_4_
  49.4 0.0 copy-start.9
  49.4 0.0 collective-permute-done.4.refs_5_
  49.4 0.0 copy-done
  49.4 0.0 copy-done.8
  49.4 0.0 copy-done.10
  49.4 0.9 copy-done.9
  50.3 5.0 %shard_map.92 = (bf16[256,512]{1,0:T(8,128)(2,1)}, bf16[256,512]{1,0:T(8,128)(2,1)}, bf16[528,1024]{1,0:T(8,128)(2,1)}) custom-call(s32[4]{0:T(128)} %pad_add_fusion.1.order, bf16[272,1024]{1,0:T(8,128)(2,1)} %copy-done.10, bf16[272,1024]{1,0:T(8,128)(2,1)} %collective-permute-done.1.refs_1_, bf16[256,1536]{1,0:T(8,128)(2,1)} %copy-done, ...), custom_call_target="tpu_custom_call" | custom-call | flops 1610612736 | bytes 5865488 | tf_op jit(solution)/shard_map/pallas_call | solution.py:21
  55.3 0.0 collective-permute-start.5
  55.3 0.0 copy-done.1
  55.3 1.3 %collective-permute-start.8 = (bf16[1024,256]{1,0:T(8,128)(2,1)S(1)}, bf16[1024,256]{1,0:T(8,128)(2,1)S(1)}, u32[]{:S(2)}, u32[]{:S(2)}) collective-permute-start(bf16[1024,256]{1,0:T(8,128)(2,1)S(1)} %copy-done.1), channel_id=1, source_target_pairs={{0,2},{1,3},{2,0},{3,1},{4,6},{5,7},{6,4},{7,5},{8,10},{9,11},{10,... | collective-permute-start | bytes 1572872 | tf_op jit(solution)/shard_map/ppermute | solution.py:169
  56.6 0.7 collective-permute-start.9
  57.3 11.1 %collective-permute-done.8.refs_3_ = bf16[1024,256]{1,0:T(8,128)(2,1)S(1)} collective-permute-done((bf16[1024,256]{1,0:T(8,128)(2,1)S(1)}, bf16[1024,256]{1,0:T(8,128)(2,1)S(1)}, u32[]{:S(2)}, u32[]{:S(2)}) %collective-permute-start.8) | collective-permute-done | bytes 524320 | tf_op jit(solution)/shard_map/ppermute | solution.py:169
  68.4 0.0 copy-start.2
  68.4 1.3 %collective-permute-start.10 = (bf16[1024,256]{1,0:T(8,128)(2,1)S(1)}, bf16[1024,256]{1,0:T(8,128)(2,1)S(1)}, u32[]{:S(2)}, u32[]{:S(2)}) collective-permute-start(bf16[1024,256]{1,0:T(8,128)(2,1)S(1)} %collective-permute-done.8.refs_3_), channel_id=1, source_target_pairs={{0,1},{1,0},{2,3},{3,2},{4,5},{5,4},{6,7},{7,6},{8,9},{9,8},{10,11... | collective-permute-start | bytes 1572872 | tf_op jit(solution)/shard_map/ppermute | solution.py:172
  69.7 0.0 collective-permute-done.5.far
  69.7 0.0 copy-start.7
  69.7 1.0 copy-done.7
  70.7 7.3 %shard_map.93 = bf16[256,512]{1,0:T(8,128)(2,1)} custom-call(bf16[256,512]{1,0:T(8,128)(2,1)} %get-tuple-element.12.q, bf16[528,1024]{1,0:T(8,128)(2,1)} %get-tuple-element.13.near, bf16[528,1024]{1,0:T(8,128)(2,1)} %copy-done.7), custom_call_target="tpu_custom_call" | custom-call | flops 1073741824 | bytes 2686976 | tf_op jit(solution)/shard_map/pallas_call | solution.py:21
  78.0 0.0 copy-done.2
  78.0 9.9 %collective-permute-start.6 = (bf16[256,512]{1,0:T(8,128)(2,1)}, bf16[256,512]{1,0:T(8,128)(2,1)S(1)}, u32[]{:S(2)}, u32[]{:S(2)}) collective-permute-start(bf16[256,512]{1,0:T(8,128)(2,1)} %shard_map.93), channel_id=1, source_target_pairs={{0,0},{8,1},{2,2},{10,3},{4,4},{12,5},{6,6},{14,7},{1,8},{9,9},{3,... | collective-permute-start | bytes 786440 | tf_op jit(solution)/shard_map/ppermute | solution.py:235
  87.9 7.3 %shard_map.94 = bf16[256,512]{1,0:T(8,128)(2,1)} custom-call(bf16[256,512]{1,0:T(8,128)(2,1)} %get-tuple-element.14.q, bf16[528,1024]{1,0:T(8,128)(2,1)} %get-tuple-element.13.near, bf16[528,1024]{1,0:T(8,128)(2,1)} %copy-done.7), custom_call_target="tpu_custom_call" | custom-call | flops 1073741824 | bytes 2686976 | tf_op jit(solution)/shard_map/pallas_call | solution.py:21
  95.1 0.2 collective-permute-start.7
  95.3 0.6 pad_add_fusion.places
  96.0 0.0 collective-permute-done.9.refs_4_
  96.0 0.0 copy-start.3
  96.0 0.0 collective-permute-done.10.refs_5_
  96.0 0.0 copy-start.4
  96.0 0.0 collective-permute-done.6.refs_0_
  96.0 0.0 copy-start.5
  96.0 6.9 %collective-permute-done.7.refs_1_ = bf16[256,512]{1,0:T(8,128)(2,1)S(1)} collective-permute-done((bf16[256,512]{1,0:T(8,128)(2,1)}, bf16[256,512]{1,0:T(8,128)(2,1)S(1)}, u32[]{:S(2)}, u32[]{:S(2)}) %collective-permute-start.7) | collective-permute-done | bytes 262176 | tf_op jit(solution)/shard_map/ppermute | solution.py:235
  103.0 0.0 copy-start.6
  103.0 0.0 copy-done.3
  103.0 0.0 copy-done.4
  103.0 0.0 copy-done.5
  103.0 0.7 copy-done.6
  103.6 3.6 %shard_map.95 = bf16[256,1024]{1,0:T(8,128)(2,1)} custom-call(s32[2]{0:T(128)} %pad_add_fusion.places, s32[4]{0:T(128)} %pad_add_fusion.1.order, f32[256,1024]{1,0:T(8,128)} %get-tuple-element.10.embedded, bf16[256,512]{1,0:T(8,128)(2,1)} %copy-done.5, bf16[256,512]{1,0:T(8,128)(2,1)} %copy-done.6, bf16[1024,256]{1,0:T(8,128)(2,1)} %refs_2_.1, ...), custom_call_target="tpu_custom_call" | custom-call | flops 536870912 | bytes 4194328 | tf_op jit(solution)/shard_map/pallas_call | solution.py:21
Async XLA Ops:
  1.2 48.2 %copy-start = (bf16[256,1536]{1,0:T(8,128)(2,1)}, bf16[256,1536]{1,0:T(8,128)(2,1)S(1)}, u32[]{:S(2)}) copy-start(bf16[256,1536]{1,0:T(8,128)(2,1)S(1)} %pad_maximum_fusion.refs_2_) | copy-start | bytes 2359300
  1.2 19.3 %collective-permute-start.2 = (bf16[256,1536]{1,0:T(8,128)(2,1)S(1)}, bf16[256,1536]{1,0:T(8,128)(2,1)S(1)}, u32[]{:S(2)}, u32[]{:S(2)}) collective-permute-start(bf16[256,1536]{1,0:T(8,128)(2,1)S(1)} %pad_maximum_fusion.refs_2_), channel_id=1, source_target_pairs={{0,2},{1,3},{2,0},{3,1},{4,6},{5,7},{6,4},{7,5},{8,10},{9,11},{10,... | collective-permute-start | bytes 2359304 | tf_op jit(solution)/shard_map/ppermute | solution.py:169
  3.3 46.0 %collective-permute-start.3 = (bf16[256,1536]{1,0:T(8,128)(2,1)S(1)}, bf16[256,1536]{1,0:T(8,128)(2,1)S(1)}, u32[]{:S(2)}, u32[]{:S(2)}) collective-permute-start(bf16[256,1536]{1,0:T(8,128)(2,1)S(1)} %pad_maximum_fusion.refs_2_), channel_id=1, source_target_pairs={{0,1},{1,0},{2,3},{3,2},{4,5},{5,4},{6,7},{7,6},{8,9},{9,8},{10,11... | collective-permute-start | bytes 2359304 | tf_op jit(solution)/shard_map/ppermute | solution.py:172
  20.6 28.8 %copy-start.8 = (bf16[256,1536]{1,0:T(8,128)(2,1)}, bf16[256,1536]{1,0:T(8,128)(2,1)S(1)}, u32[]{:S(2)}) copy-start(bf16[256,1536]{1,0:T(8,128)(2,1)S(1)} %collective-permute-done.2.refs_3_) | copy-start | bytes 2359300
  20.6 28.8 %collective-permute-start.4 = (bf16[256,1536]{1,0:T(8,128)(2,1)S(1)}, bf16[256,1536]{1,0:T(8,128)(2,1)}, u32[]{:S(2)}, u32[]{:S(2)}) collective-permute-start(bf16[256,1536]{1,0:T(8,128)(2,1)S(1)} %collective-permute-done.2.refs_3_), channel_id=1, source_target_pairs={{0,1},{1,0},{2,3},{3,2},{4,5},{5,4},{6,7},{7,6},{8,9},{9,8},{10,11... | collective-permute-start | bytes 2359304 | tf_op jit(solution)/shard_map/ppermute | solution.py:172
  24.7 16.9 %collective-permute-start = (bf16[272,1024]{1,0:T(8,128)(2,1)}, bf16[272,1024]{1,0:T(8,128)(2,1)S(1)}, u32[]{:S(2)}, u32[]{:S(2)}) collective-permute-start(bf16[272,1024]{1,0:T(8,128)(2,1)} %get-tuple-element.11), channel_id=1, source_target_pairs={{0,0},{1,8},{2,2},{3,10},{4,4},{5,12},{6,6},{7,14},{8,1},{9,9},{10... | collective-permute-start | bytes 1671176 | tf_op jit(solution)/shard_map/ppermute | solution.py:208
  29.3 20.1 %collective-permute-start.1 = (bf16[272,1024]{1,0:T(8,128)(2,1)}, bf16[272,1024]{1,0:T(8,128)(2,1)}, u32[]{:S(2)}, u32[]{:S(2)}) collective-permute-start(bf16[272,1024]{1,0:T(8,128)(2,1)} %get-tuple-element.11), channel_id=1, source_target_pairs={{0,4},{1,12},{2,6},{3,14},{4,0},{5,8},{6,2},{7,10},{8,5},{9,13},{1... | collective-permute-start | bytes 1671176 | tf_op jit(solution)/shard_map/ppermute | solution.py:208
  31.2 24.1 %copy-start.1 = (bf16[1024,256]{1,0:T(8,128)(2,1)S(1)}, bf16[1024,256]{1,0:T(8,128)(2,1)}, u32[]{:S(2)}) copy-start(bf16[1024,256]{1,0:T(8,128)(2,1)} %refs_2_.1) | copy-start | bytes 1572868
  41.6 7.8 %copy-start.10 = (bf16[272,1024]{1,0:T(8,128)(2,1)}, bf16[272,1024]{1,0:T(8,128)(2,1)S(1)}, u32[]{:S(2)}) copy-start(bf16[272,1024]{1,0:T(8,128)(2,1)S(1)} %collective-permute-done.refs_0_) | copy-start | bytes 1671172
  49.4 0.9 copy-start.9
  55.3 14.4 %collective-permute-start.5 = (bf16[528,1024]{1,0:T(8,128)(2,1)}, bf16[528,1024]{1,0:T(8,128)(2,1)S(1)}, u32[]{:S(2)}, u32[]{:S(2)}) collective-permute-start(bf16[528,1024]{1,0:T(8,128)(2,1)} %get-tuple-element.13.near), channel_id=1, source_target_pairs={{0,1},{1,0},{2,3},{3,2},{4,5},{5,4},{6,7},{7,6},{8,9},{9,8},{10,11... | collective-permute-start | bytes 3244040 | tf_op jit(solution)/shard_map/ppermute | solution.py:172
  55.3 13.1 %collective-permute-start.8 = (bf16[1024,256]{1,0:T(8,128)(2,1)S(1)}, bf16[1024,256]{1,0:T(8,128)(2,1)S(1)}, u32[]{:S(2)}, u32[]{:S(2)}) collective-permute-start(bf16[1024,256]{1,0:T(8,128)(2,1)S(1)} %copy-done.1), channel_id=1, source_target_pairs={{0,2},{1,3},{2,0},{3,1},{4,6},{5,7},{6,4},{7,5},{8,10},{9,11},{10,... | collective-permute-start | bytes 1572872 | tf_op jit(solution)/shard_map/ppermute | solution.py:169
  56.6 39.4 %collective-permute-start.9 = (bf16[1024,256]{1,0:T(8,128)(2,1)S(1)}, bf16[1024,256]{1,0:T(8,128)(2,1)S(1)}, u32[]{:S(2)}, u32[]{:S(2)}) collective-permute-start(bf16[1024,256]{1,0:T(8,128)(2,1)S(1)} %copy-done.1), channel_id=1, source_target_pairs={{0,1},{1,0},{2,3},{3,2},{4,5},{5,4},{6,7},{7,6},{8,9},{9,8},{10,11... | collective-permute-start | bytes 1572872 | tf_op jit(solution)/shard_map/ppermute | solution.py:172
  68.4 9.6 %copy-start.2 = (bf16[1024,256]{1,0:T(8,128)(2,1)}, bf16[1024,256]{1,0:T(8,128)(2,1)S(1)}, u32[]{:S(2)}) copy-start(bf16[1024,256]{1,0:T(8,128)(2,1)S(1)} %collective-permute-done.8.refs_3_) | copy-start | bytes 1572868
  68.4 27.6 %collective-permute-start.10 = (bf16[1024,256]{1,0:T(8,128)(2,1)S(1)}, bf16[1024,256]{1,0:T(8,128)(2,1)S(1)}, u32[]{:S(2)}, u32[]{:S(2)}) collective-permute-start(bf16[1024,256]{1,0:T(8,128)(2,1)S(1)} %collective-permute-done.8.refs_3_), channel_id=1, source_target_pairs={{0,1},{1,0},{2,3},{3,2},{4,5},{5,4},{6,7},{7,6},{8,9},{9,8},{10,11... | collective-permute-start | bytes 1572872 | tf_op jit(solution)/shard_map/ppermute | solution.py:172
  69.7 1.0 copy-start.7
  78.0 18.0 %collective-permute-start.6 = (bf16[256,512]{1,0:T(8,128)(2,1)}, bf16[256,512]{1,0:T(8,128)(2,1)S(1)}, u32[]{:S(2)}, u32[]{:S(2)}) collective-permute-start(bf16[256,512]{1,0:T(8,128)(2,1)} %shard_map.93), channel_id=1, source_target_pairs={{0,0},{8,1},{2,2},{10,3},{4,4},{12,5},{6,6},{14,7},{1,8},{9,9},{3,... | collective-permute-start | bytes 786440 | tf_op jit(solution)/shard_map/ppermute | solution.py:235
  95.1 7.8 %collective-permute-start.7 = (bf16[256,512]{1,0:T(8,128)(2,1)}, bf16[256,512]{1,0:T(8,128)(2,1)S(1)}, u32[]{:S(2)}, u32[]{:S(2)}) collective-permute-start(bf16[256,512]{1,0:T(8,128)(2,1)} %shard_map.94), channel_id=1, source_target_pairs={{4,0},{12,1},{6,2},{14,3},{0,4},{8,5},{2,6},{10,7},{5,8},{13,9},{7... | collective-permute-start | bytes 786440 | tf_op jit(solution)/shard_map/ppermute | solution.py:235
  96.0 7.0 %copy-start.3 = (bf16[1024,256]{1,0:T(8,128)(2,1)}, bf16[1024,256]{1,0:T(8,128)(2,1)S(1)}, u32[]{:S(2)}) copy-start(bf16[1024,256]{1,0:T(8,128)(2,1)S(1)} %collective-permute-done.9.refs_4_) | copy-start | bytes 1572868
  96.0 7.0 %copy-start.4 = (bf16[1024,256]{1,0:T(8,128)(2,1)}, bf16[1024,256]{1,0:T(8,128)(2,1)S(1)}, u32[]{:S(2)}) copy-start(bf16[1024,256]{1,0:T(8,128)(2,1)S(1)} %collective-permute-done.10.refs_5_) | copy-start | bytes 1572868
  96.0 7.0 %copy-start.5 = (bf16[256,512]{1,0:T(8,128)(2,1)}, bf16[256,512]{1,0:T(8,128)(2,1)S(1)}, u32[]{:S(2)}) copy-start(bf16[256,512]{1,0:T(8,128)(2,1)S(1)} %collective-permute-done.6.refs_0_) | copy-start | bytes 786436
  103.0 0.7 copy-start.6
where the time goes:
time: 108 us; the launch traced here: 107 us
  waiting for transfers between devices  52.5 us (49%)
  Pallas kernels  25.9 us (24%)
  starting transfers between devices  23.6 us (22%)
  local copies, waits for them, and re-layouts  3.73 us (3%)
  other arithmetic  1.34 us (1%)
    ppermute x2, waiting for transfers between devices, along(): lax.ppermute(value, 'fsdp', [(i, (i + 2 * by) % lanes) for i in range(lan...  27.4 us
    pallas_call x5, Pallas kernels, call(): pl.pallas_call(kernel, out_shape=outs, in_specs=specs, out_specs=[VM] * l...  25.9 us
    ppermute x2, waiting for transfers between devices, body(): blocks.append(lax.ppermute(block, ('ctx', 'fsdp'), spread(j)))  18.2 us
    ppermute x2, starting transfers between devices, body(): contexts.append(lax.ppermute(context, ('ctx', 'fsdp'), back))  10.1 us
    ppermute x2, waiting for transfers between devices, body(): contexts.append(lax.ppermute(context, ('ctx', 'fsdp'), back))  6.93 us
    ppermute x2, starting transfers between devices, body(): blocks.append(lax.ppermute(block, ('ctx', 'fsdp'), spread(j)))  5.86 us
    ppermute x5, starting transfers between devices, partner(): return lax.ppermute(value, 'fsdp', [(i, i ^ 1) for i in range(lanes)])  4.22 us
    ppermute x2, starting transfers between devices, along(): lax.ppermute(value, 'fsdp', [(i, (i + 2 * by) % lanes) for i in range(lan...  3.37 us
  transfers between devices with their start and end apart: 11, of which 5 were waited for; matrix products, arithmetic and copies ran while one was open for 1% of the time, Pallas kernels for 16%

commit v1 on v0

v1 whole, which is shorter than its diff:
```python
import functools

import jax
import jax.numpy as jnp
from jax import lax
from jax.experimental import pallas as pl
from jax.experimental.pallas import tpu as pltpu
from jax.sharding import PartitionSpec as P


HEADS = 16
floor_score = -1e30
epsilon = 1e-06
VM = pl.BlockSpec(memory_space=pltpu.VMEM)
SM = pl.BlockSpec(memory_space=pltpu.SMEM)
PAD = 16


HB = pl.BlockSpec(memory_space=pltpu.HBM)


def call(kernel, outs, args, specs, flops, scratch=(), limit=16 << 20):
    moved = sum(a.size * a.dtype.itemsize for a in (*args, *outs))
    return pl.pallas_call(
        kernel,
        out_shape=outs,
        in_specs=specs,
        out_specs=[VM] * len(outs),
        scratch_shapes=scratch,
        compiler_params=pltpu.CompilerParams(vmem_limit_bytes=limit),
        cost_estimate=pl.CostEstimate(flops=flops, bytes_accessed=moved, transcendentals=0),
    )(*args)


def embed_kernel(place, *refs):
    inputs, weight, (embedded, block, share) = refs[:7], refs[7], refs[8:11]
    local, sems = refs[11:18], refs[18]
    copies = [pltpu.make_async_copy(a, b, sems.at[i]) for i, (a, b) in enumerate(zip(inputs, local))]
    group = share.shape[1] // 3
    for part in range(3):
        first = pl.multiple_of(part * (weight.shape[1] // 3) + place[0] * group, group)
        copies.append(
            pltpu.make_async_copy(
                weight.at[:, pl.ds(first, group)],
                share.at[:, pl.ds(part * group, group)],
                sems.at[7 + part],
            )
        )
    for copy in copies:
        copy.start()
    for copy in copies[:7]:
        copy.wait()
    patches, rows, cols, segs, row_table, col_table, gain = local
    length, grid = patches.shape[0], row_table.shape[0]
    level = lax.broadcasted_iota(jnp.int32, (grid, length), 0)
    row_hot = jnp.where(rows[...] == level, 1.0, 0.0).T.astype(jnp.bfloat16)
    col_hot = jnp.where(cols[...] == level, 1.0, 0.0).T.astype(jnp.bfloat16)
    x = (
        patches[...].astype(jnp.float32)
        + jnp.dot(row_hot, row_table[...], preferred_element_type=jnp.float32)
        + jnp.dot(col_hot, col_table[...], preferred_element_type=jnp.float32)
    )
    embedded[...] = x
    centered = x - jnp.mean(x, axis=-1, keepdims=True)
    variance = jnp.mean(centered * centered, axis=-1, keepdims=True)
    block[:length, :] = (centered * lax.rsqrt(variance + epsilon) * gain[...]).astype(jnp.bfloat16)
    block[length:, :] = jnp.zeros((PAD, block.shape[1]), jnp.bfloat16)
    block[length:, :length] = jnp.broadcast_to(
        segs[...].astype(jnp.float32), (PAD, length)
    ).astype(jnp.bfloat16)
    for copy in copies[7:]:
        copy.wait()


def qkv_kernel(pieces, parts, tile, scale, order, *refs):
    blocks, weights = refs[:parts], refs[parts : parts + pieces]
    q_out, kv_out = refs[parts + pieces : parts + pieces + 2]
    length = q_out.shape[0]
    depth, width = weights[0].shape
    third = width // 3
    block = blocks[0]
    if parts > 1:
        block = refs[-1]
        block[...] = sum(b[...] for b in blocks[1:]) + blocks[0][...]
    for first in range(0, width, tile):
        total = None
        for piece in range(pieces):
            lanes = pl.ds(pl.multiple_of(order[piece] * depth, depth), depth)
            part = jnp.dot(
                block[:length, lanes],
                weights[piece][:, first : first + tile],
                preferred_element_type=jnp.float32,
            )
            total = part if total is None else total + part
        total = total.astype(jnp.bfloat16)
        if first < third:
            q_out[:, first : first + tile] = total * jnp.bfloat16(scale)
        else:
            kv_out[:length, first - third : first - third + tile] = total
    kv_out[length:, :] = jnp.zeros((PAD, 2 * third), jnp.bfloat16)
    kv_out[length:, :length] = block[length:, :length]


def attend_kernel(slots, slot, head, q, *refs):
    keys, (out, hot, gate) = refs[: 2 * slots], refs[2 * slots :]
    length, third = q.shape
    level = lax.broadcasted_iota(jnp.int32, (128, length), 0).astype(jnp.float32)
    for j, ref in enumerate(keys):
        match = ref[length : length + 1, :length].astype(jnp.float32) == level
        gate[pl.ds(j * length, length), :] = (
            jnp.where(match, 0.0, floor_score).T.astype(jnp.bfloat16)
        )
        if j == slot:
            hot[...] = jnp.where(match, 1.0, 0.0).T.astype(jnp.bfloat16)
    lane = lax.broadcasted_iota(jnp.int32, (length, 2 * head), 1)
    nt = (((1,), (1,)), ((), ()))
    ones = jnp.ones((length, 2 * head), jnp.bfloat16)

    def pair(index, carry):
        lanes = pl.ds(pl.multiple_of(index * 2 * head, 2 * head), 2 * head)
        values = pl.ds(pl.multiple_of(third + index * 2 * head, 2 * head), 2 * head)
        both = q[:, lanes]
        mixed = []
        for low in (True, False):
            mask = (lane < head) if low else (lane >= head)
            one = jnp.concatenate([jnp.where(mask, both, jnp.zeros_like(both)), hot[...]], axis=1)
            scores = [
                lax.dot_general(
                    one,
                    jnp.concatenate([ref[:length, lanes], gate[pl.ds(j * length, length), :]], axis=1),
                    nt,
                    preferred_element_type=jnp.float32,
                )
                for j, ref in enumerate(keys)
            ]
            highest = functools.reduce(
                jnp.maximum, [jnp.max(s, axis=-1, keepdims=True) for s in scores]
            )
            product = sum(
                jnp.dot(
                    jnp.exp(s - highest).astype(jnp.bfloat16),
                    jnp.concatenate([ref[:length, values], ones], axis=1),
                    preferred_element_type=jnp.float32,
                )
                for s, ref in zip(scores, keys)
            )
            mixed.append(product[:, : 2 * head] / product[:, 2 * head :])
        out[:, lanes] = jnp.where(lane < head, mixed[0], mixed[1]).astype(jnp.bfloat16)
        return carry

    lax.fori_loop(0, third // (2 * head), pair, 0)


def out_kernel(slots, pieces, places, order, embedded, *refs):
    contexts, weights, out, context = refs[:slots], refs[slots : slots + pieces], refs[-2], refs[-1]
    width = contexts[0].shape[1]
    for slot in range(slots):
        lanes = pl.ds(pl.multiple_of(places[slot] * width, width), width)
        context[:, lanes] = contexts[slot][...]
    span = weights[0].shape[1]
    for piece in range(pieces):
        lanes = pl.ds(pl.multiple_of(order[piece] * span, span), span)
        out[:, lanes] = (
            embedded[:, lanes]
            + jnp.dot(context[...], weights[piece][...], preferred_element_type=jnp.float32)
        ).astype(jnp.bfloat16)


def body(
    patches, segment_ids, patch_rows, patch_cols, row_table, col_table, norm_gain, qkv_weight, out_weight
):
    n, lanes = lax.axis_size("ctx"), lax.axis_size("fsdp")
    half, chips = n // 2, lanes // 2
    z, f = lax.axis_index("ctx"), lax.axis_index("fsdp")
    length, model = patches.shape[1:]
    head = model // HEADS
    group = model // half
    place = z % half

    def spread(j, near=True, far=True):
        pairs = []
        for a in range(n):
            for b in range(lanes):
                core = b % 2
                here = a // half == core
                to = core * half + (a % half + j) % half
                if near if here else far:
                    pairs.append((a * lanes + b, to * lanes + b - core + (core if here else 1 - core)))
        return pairs

    def around(j):
        return [
            (a * lanes + b, (a - a % half + (a % half + j) % half) * lanes + b)
            for a in range(n)
            for b in range(lanes)
            if a // half != b % 2
        ]

    def send(value, pairs):
        return lax.ppermute(value, ("ctx", "fsdp"), pairs)

    def along(value, by):
        return lax.ppermute(value, "fsdp", [(i, (i + 2 * by) % lanes) for i in range(lanes)])

    def partner(value):
        return lax.ppermute(value, "fsdp", [(i, i ^ 1) for i in range(lanes)])

    def gather(piece):
        own = [piece] + [along(piece, by) for by in range(1, chips)]
        return own + [partner(p) for p in own]

    sources = [2 * ((f // 2 - by) % chips) + f % 2 for by in range(chips)]
    order = jnp.stack(sources + [s ^ 1 for s in sources]).astype(jnp.int32)
    depth = qkv_weight.shape[0]
    shape = jax.ShapeDtypeStruct
    inputs = (
        patches[0],
        patch_rows,
        patch_cols,
        segment_ids,
        row_table,
        col_table,
        norm_gain.reshape(1, model),
    )
    embedded, block, share = call(
        embed_kernel,
        [
            shape((length, model), jnp.float32),
            shape((length + PAD, model), jnp.bfloat16),
            shape((depth, 3 * group), jnp.bfloat16),
        ],
        (
            place.reshape(1).astype(jnp.int32),
            *[pltpu.with_memory_space_constraint(a, pltpu.HBM) for a in (*inputs, qkv_weight)],
        ),
        [SM] + [HB] * 8,
        4 * length * row_table.shape[0] * model,
        scratch=[pltpu.VMEM(a.shape, a.dtype) for a in inputs] + [pltpu.SemaphoreType.DMA((10,))],
    )
    weights = gather(share)
    out_weights = gather(out_weight)
    first = send(block, spread(0))
    blocks = [[first]] + [
        [send(block, spread(j, far=False)), send(first, around(j))]
        for j in range(1, half)
    ]
    queries, keys = [], []
    for parts in blocks:
        q, kv = call(
            functools.partial(qkv_kernel, lanes, len(parts), min(group, 256), 1.0 / head**0.5),
            [shape((length, group), jnp.bfloat16), shape((length + PAD, 2 * group), jnp.bfloat16)],
            (order, *parts, *weights),
            [SM] + [VM] * (len(parts) + lanes),
            2 * length * model * 3 * group,
            scratch=[pltpu.VMEM(block.shape, jnp.bfloat16)] * (len(parts) > 1),
        )
        queries.append(q)
        keys.append(kv)
    keys += [partner(kv) for kv in keys]
    contexts = []
    for j in range(half):
        (context,) = call(
            functools.partial(attend_kernel, half, j, head),
            [shape((length, group), jnp.bfloat16)],
            (queries[j], *keys),
            [VM] * (1 + 2 * half),
            8 * length * half * length * 2 * group,
            scratch=[
                pltpu.VMEM((length, 128), jnp.bfloat16),
                pltpu.VMEM((2 * half * length, 128), jnp.bfloat16),
            ],
        )
        contexts.append(send(context, [(b, a) for a, b in spread(j)]))
    places = jnp.stack([(place + j) % half for j in range(half)]).astype(jnp.int32)
    (encoded,) = call(
        functools.partial(out_kernel, half, lanes),
        [shape((length, model), jnp.bfloat16)],
        (places, order, embedded, *contexts, *out_weights),
        [SM, SM] + [VM] * (1 + half + lanes),
        2 * length * model * model,
        scratch=[pltpu.VMEM((length, model), jnp.bfloat16)],
    )
    return encoded[None]


def solution(mesh):
    return jax.shard_map(
        body,
        mesh=mesh,
        in_specs=(
            P(("groups", "fsdp"), "ctx", None),
            P(("groups", "fsdp"), "ctx"),
            P(("groups", "fsdp"), "ctx"),
            P(("groups", "fsdp"), "ctx"),
            P(),
            P(),
            P(),
            P("fsdp", None),
            P(None, "fsdp"),
        ),
        out_specs=P(("groups", "fsdp"), "ctx", None),
        check_vma=False,
    )
```

time: 108 us -> 71.2 us (0.66)
  the two profiles are of different devices: /device:TPU:1 before, /device:TPU:15 now
where the time goes in v1:
time: 71.2 us; the launch traced here: 70.6 us
  waiting for transfers between devices  32 us (45%)
  Pallas kernels  19.6 us (28%)
  starting transfers between devices  17.7 us (25%)
  local copies, waits for them, and re-layouts  0.98 us (1%)
    pallas_call x6, Pallas kernels, call(): pl.pallas_call(kernel, out_shape=outs, in_specs=specs, out_specs=[VM] * l...  19.6 us
    ppermute x5, waiting for transfers between devices, send(): return lax.ppermute(value, ('ctx', 'fsdp'), pairs)  19.2 us
    ppermute x5, starting transfers between devices, send(): return lax.ppermute(value, ('ctx', 'fsdp'), pairs)  12.7 us
    ppermute x2, waiting for transfers between devices, along(): lax.ppermute(value, 'fsdp', [(i, (i + 2 * by) % lanes) for i in range(lan...  11.4 us
    ppermute x6, starting transfers between devices, partner(): return lax.ppermute(value, 'fsdp', [(i, i ^ 1) for i in range(lanes)])  4.51 us
  transfers between devices with their start and end apart: 13, of which 5 were waited for; matrix products, arithmetic and copies ran while one was open for 0% of the time, Pallas kernels for 20%

profile of v1, /device:TPU:15, one launch (start us, length us, event | category | flops | bytes accessed | tf_op | source)
XLA Modules:
  0.0 70.6 jit_solution(14844559306761297357)
XLA Ops:
  0.0 2.8 %shard_map.91 = (f32[256,1024]{1,0:T(8,128)S(1)}, bf16[272,1024]{1,0:T(8,128)(2,1)}, bf16[256,1536]{1,0:T(8,128)(2,1)S(1)}) custom-call(s32[1]{0:T(128)} %bitcast.6.place, bf16[256,1024]{1,0:T(8,128)(2,1)} %bitcast.10, s32[1,256]{1,0:T(1,128)} %refs_1_.1, s32[1,256]{1,0:T(1,128)} %refs_2_.2, s32[1,256]{1,0:T(1,128)} %refs_3_.1, bf16[64,1024]{1,0:T(8,128)(2,1)} %refs_4_.1, ...), custom_call_target="tpu_custom_call" | custom-call | flops 67108864 | bytes 4758532 | tf_op jit(solution)/shard_map/pallas_call | solution.py:24
  2.8 0.0 copy-start
  2.8 1.0 %copy-done = f32[256,1024]{1,0:T(8,128)} copy-done((f32[256,1024]{1,0:T(8,128)}, f32[256,1024]{1,0:T(8,128)S(1)}, u32[]{:S(2)}) %copy-start) | copy-done | bytes 1048600
  3.8 0.3 collective-permute-start.1
  4.1 5.0 %collective-permute-start = (bf16[272,1024]{1,0:T(8,128)(2,1)}, bf16[272,1024]{1,0:T(8,128)(2,1)}, u32[]{:S(2)}, u32[]{:S(2)}) collective-permute-start(bf16[272,1024]{1,0:T(8,128)(2,1)} %get-tuple-element.13), channel_id=1, source_target_pairs={{0,0},{1,8},{2,2},{3,10},{4,4},{5,12},{6,6},{7,14},{8,1},{9,9},{10... | collective-permute-start | bytes 1671176 | tf_op jit(solution)/shard_map/ppermute | solution.py:200
  9.1 1.7 %collective-permute-start.2 = (bf16[256,1536]{1,0:T(8,128)(2,1)S(1)}, bf16[256,1536]{1,0:T(8,128)(2,1)S(1)}, u32[]{:S(2)}, u32[]{:S(2)}) collective-permute-start(bf16[256,1536]{1,0:T(8,128)(2,1)S(1)} %get-tuple-element.14.refs_1_.refs_2_), channel_id=1, source_target_pairs={{0,1},{1,0},{2,3},{3,2},{4,5},{5,4},{6,7},{7,6},{8,9},{9,8},{10,11... | collective-permute-start | bytes 2359304 | tf_op jit(solution)/shard_map/ppermute | solution.py:206
  10.9 11.4 %collective-permute-done.1.refs_2_.refs_3_ = bf16[256,1536]{1,0:T(8,128)(2,1)S(1)} collective-permute-done((bf16[256,1536]{1,0:T(8,128)(2,1)S(1)}, bf16[256,1536]{1,0:T(8,128)(2,1)S(1)}, u32[]{:S(2)}, u32[]{:S(2)}) %collective-permute-start.1) | collective-permute-done | bytes 786464 | tf_op jit(solution)/shard_map/ppermute | solution.py:203
  22.2 1.5 %collective-permute-start.3 = (bf16[256,1536]{1,0:T(8,128)(2,1)S(1)}, bf16[256,1536]{1,0:T(8,128)(2,1)S(1)}, u32[]{:S(2)}, u32[]{:S(2)}) collective-permute-start(bf16[256,1536]{1,0:T(8,128)(2,1)S(1)} %collective-permute-done.1.refs_2_.refs_3_), channel_id=1, source_target_pairs={{0,1},{1,0},{2,3},{3,2},{4,5},{5,4},{6,7},{7,6},{8,9},{9,8},{10,11... | collective-permute-start | bytes 2359304 | tf_op jit(solution)/shard_map/ppermute | solution.py:206
  23.8 1.5 %collective-permute-start.4 = (bf16[272,1024]{1,0:T(8,128)(2,1)}, bf16[272,1024]{1,0:T(8,128)(2,1)}, u32[]{:S(2)}, u32[]{:S(2)}) collective-permute-start(bf16[272,1024]{1,0:T(8,128)(2,1)} %get-tuple-element.13), channel_id=1, source_target_pairs={{0,4},{2,6},{4,0},{6,2},{9,13},{11,15},{13,9},{15,11},{16,20},{18,... | collective-permute-start | bytes 1671176 | tf_op jit(solution)/shard_map/ppermute | solution.py:200
  25.2 0.0 collective-permute-done.refs_0_
  25.2 2.1 %collective-permute-start.5 = (bf16[272,1024]{1,0:T(8,128)(2,1)}, bf16[272,1024]{1,0:T(8,128)(2,1)}, u32[]{:S(2)}, u32[]{:S(2)}) collective-permute-start(bf16[272,1024]{1,0:T(8,128)(2,1)} %collective-permute-done.refs_0_), channel_id=1, source_target_pairs={{1,5},{3,7},{5,1},{7,3},{8,12},{10,14},{12,8},{14,10},{17,21},{19,... | collective-permute-start | bytes 1671176 | tf_op jit(solution)/shard_map/ppermute | solution.py:200
  27.3 0.3 collective-permute-start.10
  27.6 0.1 pad_add_fusion.1.order
  27.7 0.0 collective-permute-done.2.refs_3_.refs_4_
  27.7 0.0 collective-permute-done.3.refs_4_.refs_5_
  27.7 2.1 %shard_map.92 = (bf16[256,512]{1,0:T(8,128)(2,1)S(1)}, bf16[272,1024]{1,0:T(8,128)(2,1)S(1)}) custom-call(s32[4]{0:T(128)S(1)} %pad_add_fusion.1.order, bf16[272,1024]{1,0:T(8,128)(2,1)} %collective-permute-done.refs_0_, bf16[256,1536]{1,0:T(8,128)(2,1)S(1)} %get-tuple-element.14.refs_1_.refs_2_, ...), custom_call_target="tpu_custom_call" | custom-call | flops 805306368 | bytes 4522000 | tf_op jit(solution)/shard_map/pallas_call | solution.py:24
  29.8 0.6 collective-permute-start.6
  30.4 0.0 collective-permute-done.4.refs_0_
  30.4 10.7 %collective-permute-done.5.refs_1_ = bf16[272,1024]{1,0:T(8,128)(2,1)} collective-permute-done((bf16[272,1024]{1,0:T(8,128)(2,1)}, bf16[272,1024]{1,0:T(8,128)(2,1)}, u32[]{:S(2)}, u32[]{:S(2)}) %collective-permute-start.5) | collective-permute-done | bytes 557088 | tf_op jit(solution)/shard_map/ppermute | solution.py:200
  41.1 2.3 %shard_map.93 = (bf16[256,512]{1,0:T(8,128)(2,1)S(1)}, bf16[272,1024]{1,0:T(8,128)(2,1)S(1)}) custom-call(s32[4]{0:T(128)S(1)} %pad_add_fusion.1.order, bf16[272,1024]{1,0:T(8,128)(2,1)} %collective-permute-done.4.refs_0_, bf16[272,1024]{1,0:T(8,128)(2,1)} %collective-permute-done.5.refs_1_, bf16[256,1536]{1,0:T(8,128)(2,1)S(1)} %get-tuple-element.14.refs_1_.refs_2_, ...), custom_call_target="tpu_custom_call" | custom-call | flops 805306368 | bytes 5079056 | tf_op jit(solution)/shard_map/pallas_call | solution.py:24
  43.4 0.1 collective-permute-start.7
  43.5 0.5 collective-permute-start.11
  44.0 0.0 collective-permute-done.10.refs_3_
  44.0 0.1 collective-permute-start.12
  44.0 0.0 collective-permute-done.6.refs_2_
  44.0 1.4 %collective-permute-done.7.refs_3_ = bf16[272,1024]{1,0:T(8,128)(2,1)S(1)} collective-permute-done((bf16[272,1024]{1,0:T(8,128)(2,1)S(1)}, bf16[272,1024]{1,0:T(8,128)(2,1)S(1)}, u32[]{:S(2)}, u32[]{:S(2)}) %collective-permute-start.7) | collective-permute-done | bytes 557088 | tf_op jit(solution)/shard_map/ppermute | solution.py:206
  45.4 4.8 %shard_map.94 = bf16[256,512]{1,0:T(8,128)(2,1)S(1)} custom-call(bf16[256,512]{1,0:T(8,128)(2,1)S(1)} %get-tuple-element.15.q, bf16[272,1024]{1,0:T(8,128)(2,1)S(1)} %get-tuple-element.16.refs_0_, bf16[272,1024]{1,0:T(8,128)(2,1)S(1)} %get-tuple-element.17.refs_1_, bf16[272,1024]{1,0:T(8,128)(2,1)S(1)} %collective-permute-done.6.refs_2_, ...), custom_call_target="tpu_custom_call" | custom-call | flops 1073741824 | bytes 2752512 | tf_op jit(solution)/shard_map/pallas_call | solution.py:24
  50.2 4.0 %collective-permute-start.8 = (bf16[256,512]{1,0:T(8,128)(2,1)S(1)}, bf16[256,512]{1,0:T(8,128)(2,1)S(1)}, u32[]{:S(2)}, u32[]{:S(2)}) collective-permute-start(bf16[256,512]{1,0:T(8,128)(2,1)S(1)} %shard_map.94), channel_id=1, source_target_pairs={{0,0},{8,1},{2,2},{10,3},{4,4},{12,5},{6,6},{14,7},{1,8},{9,9},{3,... | collective-permute-start | bytes 786440 | tf_op jit(solution)/shard_map/ppermute | solution.py:200
  54.3 0.0 copy-start.1
  54.3 4.8 %shard_map.95 = bf16[256,512]{1,0:T(8,128)(2,1)S(1)} custom-call(bf16[256,512]{1,0:T(8,128)(2,1)S(1)} %get-tuple-element.18.q, bf16[272,1024]{1,0:T(8,128)(2,1)S(1)} %get-tuple-element.16.refs_0_, bf16[272,1024]{1,0:T(8,128)(2,1)S(1)} %get-tuple-element.17.refs_1_, bf16[272,1024]{1,0:T(8,128)(2,1)S(1)} %collective-permute-done.6.refs_2_, ...), custom_call_target="tpu_custom_call" | custom-call | flops 1073741824 | bytes 2752512 | tf_op jit(solution)/shard_map/pallas_call | solution.py:24
  59.1 0.1 collective-permute-start.9
  59.2 0.1 pad_add_fusion.places
  59.3 0.0 collective-permute-done.11.refs_4_
  59.3 0.0 collective-permute-done.12.refs_5_
  59.3 1.0 %collective-permute-done.8.refs_0_ = bf16[256,512]{1,0:T(8,128)(2,1)S(1)} collective-permute-done((bf16[256,512]{1,0:T(8,128)(2,1)S(1)}, bf16[256,512]{1,0:T(8,128)(2,1)S(1)}, u32[]{:S(2)}, u32[]{:S(2)}) %collective-permute-start.8) | collective-permute-done | bytes 262176 | tf_op jit(solution)/shard_map/ppermute | solution.py:200
  60.3 7.5 %collective-permute-done.9.refs_1_ = bf16[256,512]{1,0:T(8,128)(2,1)S(1)} collective-permute-done((bf16[256,512]{1,0:T(8,128)(2,1)S(1)}, bf16[256,512]{1,0:T(8,128)(2,1)S(1)}, u32[]{:S(2)}, u32[]{:S(2)}) %collective-permute-start.9) | collective-permute-done | bytes 262176 | tf_op jit(solution)/shard_map/ppermute | solution.py:200
  67.8 0.0 copy-done.1
  67.8 2.8 %shard_map.96 = bf16[256,1024]{1,0:T(8,128)(2,1)} custom-call(s32[2]{0:T(128)S(1)} %pad_add_fusion.places, s32[4]{0:T(128)S(1)} %pad_add_fusion.1.order, f32[256,1024]{1,0:T(8,128)S(1)} %copy-done.1, bf16[256,512]{1,0:T(8,128)(2,1)S(1)} %collective-permute-done.8.refs_0_, bf16[256,512]{1,0:T(8,128)(2,1)S(1)} %collective-permute-done.9.refs_1_, ...), custom_call_target="tpu_custom_call" | custom-call | flops 536870912 | bytes 4194328 | tf_op jit(solution)/shard_map/pallas_call | solution.py:24
Async XLA Ops:
  2.8 1.0 %copy-start = (f32[256,1024]{1,0:T(8,128)}, f32[256,1024]{1,0:T(8,128)S(1)}, u32[]{:S(2)}) copy-start(f32[256,1024]{1,0:T(8,128)S(1)} %get-tuple-element.12.embedded) | copy-start | bytes 3145732
  3.8 18.4 %collective-permute-start.1 = (bf16[256,1536]{1,0:T(8,128)(2,1)S(1)}, bf16[256,1536]{1,0:T(8,128)(2,1)S(1)}, u32[]{:S(2)}, u32[]{:S(2)}) collective-permute-start(bf16[256,1536]{1,0:T(8,128)(2,1)S(1)} %get-tuple-element.14.refs_1_.refs_2_), channel_id=1, source_target_pairs={{0,2},{1,3},{2,0},{3,1},{4,6},{5,7},{6,4},{7,5},{8,10},{9,11},{10,... | collective-permute-start | bytes 2359304 | tf_op jit(solution)/shard_map/ppermute | solution.py:203
  4.1 21.2 %collective-permute-start = (bf16[272,1024]{1,0:T(8,128)(2,1)}, bf16[272,1024]{1,0:T(8,128)(2,1)}, u32[]{:S(2)}, u32[]{:S(2)}) collective-permute-start(bf16[272,1024]{1,0:T(8,128)(2,1)} %get-tuple-element.13), channel_id=1, source_target_pairs={{0,0},{1,8},{2,2},{3,10},{4,4},{5,12},{6,6},{7,14},{8,1},{9,9},{10... | collective-permute-start | bytes 1671176 | tf_op jit(solution)/shard_map/ppermute | solution.py:200
  9.1 18.6 %collective-permute-start.2 = (bf16[256,1536]{1,0:T(8,128)(2,1)S(1)}, bf16[256,1536]{1,0:T(8,128)(2,1)S(1)}, u32[]{:S(2)}, u32[]{:S(2)}) collective-permute-start(bf16[256,1536]{1,0:T(8,128)(2,1)S(1)} %get-tuple-element.14.refs_1_.refs_2_), channel_id=1, source_target_pairs={{0,1},{1,0},{2,3},{3,2},{4,5},{5,4},{6,7},{7,6},{8,9},{9,8},{10,11... | collective-permute-start | bytes 2359304 | tf_op jit(solution)/shard_map/ppermute | solution.py:206
  22.2 5.5 %collective-permute-start.3 = (bf16[256,1536]{1,0:T(8,128)(2,1)S(1)}, bf16[256,1536]{1,0:T(8,128)(2,1)S(1)}, u32[]{:S(2)}, u32[]{:S(2)}) collective-permute-start(bf16[256,1536]{1,0:T(8,128)(2,1)S(1)} %collective-permute-done.1.refs_2_.refs_3_), channel_id=1, source_target_pairs={{0,1},{1,0},{2,3},{3,2},{4,5},{5,4},{6,7},{7,6},{8,9},{9,8},{10,11... | collective-permute-start | bytes 2359304 | tf_op jit(solution)/shard_map/ppermute | solution.py:206
  23.8 6.6 %collective-permute-start.4 = (bf16[272,1024]{1,0:T(8,128)(2,1)}, bf16[272,1024]{1,0:T(8,128)(2,1)}, u32[]{:S(2)}, u32[]{:S(2)}) collective-permute-start(bf16[272,1024]{1,0:T(8,128)(2,1)} %get-tuple-element.13), channel_id=1, source_target_pairs={{0,4},{2,6},{4,0},{6,2},{9,13},{11,15},{13,9},{15,11},{16,20},{18,... | collective-permute-start | bytes 1671176 | tf_op jit(solution)/shard_map/ppermute | solution.py:200
  25.2 15.9 %collective-permute-start.5 = (bf16[272,1024]{1,0:T(8,128)(2,1)}, bf16[272,1024]{1,0:T(8,128)(2,1)}, u32[]{:S(2)}, u32[]{:S(2)}) collective-permute-start(bf16[272,1024]{1,0:T(8,128)(2,1)} %collective-permute-done.refs_0_), channel_id=1, source_target_pairs={{1,5},{3,7},{5,1},{7,3},{8,12},{10,14},{12,8},{14,10},{17,21},{19,... | collective-permute-start | bytes 1671176 | tf_op jit(solution)/shard_map/ppermute | solution.py:200
  27.3 16.7 %collective-permute-start.10 = (bf16[1024,256]{1,0:T(8,128)(2,1)}, bf16[1024,256]{1,0:T(8,128)(2,1)}, u32[]{:S(2)}, u32[]{:S(2)}) collective-permute-start(bf16[1024,256]{1,0:T(8,128)(2,1)} %refs_2_.3), channel_id=1, source_target_pairs={{0,2},{1,3},{2,0},{3,1},{4,6},{5,7},{6,4},{7,5},{8,10},{9,11},{10,... | collective-permute-start | bytes 1572872 | tf_op jit(solution)/shard_map/ppermute | solution.py:203
  29.8 14.3 %collective-permute-start.6 = (bf16[272,1024]{1,0:T(8,128)(2,1)S(1)}, bf16[272,1024]{1,0:T(8,128)(2,1)S(1)}, u32[]{:S(2)}, u32[]{:S(2)}) collective-permute-start(bf16[272,1024]{1,0:T(8,128)(2,1)S(1)} %get-tuple-element.16.refs_0_), channel_id=1, source_target_pairs={{0,1},{1,0},{2,3},{3,2},{4,5},{5,4},{6,7},{7,6},{8,9},{9,8},{10,11... | collective-permute-start | bytes 1671176 | tf_op jit(solution)/shard_map/ppermute | solution.py:206
  43.4 2.0 %collective-permute-start.7 = (bf16[272,1024]{1,0:T(8,128)(2,1)S(1)}, bf16[272,1024]{1,0:T(8,128)(2,1)S(1)}, u32[]{:S(2)}, u32[]{:S(2)}) collective-permute-start(bf16[272,1024]{1,0:T(8,128)(2,1)S(1)} %get-tuple-element.17.refs_1_), channel_id=1, source_target_pairs={{0,1},{1,0},{2,3},{3,2},{4,5},{5,4},{6,7},{7,6},{8,9},{9,8},{10,11... | collective-permute-start | bytes 1671176 | tf_op jit(solution)/shard_map/ppermute | solution.py:206
  43.5 15.8 %collective-permute-start.11 = (bf16[1024,256]{1,0:T(8,128)(2,1)}, bf16[1024,256]{1,0:T(8,128)(2,1)S(1)}, u32[]{:S(2)}, u32[]{:S(2)}) collective-permute-start(bf16[1024,256]{1,0:T(8,128)(2,1)} %refs_2_.3), channel_id=1, source_target_pairs={{0,1},{1,0},{2,3},{3,2},{4,5},{5,4},{6,7},{7,6},{8,9},{9,8},{10,11... | collective-permute-start | bytes 1572872 | tf_op jit(solution)/shard_map/ppermute | solution.py:206
  44.0 15.3 %collective-permute-start.12 = (bf16[1024,256]{1,0:T(8,128)(2,1)}, bf16[1024,256]{1,0:T(8,128)(2,1)S(1)}, u32[]{:S(2)}, u32[]{:S(2)}) collective-permute-start(bf16[1024,256]{1,0:T(8,128)(2,1)} %collective-permute-done.10.refs_3_), channel_id=1, source_target_pairs={{0,1},{1,0},{2,3},{3,2},{4,5},{5,4},{6,7},{7,6},{8,9},{9,8},{10,11... | collective-permute-start | bytes 1572872 | tf_op jit(solution)/shard_map/ppermute | solution.py:206
  50.2 10.1 %collective-permute-start.8 = (bf16[256,512]{1,0:T(8,128)(2,1)S(1)}, bf16[256,512]{1,0:T(8,128)(2,1)S(1)}, u32[]{:S(2)}, u32[]{:S(2)}) collective-permute-start(bf16[256,512]{1,0:T(8,128)(2,1)S(1)} %shard_map.94), channel_id=1, source_target_pairs={{0,0},{8,1},{2,2},{10,3},{4,4},{12,5},{6,6},{14,7},{1,8},{9,9},{3,... | collective-permute-start | bytes 786440 | tf_op jit(solution)/shard_map/ppermute | solution.py:200
  54.3 13.5 %copy-start.1 = (f32[256,1024]{1,0:T(8,128)S(1)}, f32[256,1024]{1,0:T(8,128)}, u32[]{:S(2)}) copy-start(f32[256,1024]{1,0:T(8,128)} %copy-done) | copy-start | bytes 3145732
  59.1 8.7 %collective-permute-start.9 = (bf16[256,512]{1,0:T(8,128)(2,1)S(1)}, bf16[256,512]{1,0:T(8,128)(2,1)S(1)}, u32[]{:S(2)}, u32[]{:S(2)}) collective-permute-start(bf16[256,512]{1,0:T(8,128)(2,1)S(1)} %shard_map.95), channel_id=1, source_target_pairs={{4,0},{12,1},{6,2},{14,3},{0,4},{8,5},{2,6},{10,7},{5,8},{13,9},{7... | collective-permute-start | bytes 786440 | tf_op jit(solution)/shard_map/ppermute | solution.py:200

commit v2 on v1

--- a/solution.py
+++ b/solution.py
@@ -14,6 +14,7 @@
 VM = pl.BlockSpec(memory_space=pltpu.VMEM)
 SM = pl.BlockSpec(memory_space=pltpu.SMEM)
 PAD = 16
+CUTS = 2
 
 
 HB = pl.BlockSpec(memory_space=pltpu.HBM)
@@ -32,9 +33,21 @@
     )(*args)
 
 
+def embedding(patches, rows, cols, row_table, col_table):
+    length, grid = patches.shape[0], row_table.shape[0]
+    level = lax.broadcasted_iota(jnp.int32, (grid, length), 0)
+    row_hot = jnp.where(rows[...] == level, 1.0, 0.0).T.astype(jnp.bfloat16)
+    col_hot = jnp.where(cols[...] == level, 1.0, 0.0).T.astype(jnp.bfloat16)
+    return (
+        patches[...].astype(jnp.float32)
+        + jnp.dot(row_hot, row_table[...], preferred_element_type=jnp.float32)
+        + jnp.dot(col_hot, col_table[...], preferred_element_type=jnp.float32)
+    )
+
+
 def embed_kernel(place, *refs):
-    inputs, weight, (embedded, block, share) = refs[:7], refs[7], refs[8:11]
-    local, sems = refs[11:18], refs[18]
+    inputs, weight, share, blocks = refs[:7], refs[7], refs[8], refs[9 : 9 + CUTS]
+    local, sems = refs[9 + CUTS : 16 + CUTS], refs[16 + CUTS]
     copies = [pltpu.make_async_copy(a, b, sems.at[i]) for i, (a, b) in enumerate(zip(inputs, local))]
     group = share.shape[1] // 3
     for part in range(3):
@@ -50,44 +63,43 @@
         copy.start()
     for copy in copies[:7]:
         copy.wait()
-    patches, rows, cols, segs, row_table, col_table, gain = local
-    length, grid = patches.shape[0], row_table.shape[0]
-    level = lax.broadcasted_iota(jnp.int32, (grid, length), 0)
-    row_hot = jnp.where(rows[...] == level, 1.0, 0.0).T.astype(jnp.bfloat16)
-    col_hot = jnp.where(cols[...] == level, 1.0, 0.0).T.astype(jnp.bfloat16)
-    x = (
-        patches[...].astype(jnp.float32)
-        + jnp.dot(row_hot, row_table[...], preferred_element_type=jnp.float32)
-        + jnp.dot(col_hot, col_table[...], preferred_element_type=jnp.float32)
-    )
-    embedded[...] = x
+    patches, rows, cols, row_table, col_table, segs, gain = local
+    length = patches.shape[0]
+    x = embedding(patches, rows, cols, row_table, col_table)
     centered = x - jnp.mean(x, axis=-1, keepdims=True)
     variance = jnp.mean(centered * centered, axis=-1, keepdims=True)
-    block[:length, :] = (centered * lax.rsqrt(variance + epsilon) * gain[...]).astype(jnp.bfloat16)
-    block[length:, :] = jnp.zeros((PAD, block.shape[1]), jnp.bfloat16)
-    block[length:, :length] = jnp.broadcast_to(
-        segs[...].astype(jnp.float32), (PAD, length)
-    ).astype(jnp.bfloat16)
+    normed = (centered * lax.rsqrt(variance + epsilon) * gain[...]).astype(jnp.bfloat16)
+    labels = jnp.broadcast_to(segs[...].astype(jnp.float32), (PAD, length)).astype(jnp.bfloat16)
+    cut = length // CUTS
+    for i, block in enumerate(blocks):
+        block[:cut, :] = normed[i * cut : (i + 1) * cut]
+        block[cut:, :] = jnp.zeros((PAD, block.shape[1]), jnp.bfloat16)
+        block[cut:, :cut] = labels[:, i * cut : (i + 1) * cut]
     for copy in copies[7:]:
         copy.wait()
 
 
-def qkv_kernel(pieces, parts, tile, scale, order, *refs):
-    blocks, weights = refs[:parts], refs[parts : parts + pieces]
-    q_out, kv_out = refs[parts + pieces : parts + pieces + 2]
+def qkv_kernel(pieces, choose, tile, scale, order, own, *refs):
+    ways, weights = (refs[:CUTS], refs[CUTS : 2 * CUTS]), refs[2 * CUTS : 2 * CUTS + pieces]
+    q_out, kv_out, block = refs[2 * CUTS + pieces :]
     length = q_out.shape[0]
     depth, width = weights[0].shape
     third = width // 3
-    block = blocks[0]
-    if parts > 1:
-        block = refs[-1]
-        block[...] = sum(b[...] for b in blocks[1:]) + blocks[0][...]
+    cut = length // CUTS
+    kv_out[length:, :] = jnp.zeros((PAD, 2 * third), jnp.bfloat16)
+    for i, (one, two) in enumerate(zip(*ways)):
+        if choose:
+            part = jnp.where(own[0] == 1, one[...], two[...])
+        else:
+            part = one[...] + two[...]
+        block[i * cut : (i + 1) * cut, :] = part[:cut]
+        kv_out[length:, i * cut : (i + 1) * cut] = part[cut:, :cut]
     for first in range(0, width, tile):
         total = None
         for piece in range(pieces):
             lanes = pl.ds(pl.multiple_of(order[piece] * depth, depth), depth)
             part = jnp.dot(
-                block[:length, lanes],
+                block[:, lanes],
                 weights[piece][:, first : first + tile],
                 preferred_element_type=jnp.float32,
             )
@@ -97,8 +109,6 @@
             q_out[:, first : first + tile] = total * jnp.bfloat16(scale)
         else:
             kv_out[:length, first - third : first - third + tile] = total
-    kv_out[length:, :] = jnp.zeros((PAD, 2 * third), jnp.bfloat16)
-    kv_out[length:, :length] = block[length:, :length]
 
 
 def attend_kernel(slots, slot, head, q, *refs):
@@ -151,19 +161,30 @@
     lax.fori_loop(0, third // (2 * head), pair, 0)
 
 
-def out_kernel(slots, pieces, places, order, embedded, *refs):
-    contexts, weights, out, context = refs[:slots], refs[slots : slots + pieces], refs[-2], refs[-1]
-    width = contexts[0].shape[1]
-    for slot in range(slots):
-        lanes = pl.ds(pl.multiple_of(places[slot] * width, width), width)
-        context[:, lanes] = contexts[slot][...]
-    span = weights[0].shape[1]
-    for piece in range(pieces):
+def first_kernel(slots, pieces, places, order, *refs):
+    inputs, refs = refs[:5], refs[5:]
+    contexts, weights = refs[: slots - 1], refs[slots - 1 : slots - 1 + pieces]
+    out, kept = refs[slots - 1 + pieces : slots + 1 + pieces]
+    local, sems = refs[slots + 1 + pieces : -1], refs[-1]
+    copies = [pltpu.make_async_copy(a, b, sems.at[i]) for i, (a, b) in enumerate(zip(inputs, local))]
+    for copy in copies:
+        copy.start()
+    for copy in copies:
+        copy.wait()
+    out[...] = embedding(*local)
+    width, span = kept.shape[0], weights[0].shape[1]
+    rows = [pl.ds(pl.multiple_of(places[j] * width, width), width) for j in range(slots)]
+    for piece, weight in enumerate(weights):
         lanes = pl.ds(pl.multiple_of(order[piece] * span, span), span)
-        out[:, lanes] = (
-            embedded[:, lanes]
-            + jnp.dot(context[...], weights[piece][...], preferred_element_type=jnp.float32)
-        ).astype(jnp.bfloat16)
+        kept[:, lanes] = weight[rows[-1], :]
+        for context, row in zip(contexts, rows):
+            out[:, lanes] += jnp.dot(context[...], weight[row, :], preferred_element_type=jnp.float32)
+
+
+def last_kernel(base, context, weight, out):
+    out[...] = (
+        base[...] + jnp.dot(context[...], weight[...], preferred_element_type=jnp.float32)
+    ).astype(out.dtype)
 
 
 def body(
@@ -196,6 +217,9 @@
             if a // half != b % 2
         ]
 
+    def send_cuts(values, pairs):
+        return [send(value, pairs) for value in values]
+
     def send(value, pairs):
         return lax.ppermute(value, ("ctx", "fsdp"), pairs)
 
@@ -217,42 +241,41 @@
         patches[0],
         patch_rows,
         patch_cols,
-        segment_ids,
         row_table,
         col_table,
+        segment_ids,
         norm_gain.reshape(1, model),
     )
-    embedded, block, share = call(
+    kept = [pltpu.with_memory_space_constraint(a, pltpu.HBM) for a in (*inputs, qkv_weight)]
+    local = [pltpu.VMEM(a.shape, a.dtype) for a in inputs]
+    share, *block = call(
         embed_kernel,
         [
-            shape((length, model), jnp.float32),
-            shape((length + PAD, model), jnp.bfloat16),
             shape((depth, 3 * group), jnp.bfloat16),
+            *[shape((length // CUTS + PAD, model), jnp.bfloat16)] * CUTS,
         ],
-        (
-            place.reshape(1).astype(jnp.int32),
-            *[pltpu.with_memory_space_constraint(a, pltpu.HBM) for a in (*inputs, qkv_weight)],
-        ),
+        (place.reshape(1).astype(jnp.int32), *kept),
         [SM] + [HB] * 8,
         4 * length * row_table.shape[0] * model,
-        scratch=[pltpu.VMEM(a.shape, a.dtype) for a in inputs] + [pltpu.SemaphoreType.DMA((10,))],
+        scratch=local + [pltpu.SemaphoreType.DMA((10,))],
     )
     weights = gather(share)
     out_weights = gather(out_weight)
-    first = send(block, spread(0))
-    blocks = [[first]] + [
-        [send(block, spread(j, far=False)), send(first, around(j))]
+    own = (z // half == f % 2).astype(jnp.int32).reshape(1)
+    first = send_cuts(block, spread(0, near=False))
+    blocks = [[block, first]] + [
+        [send_cuts(block, spread(j, far=False)), send_cuts(first, around(j))]
         for j in range(1, half)
     ]
     queries, keys = [], []
-    for parts in blocks:
+    for j, parts in enumerate(blocks):
         q, kv = call(
-            functools.partial(qkv_kernel, lanes, len(parts), min(group, 256), 1.0 / head**0.5),
+            functools.partial(qkv_kernel, lanes, j == 0, min(group, 256), 1.0 / head**0.5),
             [shape((length, group), jnp.bfloat16), shape((length + PAD, 2 * group), jnp.bfloat16)],
-            (order, *parts, *weights),
-            [SM] + [VM] * (len(parts) + lanes),
+            (order, own, *parts[0], *parts[1], *weights),
+            [SM, SM] + [VM] * (2 * CUTS + lanes),
             2 * length * model * 3 * group,
-            scratch=[pltpu.VMEM(block.shape, jnp.bfloat16)] * (len(parts) > 1),
+            scratch=[pltpu.VMEM((length, model), jnp.bfloat16)],
         )
         queries.append(q)
         keys.append(kv)
@@ -272,13 +295,20 @@
         )
         contexts.append(send(context, [(b, a) for a, b in spread(j)]))
     places = jnp.stack([(place + j) % half for j in range(half)]).astype(jnp.int32)
+    base, kept_rows = call(
+        functools.partial(first_kernel, half, lanes),
+        [shape((length, model), jnp.float32), shape((group, model), jnp.bfloat16)],
+        (places, order, *kept[:5], *contexts[:-1], *out_weights),
+        [SM, SM] + [HB] * 5 + [VM] * (half - 1 + lanes),
+        2 * length * model * (model - group),
+        scratch=local[:5] + [pltpu.SemaphoreType.DMA((5,))],
+    )
     (encoded,) = call(
-        functools.partial(out_kernel, half, lanes),
+        last_kernel,
         [shape((length, model), jnp.bfloat16)],
-        (places, order, embedded, *contexts, *out_weights),
-        [SM, SM] + [VM] * (1 + half + lanes),
-        2 * length * model * model,
-        scratch=[pltpu.VMEM((length, model), jnp.bfloat16)],
+        (base, contexts[-1], kept_rows),
+        [VM] * 3,
+        2 * length * model * group,
     )
     return encoded[None]
 

time: 71.2 us -> 82.1 us (1.15)
  the two profiles are of different devices: /device:TPU:15 before, /device:TPU:1 now
where the time goes in v2:
time: 82.1 us; the launch traced here: 81.8 us
  waiting for transfers between devices  32.6 us (40%)
  starting transfers between devices  27.4 us (33%)
  Pallas kernels  21.4 us (26%)
    pallas_call x7, Pallas kernels, call(): pl.pallas_call(kernel, out_shape=outs, in_specs=specs, out_specs=[VM] * l...  21.4 us
    ppermute x8, starting transfers between devices, send(): return lax.ppermute(value, ('ctx', 'fsdp'), pairs)  20.9 us
    ppermute x2, waiting for transfers between devices, along(): lax.ppermute(value, 'fsdp', [(i, (i + 2 * by) % lanes) for i in range(lan...  16.3 us
    ppermute x8, waiting for transfers between devices, send(): return lax.ppermute(value, ('ctx', 'fsdp'), pairs)  14.9 us
    ppermute x2, starting transfers between devices, along(): lax.ppermute(value, 'fsdp', [(i, (i + 2 * by) % lanes) for i in range(lan...  3.57 us
    ppermute x6, starting transfers between devices, partner(): return lax.ppermute(value, 'fsdp', [(i, i ^ 1) for i in range(lanes)])  2.92 us
  transfers between devices with their start and end apart: 16, of which 7 were waited for; matrix products, arithmetic and copies ran while one was open for 0% of the time, Pallas kernels for 21%

profile of v2, /device:TPU:1, one launch (start us, length us, event | category | flops | bytes accessed | tf_op | source)
XLA Modules:
  0.0 81.8 jit_solution(14224879634582853423)
XLA Ops:
  0.0 2.7 %shard_map.91 = (bf16[256,1536]{1,0:T(8,128)(2,1)S(1)}, bf16[144,1024]{1,0:T(8,128)(2,1)}, bf16[144,1024]{1,0:T(8,128)(2,1)S(1)}) custom-call(s32[1]{0:T(128)} %bitcast.8.place, bf16[256,1024]{1,0:T(8,128)(2,1)} %bitcast.11, s32[1,256]{1,0:T(1,128)} %refs_1_.3, s32[1,256]{1,0:T(1,128)} %refs_2_.3, bf16[64,1024]{1,0:T(8,128)(2,1)} %refs_3_.3, ...), custom_call_target="tpu_custom_call" | custom-call | flops 67108864 | bytes 3742724 | tf_op jit(solution)/shard_map/pallas_call | solution.py:25
  2.7 2.1 %collective-permute-start.2 = (bf16[256,1536]{1,0:T(8,128)(2,1)S(1)}, bf16[256,1536]{1,0:T(8,128)(2,1)S(1)}, u32[]{:S(2)}, u32[]{:S(2)}) collective-permute-start(bf16[256,1536]{1,0:T(8,128)(2,1)S(1)} %get-tuple-element.16.refs_4_), channel_id=1, source_target_pairs={{0,2},{1,3},{2,0},{3,1},{4,6},{5,7},{6,4},{7,5},{8,10},{9,11},{10,... | collective-permute-start | bytes 2359304 | tf_op jit(solution)/shard_map/ppermute | solution.py:227
  4.8 1.0 %collective-permute-start.3 = (bf16[256,1536]{1,0:T(8,128)(2,1)S(1)}, bf16[256,1536]{1,0:T(8,128)(2,1)S(1)}, u32[]{:S(2)}, u32[]{:S(2)}) collective-permute-start(bf16[256,1536]{1,0:T(8,128)(2,1)S(1)} %get-tuple-element.16.refs_4_), channel_id=1, source_target_pairs={{0,1},{1,0},{2,3},{3,2},{4,5},{5,4},{6,7},{7,6},{8,9},{9,8},{10,11... | collective-permute-start | bytes 2359304 | tf_op jit(solution)/shard_map/ppermute | solution.py:230
  5.8 16.3 %collective-permute-done.2.refs_5_ = bf16[256,1536]{1,0:T(8,128)(2,1)S(1)} collective-permute-done((bf16[256,1536]{1,0:T(8,128)(2,1)S(1)}, bf16[256,1536]{1,0:T(8,128)(2,1)S(1)}, u32[]{:S(2)}, u32[]{:S(2)}) %collective-permute-start.2) | collective-permute-done | bytes 786464 | tf_op jit(solution)/shard_map/ppermute | solution.py:227
  22.0 1.3 %collective-permute-start.4 = (bf16[256,1536]{1,0:T(8,128)(2,1)S(1)}, bf16[256,1536]{1,0:T(8,128)(2,1)S(1)}, u32[]{:S(2)}, u32[]{:S(2)}) collective-permute-start(bf16[256,1536]{1,0:T(8,128)(2,1)S(1)} %collective-permute-done.2.refs_5_), channel_id=1, source_target_pairs={{0,1},{1,0},{2,3},{3,2},{4,5},{5,4},{6,7},{7,6},{8,9},{9,8},{10,11... | collective-permute-start | bytes 2359304 | tf_op jit(solution)/shard_map/ppermute | solution.py:230
  23.3 4.3 %collective-permute-start = (bf16[144,1024]{1,0:T(8,128)(2,1)}, bf16[144,1024]{1,0:T(8,128)(2,1)}, u32[]{:S(2)}, u32[]{:S(2)}) collective-permute-start(bf16[144,1024]{1,0:T(8,128)(2,1)} %get-tuple-element.14.refs_0_), channel_id=1, source_target_pairs={{1,8},{3,10},{5,12},{7,14},{8,1},{10,3},{12,5},{14,7},{17,24},{19,... | collective-permute-start | bytes 884744 | tf_op jit(solution)/shard_map/ppermute | solution.py:224
  27.6 2.1 %collective-permute-start.1 = (bf16[144,1024]{1,0:T(8,128)(2,1)S(1)}, bf16[144,1024]{1,0:T(8,128)(2,1)}, u32[]{:S(2)}, u32[]{:S(2)}) collective-permute-start(bf16[144,1024]{1,0:T(8,128)(2,1)S(1)} %get-tuple-element.15.refs_1_), channel_id=1, source_target_pairs={{1,8},{3,10},{5,12},{7,14},{8,1},{10,3},{12,5},{14,7},{17,24},{19,... | collective-permute-start | bytes 884744 | tf_op jit(solution)/shard_map/ppermute | solution.py:224
  29.8 1.4 %collective-permute-start.5 = (bf16[144,1024]{1,0:T(8,128)(2,1)}, bf16[144,1024]{1,0:T(8,128)(2,1)}, u32[]{:S(2)}, u32[]{:S(2)}) collective-permute-start(bf16[144,1024]{1,0:T(8,128)(2,1)} %get-tuple-element.14.refs_0_), channel_id=1, source_target_pairs={{0,4},{2,6},{4,0},{6,2},{9,13},{11,15},{13,9},{15,11},{16,20},{18,... | collective-permute-start | bytes 884744 | tf_op jit(solution)/shard_map/ppermute | solution.py:224
  31.1 5.5 %collective-permute-done.refs_2_ = bf16[144,1024]{1,0:T(8,128)(2,1)} collective-permute-done((bf16[144,1024]{1,0:T(8,128)(2,1)}, bf16[144,1024]{1,0:T(8,128)(2,1)}, u32[]{:S(2)}, u32[]{:S(2)}) %collective-permute-start) | collective-permute-done | bytes 294944 | tf_op jit(solution)/shard_map/ppermute | solution.py:224
  36.6 1.4 %collective-permute-start.6 = (bf16[144,1024]{1,0:T(8,128)(2,1)S(1)}, bf16[144,1024]{1,0:T(8,128)(2,1)}, u32[]{:S(2)}, u32[]{:S(2)}) collective-permute-start(bf16[144,1024]{1,0:T(8,128)(2,1)S(1)} %get-tuple-element.15.refs_1_), channel_id=1, source_target_pairs={{0,4},{2,6},{4,0},{6,2},{9,13},{11,15},{13,9},{15,11},{16,20},{18,... | collective-permute-start | bytes 884744 | tf_op jit(solution)/shard_map/ppermute | solution.py:224
  38.0 4.1 %collective-permute-done.1.refs_3_ = bf16[144,1024]{1,0:T(8,128)(2,1)} collective-permute-done((bf16[144,1024]{1,0:T(8,128)(2,1)S(1)}, bf16[144,1024]{1,0:T(8,128)(2,1)}, u32[]{:S(2)}, u32[]{:S(2)}) %collective-permute-start.1) | collective-permute-done | bytes 294944 | tf_op jit(solution)/shard_map/ppermute | solution.py:224
  42.1 2.0 %collective-permute-start.7 = (bf16[144,1024]{1,0:T(8,128)(2,1)}, bf16[144,1024]{1,0:T(8,128)(2,1)}, u32[]{:S(2)}, u32[]{:S(2)}) collective-permute-start(bf16[144,1024]{1,0:T(8,128)(2,1)} %collective-permute-done.refs_2_), channel_id=1, source_target_pairs={{1,5},{3,7},{5,1},{7,3},{8,12},{10,14},{12,8},{14,10},{17,21},{19,... | collective-permute-start | bytes 884744 | tf_op jit(solution)/shard_map/ppermute | solution.py:224
  44.1 0.0 collective-permute-done.3.refs_6_
  44.1 3.3 %collective-permute-start.8 = (bf16[144,1024]{1,0:T(8,128)(2,1)}, bf16[144,1024]{1,0:T(8,128)(2,1)}, u32[]{:S(2)}, u32[]{:S(2)}) collective-permute-start(bf16[144,1024]{1,0:T(8,128)(2,1)} %collective-permute-done.1.refs_3_), channel_id=1, source_target_pairs={{1,5},{3,7},{5,1},{7,3},{8,12},{10,14},{12,8},{14,10},{17,21},{19,... | collective-permute-start | bytes 884744 | tf_op jit(solution)/shard_map/ppermute | solution.py:224
  47.5 0.1 pad_add_fusion.1.order
  47.6 0.0 collective-permute-done.4.refs_7_
  47.6 1.5 %collective-permute-start.12 = (bf16[1024,256]{1,0:T(8,128)(2,1)}, bf16[1024,256]{1,0:T(8,128)(2,1)}, u32[]{:S(2)}, u32[]{:S(2)}) collective-permute-start(bf16[1024,256]{1,0:T(8,128)(2,1)} %refs_6_.1), channel_id=1, source_target_pairs={{0,2},{1,3},{2,0},{3,1},{4,6},{5,7},{6,4},{7,5},{8,10},{9,11},{10,... | collective-permute-start | bytes 1572872 | tf_op jit(solution)/shard_map/ppermute | solution.py:227
  49.0 2.2 %shard_map.92 = (bf16[256,512]{1,0:T(8,128)(2,1)S(1)}, bf16[272,1024]{1,0:T(8,128)(2,1)S(1)}) custom-call(s32[4]{0:T(128)S(1)} %pad_add_fusion.1.order, s32[1]{0:T(128)} %bitcast.7.own, bf16[144,1024]{1,0:T(8,128)(2,1)} %get-tuple-element.14.refs_0_, bf16[144,1024]{1,0:T(8,128)(2,1)S(1)} %get-tuple-element.15.refs_1_, ...), custom_call_target="tpu_custom_call" | custom-call | flops 805306368 | bytes 5144596 | tf_op jit(solution)/shard_map/pallas_call | solution.py:25
  51.3 0.0 collective-permute-done.5.refs_0_
  51.3 0.1 collective-permute-start.9
  51.4 0.0 collective-permute-done.6.refs_1_
  51.4 0.0 collective-permute-done.7.refs_2_
  51.4 1.7 %collective-permute-done.8.refs_3_ = bf16[144,1024]{1,0:T(8,128)(2,1)} collective-permute-done((bf16[144,1024]{1,0:T(8,128)(2,1)}, bf16[144,1024]{1,0:T(8,128)(2,1)}, u32[]{:S(2)}, u32[]{:S(2)}) %collective-permute-start.8) | collective-permute-done | bytes 294944 | tf_op jit(solution)/shard_map/ppermute | solution.py:224
  53.1 2.3 %shard_map.93 = (bf16[256,512]{1,0:T(8,128)(2,1)S(1)}, bf16[272,1024]{1,0:T(8,128)(2,1)S(1)}) custom-call(s32[4]{0:T(128)S(1)} %pad_add_fusion.1.order, s32[1]{0:T(128)} %bitcast.7.own, bf16[144,1024]{1,0:T(8,128)(2,1)} %collective-permute-done.5.refs_0_, bf16[144,1024]{1,0:T(8,128)(2,1)} %collective-permute-done.6.refs_1_, ...), custom_call_target="tpu_custom_call" | custom-call | flops 805306368 | bytes 5144596 | tf_op jit(solution)/shard_map/pallas_call | solution.py:25
  55.4 0.1 collective-permute-start.10
  55.4 0.5 collective-permute-start.13
  55.9 0.0 collective-permute-done.12.refs_7_
  55.9 0.1 collective-permute-start.14
  56.0 0.0 collective-permute-done.9.refs_2_
  56.0 1.4 %collective-permute-done.10.refs_3_ = bf16[272,1024]{1,0:T(8,128)(2,1)S(1)} collective-permute-done((bf16[272,1024]{1,0:T(8,128)(2,1)S(1)}, bf16[272,1024]{1,0:T(8,128)(2,1)S(1)}, u32[]{:S(2)}, u32[]{:S(2)}) %collective-permute-start.10) | collective-permute-done | bytes 557088 | tf_op jit(solution)/shard_map/ppermute | solution.py:230
  57.4 4.8 %shard_map.94 = bf16[256,512]{1,0:T(8,128)(2,1)S(1)} custom-call(bf16[256,512]{1,0:T(8,128)(2,1)S(1)} %get-tuple-element.17.q, bf16[272,1024]{1,0:T(8,128)(2,1)S(1)} %get-tuple-element.18.refs_0_, bf16[272,1024]{1,0:T(8,128)(2,1)S(1)} %get-tuple-element.19.refs_1_, bf16[272,1024]{1,0:T(8,128)(2,1)S(1)} %collective-permute-done.9.refs_2_, ...), custom_call_target="tpu_custom_call" | custom-call | flops 1073741824 | bytes 2752512 | tf_op jit(solution)/shard_map/pallas_call | solution.py:25
  62.2 5.7 %collective-permute-start.11 = (bf16[256,512]{1,0:T(8,128)(2,1)S(1)}, bf16[256,512]{1,0:T(8,128)(2,1)S(1)}, u32[]{:S(2)}, u32[]{:S(2)}) collective-permute-start(bf16[256,512]{1,0:T(8,128)(2,1)S(1)} %shard_map.94), channel_id=1, source_target_pairs={{0,0},{8,1},{2,2},{10,3},{4,4},{12,5},{6,6},{14,7},{1,8},{9,9},{3,... | collective-permute-start | bytes 786440 | tf_op jit(solution)/shard_map/ppermute | solution.py:224
  68.0 4.8 %shard_map.96 = bf16[256,512]{1,0:T(8,128)(2,1)S(1)} custom-call(bf16[256,512]{1,0:T(8,128)(2,1)S(1)} %get-tuple-element.21.q, bf16[272,1024]{1,0:T(8,128)(2,1)S(1)} %get-tuple-element.18.refs_0_, bf16[272,1024]{1,0:T(8,128)(2,1)S(1)} %get-tuple-element.19.refs_1_, bf16[272,1024]{1,0:T(8,128)(2,1)S(1)} %collective-permute-done.9.refs_2_, ...), custom_call_target="tpu_custom_call" | custom-call | flops 1073741824 | bytes 2752512 | tf_op jit(solution)/shard_map/pallas_call | solution.py:25
  72.8 0.7 collective-permute-start.15
  73.5 0.1 pad_add_fusion.places
  73.6 0.0 collective-permute-done.13.refs_8_
  73.6 0.0 collective-permute-done.14.refs_9_
  73.6 1.3 %collective-permute-done.11.refs_5_ = bf16[256,512]{1,0:T(8,128)(2,1)S(1)} collective-permute-done((bf16[256,512]{1,0:T(8,128)(2,1)S(1)}, bf16[256,512]{1,0:T(8,128)(2,1)S(1)}, u32[]{:S(2)}, u32[]{:S(2)}) %collective-permute-start.11) | collective-permute-done | bytes 262176 | tf_op jit(solution)/shard_map/ppermute | solution.py:224
  74.9 3.3 %shard_map.95 = (f32[256,1024]{1,0:T(8,128)S(1)}, bf16[512,1024]{1,0:T(8,128)(2,1)S(1)}) custom-call(s32[2]{0:T(128)S(1)} %pad_add_fusion.places, s32[4]{0:T(128)S(1)} %pad_add_fusion.1.order, bf16[256,1024]{1,0:T(8,128)(2,1)} %bitcast.12, s32[1,256]{1,0:T(1,128)} %refs_1_.3, s32[1,256]{1,0:T(1,128)} %refs_2_.3, bf16[64,1024]{1,0:T(8,128)(2,1)} %refs_3_.3, ...), custom_call_target="tpu_custom_call" | custom-call | flops 268435456 | bytes 5244952 | tf_op jit(solution)/shard_map/pallas_call | solution.py:25
  78.2 2.4 %collective-permute-done.15.context = bf16[256,512]{1,0:T(8,128)(2,1)S(1)} collective-permute-done((bf16[256,512]{1,0:T(8,128)(2,1)S(1)}, bf16[256,512]{1,0:T(8,128)(2,1)S(1)}, u32[]{:S(2)}, u32[]{:S(2)}) %collective-permute-start.15) | collective-permute-done | bytes 262176 | tf_op jit(solution)/shard_map/ppermute | solution.py:224
  80.5 1.2 %shard_map.97 = bf16[256,1024]{1,0:T(8,128)(2,1)} custom-call(f32[256,1024]{1,0:T(8,128)S(1)} %get-tuple-element.20.base, bf16[256,512]{1,0:T(8,128)(2,1)S(1)} %collective-permute-done.15.context, bf16[512,1024]{1,0:T(8,128)(2,1)S(1)} %get-tuple-element.22.weight), custom_call_target="tpu_custom_call" | custom-call | flops 268435456 | bytes 2883584 | tf_op jit(solution)/shard_map/pallas_call | solution.py:25
Async XLA Ops:
  2.7 19.3 %collective-permute-start.2 = (bf16[256,1536]{1,0:T(8,128)(2,1)S(1)}, bf16[256,1536]{1,0:T(8,128)(2,1)S(1)}, u32[]{:S(2)}, u32[]{:S(2)}) collective-permute-start(bf16[256,1536]{1,0:T(8,128)(2,1)S(1)} %get-tuple-element.16.refs_4_), channel_id=1, source_target_pairs={{0,2},{1,3},{2,0},{3,1},{4,6},{5,7},{6,4},{7,5},{8,10},{9,11},{10,... | collective-permute-start | bytes 2359304 | tf_op jit(solution)/shard_map/ppermute | solution.py:227
  4.8 39.3 %collective-permute-start.3 = (bf16[256,1536]{1,0:T(8,128)(2,1)S(1)}, bf16[256,1536]{1,0:T(8,128)(2,1)S(1)}, u32[]{:S(2)}, u32[]{:S(2)}) collective-permute-start(bf16[256,1536]{1,0:T(8,128)(2,1)S(1)} %get-tuple-element.16.refs_4_), channel_id=1, source_target_pairs={{0,1},{1,0},{2,3},{3,2},{4,5},{5,4},{6,7},{7,6},{8,9},{9,8},{10,11... | collective-permute-start | bytes 2359304 | tf_op jit(solution)/shard_map/ppermute | solution.py:230
  22.0 25.5 %collective-permute-start.4 = (bf16[256,1536]{1,0:T(8,128)(2,1)S(1)}, bf16[256,1536]{1,0:T(8,128)(2,1)S(1)}, u32[]{:S(2)}, u32[]{:S(2)}) collective-permute-start(bf16[256,1536]{1,0:T(8,128)(2,1)S(1)} %collective-permute-done.2.refs_5_), channel_id=1, source_target_pairs={{0,1},{1,0},{2,3},{3,2},{4,5},{5,4},{6,7},{7,6},{8,9},{9,8},{10,11... | collective-permute-start | bytes 2359304 | tf_op jit(solution)/shard_map/ppermute | solution.py:230
  23.3 13.3 %collective-permute-start = (bf16[144,1024]{1,0:T(8,128)(2,1)}, bf16[144,1024]{1,0:T(8,128)(2,1)}, u32[]{:S(2)}, u32[]{:S(2)}) collective-permute-start(bf16[144,1024]{1,0:T(8,128)(2,1)} %get-tuple-element.14.refs_0_), channel_id=1, source_target_pairs={{1,8},{3,10},{5,12},{7,14},{8,1},{10,3},{12,5},{14,7},{17,24},{19,... | collective-permute-start | bytes 884744 | tf_op jit(solution)/shard_map/ppermute | solution.py:224
  27.6 14.5 %collective-permute-start.1 = (bf16[144,1024]{1,0:T(8,128)(2,1)S(1)}, bf16[144,1024]{1,0:T(8,128)(2,1)}, u32[]{:S(2)}, u32[]{:S(2)}) collective-permute-start(bf16[144,1024]{1,0:T(8,128)(2,1)S(1)} %get-tuple-element.15.refs_1_), channel_id=1, source_target_pairs={{1,8},{3,10},{5,12},{7,14},{8,1},{10,3},{12,5},{14,7},{17,24},{19,... | collective-permute-start | bytes 884744 | tf_op jit(solution)/shard_map/ppermute | solution.py:224
  29.8 21.5 %collective-permute-start.5 = (bf16[144,1024]{1,0:T(8,128)(2,1)}, bf16[144,1024]{1,0:T(8,128)(2,1)}, u32[]{:S(2)}, u32[]{:S(2)}) collective-permute-start(bf16[144,1024]{1,0:T(8,128)(2,1)} %get-tuple-element.14.refs_0_), channel_id=1, source_target_pairs={{0,4},{2,6},{4,0},{6,2},{9,13},{11,15},{13,9},{15,11},{16,20},{18,... | collective-permute-start | bytes 884744 | tf_op jit(solution)/shard_map/ppermute | solution.py:224
  36.6 14.7 %collective-permute-start.6 = (bf16[144,1024]{1,0:T(8,128)(2,1)S(1)}, bf16[144,1024]{1,0:T(8,128)(2,1)}, u32[]{:S(2)}, u32[]{:S(2)}) collective-permute-start(bf16[144,1024]{1,0:T(8,128)(2,1)S(1)} %get-tuple-element.15.refs_1_), channel_id=1, source_target_pairs={{0,4},{2,6},{4,0},{6,2},{9,13},{11,15},{13,9},{15,11},{16,20},{18,... | collective-permute-start | bytes 884744 | tf_op jit(solution)/shard_map/ppermute | solution.py:224
  42.1 9.2 %collective-permute-start.7 = (bf16[144,1024]{1,0:T(8,128)(2,1)}, bf16[144,1024]{1,0:T(8,128)(2,1)}, u32[]{:S(2)}, u32[]{:S(2)}) collective-permute-start(bf16[144,1024]{1,0:T(8,128)(2,1)} %collective-permute-done.refs_2_), channel_id=1, source_target_pairs={{1,5},{3,7},{5,1},{7,3},{8,12},{10,14},{12,8},{14,10},{17,21},{19,... | collective-permute-start | bytes 884744 | tf_op jit(solution)/shard_map/ppermute | solution.py:224
  44.1 8.9 %collective-permute-start.8 = (bf16[144,1024]{1,0:T(8,128)(2,1)}, bf16[144,1024]{1,0:T(8,128)(2,1)}, u32[]{:S(2)}, u32[]{:S(2)}) collective-permute-start(bf16[144,1024]{1,0:T(8,128)(2,1)} %collective-permute-done.1.refs_3_), channel_id=1, source_target_pairs={{1,5},{3,7},{5,1},{7,3},{8,12},{10,14},{12,8},{14,10},{17,21},{19,... | collective-permute-start | bytes 884744 | tf_op jit(solution)/shard_map/ppermute | solution.py:224
  47.6 8.4 %collective-permute-start.12 = (bf16[1024,256]{1,0:T(8,128)(2,1)}, bf16[1024,256]{1,0:T(8,128)(2,1)}, u32[]{:S(2)}, u32[]{:S(2)}) collective-permute-start(bf16[1024,256]{1,0:T(8,128)(2,1)} %refs_6_.1), channel_id=1, source_target_pairs={{0,2},{1,3},{2,0},{3,1},{4,6},{5,7},{6,4},{7,5},{8,10},{9,11},{10,... | collective-permute-start | bytes 1572872 | tf_op jit(solution)/shard_map/ppermute | solution.py:227
  51.3 4.8 %collective-permute-start.9 = (bf16[272,1024]{1,0:T(8,128)(2,1)S(1)}, bf16[272,1024]{1,0:T(8,128)(2,1)S(1)}, u32[]{:S(2)}, u32[]{:S(2)}) collective-permute-start(bf16[272,1024]{1,0:T(8,128)(2,1)S(1)} %get-tuple-element.18.refs_0_), channel_id=1, source_target_pairs={{0,1},{1,0},{2,3},{3,2},{4,5},{5,4},{6,7},{7,6},{8,9},{9,8},{10,11... | collective-permute-start | bytes 1671176 | tf_op jit(solution)/shard_map/ppermute | solution.py:230
  55.4 2.0 %collective-permute-start.10 = (bf16[272,1024]{1,0:T(8,128)(2,1)S(1)}, bf16[272,1024]{1,0:T(8,128)(2,1)S(1)}, u32[]{:S(2)}, u32[]{:S(2)}) collective-permute-start(bf16[272,1024]{1,0:T(8,128)(2,1)S(1)} %get-tuple-element.19.refs_1_), channel_id=1, source_target_pairs={{0,1},{1,0},{2,3},{3,2},{4,5},{5,4},{6,7},{7,6},{8,9},{9,8},{10,11... | collective-permute-start | bytes 1671176 | tf_op jit(solution)/shard_map/ppermute | solution.py:230
  55.4 18.2 %collective-permute-start.13 = (bf16[1024,256]{1,0:T(8,128)(2,1)}, bf16[1024,256]{1,0:T(8,128)(2,1)S(1)}, u32[]{:S(2)}, u32[]{:S(2)}) collective-permute-start(bf16[1024,256]{1,0:T(8,128)(2,1)} %refs_6_.1), channel_id=1, source_target_pairs={{0,1},{1,0},{2,3},{3,2},{4,5},{5,4},{6,7},{7,6},{8,9},{9,8},{10,11... | collective-permute-start | bytes 1572872 | tf_op jit(solution)/shard_map/ppermute | solution.py:230
  55.9 17.7 %collective-permute-start.14 = (bf16[1024,256]{1,0:T(8,128)(2,1)}, bf16[1024,256]{1,0:T(8,128)(2,1)S(1)}, u32[]{:S(2)}, u32[]{:S(2)}) collective-permute-start(bf16[1024,256]{1,0:T(8,128)(2,1)} %collective-permute-done.12.refs_7_), channel_id=1, source_target_pairs={{0,1},{1,0},{2,3},{3,2},{4,5},{5,4},{6,7},{7,6},{8,9},{9,8},{10,11... | collective-permute-start | bytes 1572872 | tf_op jit(solution)/shard_map/ppermute | solution.py:230
  62.2 12.7 %collective-permute-start.11 = (bf16[256,512]{1,0:T(8,128)(2,1)S(1)}, bf16[256,512]{1,0:T(8,128)(2,1)S(1)}, u32[]{:S(2)}, u32[]{:S(2)}) collective-permute-start(bf16[256,512]{1,0:T(8,128)(2,1)S(1)} %shard_map.94), channel_id=1, source_target_pairs={{0,0},{8,1},{2,2},{10,3},{4,4},{12,5},{6,6},{14,7},{1,8},{9,9},{3,... | collective-permute-start | bytes 786440 | tf_op jit(solution)/shard_map/ppermute | solution.py:224
  72.8 7.8 %collective-permute-start.15 = (bf16[256,512]{1,0:T(8,128)(2,1)S(1)}, bf16[256,512]{1,0:T(8,128)(2,1)S(1)}, u32[]{:S(2)}, u32[]{:S(2)}) collective-permute-start(bf16[256,512]{1,0:T(8,128)(2,1)S(1)} %shard_map.96), channel_id=1, source_target_pairs={{4,0},{12,1},{6,2},{14,3},{0,4},{8,5},{2,6},{10,7},{5,8},{13,9},{7... | collective-permute-start | bytes 786440 | tf_op jit(solution)/shard_map/ppermute | solution.py:224

commit v3 on v2

--- a/solution.py
+++ b/solution.py
@@ -12,7 +12,6 @@
 floor_score = -1e30
 epsilon = 1e-06
 VM = pl.BlockSpec(memory_space=pltpu.VMEM)
-SM = pl.BlockSpec(memory_space=pltpu.SMEM)
 PAD = 16
 CUTS = 2
 
@@ -20,15 +19,24 @@
 HB = pl.BlockSpec(memory_space=pltpu.HBM)
 
 
-def call(kernel, outs, args, specs, flops, scratch=(), limit=16 << 20):
+def here():
+    half, lanes = lax.axis_size("ctx") // 2, lax.axis_size("fsdp")
+    z, f = lax.axis_index("ctx"), lax.axis_index("fsdp")
+    chips, core = lanes // 2, lax.rem(f, 2)
+    sources = [2 * lax.rem(lax.div(f, 2) + chips - by, chips) + core for by in range(chips)]
+    order = sources + [s + 1 - 2 * core for s in sources]
+    return lax.rem(z, half), lax.div(z, half) == core, order
+
+
+def call(kernel, outs, args, specs, flops, scratch=(), away=0):
     moved = sum(a.size * a.dtype.itemsize for a in (*args, *outs))
     return pl.pallas_call(
         kernel,
         out_shape=outs,
         in_specs=specs,
-        out_specs=[VM] * len(outs),
+        out_specs=[VM] * (len(outs) - away) + [HB] * away,
         scratch_shapes=scratch,
-        compiler_params=pltpu.CompilerParams(vmem_limit_bytes=limit),
+        compiler_params=pltpu.CompilerParams(vmem_limit_bytes=16 << 20),
         cost_estimate=pl.CostEstimate(flops=flops, bytes_accessed=moved, transcendentals=0),
     )(*args)
 
@@ -45,13 +53,14 @@
     )
 
 
-def embed_kernel(place, *refs):
+def embed_kernel(*refs):
     inputs, weight, share, blocks = refs[:7], refs[7], refs[8], refs[9 : 9 + CUTS]
-    local, sems = refs[9 + CUTS : 16 + CUTS], refs[16 + CUTS]
+    kept, refs = refs[9 + CUTS : 9 + 2 * CUTS], refs[9 + 2 * CUTS :]
+    local, sems = refs[:7], refs[7]
     copies = [pltpu.make_async_copy(a, b, sems.at[i]) for i, (a, b) in enumerate(zip(inputs, local))]
-    group = share.shape[1] // 3
+    group, (place, _, _) = share.shape[1] // 3, here()
     for part in range(3):
-        first = pl.multiple_of(part * (weight.shape[1] // 3) + place[0] * group, group)
+        first = pl.multiple_of(part * (weight.shape[1] // 3) + place * group, group)
         copies.append(
             pltpu.make_async_copy(
                 weight.at[:, pl.ds(first, group)],
@@ -75,40 +84,66 @@
         block[:cut, :] = normed[i * cut : (i + 1) * cut]
         block[cut:, :] = jnp.zeros((PAD, block.shape[1]), jnp.bfloat16)
         block[cut:, :cut] = labels[:, i * cut : (i + 1) * cut]
+        copies.append(pltpu.make_async_copy(block, kept[i], sems.at[10 + i]))
+        copies[-1].start()
     for copy in copies[7:]:
         copy.wait()
 
 
-def qkv_kernel(pieces, choose, tile, scale, order, own, *refs):
-    ways, weights = (refs[:CUTS], refs[CUTS : 2 * CUTS]), refs[2 * CUTS : 2 * CUTS + pieces]
-    q_out, kv_out, block = refs[2 * CUTS + pieces :]
-    length = q_out.shape[0]
-    depth, width = weights[0].shape
-    third = width // 3
+def matched(block, weights, columns):
+    depth, length = weights[0].shape[0], block.shape[0] - PAD
+    _, _, order = here()
+    total = None
+    for piece, weight in enumerate(weights):
+        lanes = pl.ds(pl.multiple_of(order[piece] * depth, depth), depth)
+        part = jnp.dot(
+            block[:length, lanes], weight[:, columns], preferred_element_type=jnp.float32
+        )
+        total = part if total is None else total + part
+    return total.astype(jnp.bfloat16)
+
+
+def pick_kernel(*refs):
+    away, two, block, one, sems = refs[:CUTS], refs[CUTS : 2 * CUTS], refs[-CUTS - 2], refs[-CUTS - 1 : -1], refs[-1]
+    copies = [pltpu.make_async_copy(a, b, sems.at[i]) for i, (a, b) in enumerate(zip(away, one))]
+    for copy in copies:
+        copy.start()
+    for copy in copies:
+        copy.wait()
+    pick(one, two, block)
+
+
+def pick(one, two, block):
+    _, own, _ = here()
+    length = block.shape[0] - PAD
     cut = length // CUTS
+    block[length:, :] = jnp.zeros((PAD, block.shape[1]), jnp.bfloat16)
+    for i, (a, b) in enumerate(zip(one, two)):
+        part = jnp.where(own, a[...], b[...])
+        block[i * cut : (i + 1) * cut, :] = part[:cut]
+        block[length:, i * cut : (i + 1) * cut] = part[cut:, :cut]
+
+
+def keys_kernel(pieces, tile, *refs):
+    if len(refs) == 2 + pieces:
+        block, weights, kv_out = refs[0], refs[1:-1], refs[-1]
+    else:
+        weights, (block, kv_out) = refs[2 * CUTS : 2 * CUTS + pieces], refs[2 * CUTS + pieces :]
+        pick(refs[:CUTS], refs[CUTS : 2 * CUTS], block)
+    length, third = block.shape[0] - PAD, weights[0].shape[1] // 3
     kv_out[length:, :] = jnp.zeros((PAD, 2 * third), jnp.bfloat16)
-    for i, (one, two) in enumerate(zip(*ways)):
-        if choose:
-            part = jnp.where(own[0] == 1, one[...], two[...])
-        else:
-            part = one[...] + two[...]
-        block[i * cut : (i + 1) * cut, :] = part[:cut]
-        kv_out[length:, i * cut : (i + 1) * cut] = part[cut:, :cut]
-    for first in range(0, width, tile):
-        total = None
-        for piece in range(pieces):
-            lanes = pl.ds(pl.multiple_of(order[piece] * depth, depth), depth)
-            part = jnp.dot(
-                block[:, lanes],
-                weights[piece][:, first : first + tile],
-                preferred_element_type=jnp.float32,
-            )
-            total = part if total is None else total + part
-        total = total.astype(jnp.bfloat16)
-        if first < third:
-            q_out[:, first : first + tile] = total * jnp.bfloat16(scale)
-        else:
-            kv_out[:length, first - third : first - third + tile] = total
+    kv_out[length:, :length] = block[length:, :length]
+    for first in range(0, 2 * third, tile):
+        columns = slice(third + first, third + first + tile)
+        kv_out[:length, first : first + tile] = matched(block, weights, columns)
+
+
+def queries_kernel(slots, pieces, tile, scale, *refs):
+    blocks, weights, outs = refs[:slots], refs[slots : slots + pieces], refs[slots + pieces :]
+    for block, out in zip(blocks, outs):
+        for first in range(0, out.shape[1], tile):
+            columns = slice(first, first + tile)
+            out[:, columns] = matched(block, weights, columns) * jnp.bfloat16(scale)
 
 
 def attend_kernel(slots, slot, head, q, *refs):
@@ -158,10 +193,10 @@
         out[:, lanes] = jnp.where(lane < head, mixed[0], mixed[1]).astype(jnp.bfloat16)
         return carry
 
-    lax.fori_loop(0, third // (2 * head), pair, 0)
-
-
-def first_kernel(slots, pieces, places, order, *refs):
+    lax.fori_loop(0, third // (2 * head), pair, 0, unroll=True)
+
+
+def first_kernel(slots, pieces, *refs):
     inputs, refs = refs[:5], refs[5:]
     contexts, weights = refs[: slots - 1], refs[slots - 1 : slots - 1 + pieces]
     out, kept = refs[slots - 1 + pieces : slots + 1 + pieces]
@@ -173,7 +208,10 @@
         copy.wait()
     out[...] = embedding(*local)
     width, span = kept.shape[0], weights[0].shape[1]
-    rows = [pl.ds(pl.multiple_of(places[j] * width, width), width) for j in range(slots)]
+    place, _, order = here()
+    rows = [
+        pl.ds(pl.multiple_of(lax.rem(place + j, slots) * width, width), width) for j in range(slots)
+    ]
     for piece, weight in enumerate(weights):
         lanes = pl.ds(pl.multiple_of(order[piece] * span, span), span)
         kept[:, lanes] = weight[rows[-1], :]
@@ -192,30 +230,32 @@
 ):
     n, lanes = lax.axis_size("ctx"), lax.axis_size("fsdp")
     half, chips = n // 2, lanes // 2
-    z, f = lax.axis_index("ctx"), lax.axis_index("fsdp")
+    own = lax.axis_index("ctx") // half == lax.axis_index("fsdp") % 2
     length, model = patches.shape[1:]
     head = model // HEADS
     group = model // half
-    place = z % half
-
-    def spread(j, near=True, far=True):
+
+    def spread(j):
         pairs = []
         for a in range(n):
             for b in range(lanes):
                 core = b % 2
-                here = a // half == core
                 to = core * half + (a % half + j) % half
-                if near if here else far:
-                    pairs.append((a * lanes + b, to * lanes + b - core + (core if here else 1 - core)))
+                to_core = core if a // half == core else 1 - core
+                pairs.append((a * lanes + b, to * lanes + b - core + to_core))
         return pairs
 
-    def around(j):
+    def around(j, near):
         return [
             (a * lanes + b, (a - a % half + (a % half + j) % half) * lanes + b)
             for a in range(n)
             for b in range(lanes)
-            if a // half != b % 2
+            if (a // half == b % 2) == near
         ]
+
+    def moves(near, far):
+        holders = {p for p, _ in around(0, True)}
+        return [p for p in near if p[0] in holders] + [p for p in far if p[0] not in holders]
 
     def send_cuts(values, pairs):
         return [send(value, pairs) for value in values]
@@ -233,8 +273,6 @@
         own = [piece] + [along(piece, by) for by in range(1, chips)]
         return own + [partner(p) for p in own]
 
-    sources = [2 * ((f // 2 - by) % chips) + f % 2 for by in range(chips)]
-    order = jnp.stack(sources + [s ^ 1 for s in sources]).astype(jnp.int32)
     depth = qkv_weight.shape[0]
     shape = jax.ShapeDtypeStruct
     inputs = (
@@ -248,37 +286,55 @@
     )
     kept = [pltpu.with_memory_space_constraint(a, pltpu.HBM) for a in (*inputs, qkv_weight)]
     local = [pltpu.VMEM(a.shape, a.dtype) for a in inputs]
-    share, *block = call(
+    share, *made = call(
         embed_kernel,
         [
             shape((depth, 3 * group), jnp.bfloat16),
-            *[shape((length // CUTS + PAD, model), jnp.bfloat16)] * CUTS,
+            *[shape((length // CUTS + PAD, model), jnp.bfloat16)] * (2 * CUTS),
         ],
-        (place.reshape(1).astype(jnp.int32), *kept),
-        [SM] + [HB] * 8,
+        kept,
+        [HB] * 8,
         4 * length * row_table.shape[0] * model,
-        scratch=local + [pltpu.SemaphoreType.DMA((10,))],
-    )
+        scratch=local + [pltpu.SemaphoreType.DMA((10 + CUTS,))],
+        away=CUTS,
+    )
+    block, parked = made[:CUTS], made[CUTS:]
     weights = gather(share)
     out_weights = gather(out_weight)
-    own = (z // half == f % 2).astype(jnp.int32).reshape(1)
-    first = send_cuts(block, spread(0, near=False))
-    blocks = [[block, first]] + [
-        [send_cuts(block, spread(j, far=False)), send_cuts(first, around(j))]
-        for j in range(1, half)
-    ]
-    queries, keys = [], []
-    for j, parts in enumerate(blocks):
-        q, kv = call(
-            functools.partial(qkv_kernel, lanes, j == 0, min(group, 256), 1.0 / head**0.5),
-            [shape((length, group), jnp.bfloat16), shape((length + PAD, 2 * group), jnp.bfloat16)],
-            (order, own, *parts[0], *parts[1], *weights),
-            [SM, SM] + [VM] * (2 * CUTS + lanes),
-            2 * length * model * 3 * group,
-            scratch=[pltpu.VMEM((length, model), jnp.bfloat16)],
-        )
-        queries.append(q)
+    first = send_cuts(block, moves(around(1 % half, True), spread(0)))
+    whole = shape((length + PAD, model), jnp.bfloat16)
+    (picked,) = call(
+        pick_kernel,
+        [whole],
+        (*parked, *first),
+        [HB] * CUTS + [VM] * CUTS,
+        0,
+        scratch=[pltpu.VMEM(a.shape, a.dtype) for a in block] + [pltpu.SemaphoreType.DMA((CUTS,))],
+    )
+    blocks = [(picked,), (*first, *send_cuts(first, around(1, False)))]
+    for j in range(2, half):
+        held = [jnp.where(own, a, b) for a, b in zip(block, first)]
+        held = send_cuts(held, around(j, True) + around(j, False))
+        blocks.append((*held, *held))
+    tile = min(group, 256)
+    slots, keys = [], []
+    for j, ways in enumerate(blocks):
+        *slot, kv = call(
+            functools.partial(keys_kernel, lanes, tile),
+            [whole] * (j > 0) + [shape((length + PAD, 2 * group), jnp.bfloat16)],
+            (*ways, *weights),
+            [VM] * (len(ways) + lanes),
+            4 * length * model * group,
+        )
+        slots += slot or [picked]
         keys.append(kv)
+    queries = call(
+        functools.partial(queries_kernel, half, lanes, tile, 1.0 / head**0.5),
+        [shape((length, group), jnp.bfloat16)] * half,
+        (*slots, *weights),
+        [VM] * (half + lanes),
+        2 * half * length * model * group,
+    )
     keys += [partner(kv) for kv in keys]
     contexts = []
     for j in range(half):
@@ -294,12 +350,11 @@
             ],
         )
         contexts.append(send(context, [(b, a) for a, b in spread(j)]))
-    places = jnp.stack([(place + j) % half for j in range(half)]).astype(jnp.int32)
     base, kept_rows = call(
         functools.partial(first_kernel, half, lanes),
         [shape((length, model), jnp.float32), shape((group, model), jnp.bfloat16)],
-        (places, order, *kept[:5], *contexts[:-1], *out_weights),
-        [SM, SM] + [HB] * 5 + [VM] * (half - 1 + lanes),
+        (*kept[:5], *contexts[:-1], *out_weights),
+        [HB] * 5 + [VM] * (half - 1 + lanes),
         2 * length * model * (model - group),
         scratch=local[:5] + [pltpu.SemaphoreType.DMA((5,))],
     )

time: 82.1 us -> 75.5 us (0.920)
  the two profiles are of different devices: /device:TPU:1 before, /device:TPU:0 now
where the time goes in v3:
time: 75.5 us; the launch traced here: 75.3 us
  waiting for transfers between devices  45.5 us (60%)
  starting transfers between devices  15.6 us (21%)
  Pallas kernels  14 us (19%)
    ppermute x2, waiting for transfers between devices, along(): lax.ppermute(value, 'fsdp', [(i, (i + 2 * by) % lanes) for i in range(lan...  22.8 us
    ppermute x6, waiting for transfers between devices, send(): return lax.ppermute(value, ('ctx', 'fsdp'), pairs)  22.6 us
    pallas_call x9, Pallas kernels, call(): pl.pallas_call(kernel, out_shape=outs, in_specs=specs, out_specs=[VM] * (...  14 us
    ppermute x6, starting transfers between devices, partner(): return lax.ppermute(value, 'fsdp', [(i, i ^ 1) for i in range(lanes)])  5.85 us
    ppermute x6, starting transfers between devices, send(): return lax.ppermute(value, ('ctx', 'fsdp'), pairs)  4.96 us
    ppermute x2, starting transfers between devices, along(): lax.ppermute(value, 'fsdp', [(i, (i + 2 * by) % lanes) for i in range(lan...  4.83 us
  transfers between devices with their start and end apart: 14, of which 5 were waited for; matrix products, arithmetic and copies ran while one was open for 0% of the time, Pallas kernels for 14%

profile of v3, /device:TPU:0, one launch (start us, length us, event | category | flops | bytes accessed | tf_op | source)
XLA Modules:
  0.0 75.3 jit_solution(8333396300096496097)
XLA Ops:
  0.0 0.0 copy-start
  0.0 2.2 %shard_map.91 = (bf16[256,1536]{1,0:T(8,128)(2,1)S(1)}, bf16[144,1024]{1,0:T(8,128)(2,1)S(1)}, bf16[144,1024]{1,0:T(8,128)(2,1)S(1)}, bf16[144,1024]{1,0:T(8,128)(2,1)S(1)}, bf16[144,1024]{1,0:T(8,128)(2,1)S(1)}) custom-call(bf16[256,1024]{1,0:T(8,128)(2,1)} %bitcast.3, s32[1,256]{1,0:T(1,128)} %refs_1_.3, s32[1,256]{1,0:T(1,128)} %refs_2_.3, ...), custom_call_target="tpu_custom_call" | custom-call | flops 67108864 | bytes 4332544 | tf_op jit(solution)/shard_map/pallas_call | solution.py:33
  2.2 3.0 %collective-permute-start.4 = (bf16[256,1536]{1,0:T(8,128)(2,1)S(1)}, bf16[256,1536]{1,0:T(8,128)(2,1)S(1)}, u32[]{:S(2)}, u32[]{:S(2)}) collective-permute-start(bf16[256,1536]{1,0:T(8,128)(2,1)S(1)} %get-tuple-element.20.refs_4_.refs_2_.refs_1_), channel_id=1, source_target_pairs={{0,2},{1,3},{2,0},{3,1},{4,6},{5,7},{6,4},{7,5},{8,10},{9,11},{10,... | collective-permute-start | bytes 2359304 | tf_op jit(solution)/shard_map/ppermute | solution.py:267
  5.2 0.0 collective-permute-start.5
  5.2 17.5 %collective-permute-done.4.refs_5_.refs_3_.refs_2_ = bf16[256,1536]{1,0:T(8,128)(2,1)S(1)} collective-permute-done((bf16[256,1536]{1,0:T(8,128)(2,1)S(1)}, bf16[256,1536]{1,0:T(8,128)(2,1)S(1)}, u32[]{:S(2)}, u32[]{:S(2)}) %collective-permute-start.4) | collective-permute-done | bytes 786464 | tf_op jit(solution)/shard_map/ppermute | solution.py:267
  22.8 0.0 collective-permute-start.6
  22.8 1.8 %collective-permute-start = (bf16[144,1024]{1,0:T(8,128)(2,1)S(1)}, bf16[144,1024]{1,0:T(8,128)(2,1)S(1)}, u32[]{:S(2)}, u32[]{:S(2)}) collective-permute-start(bf16[144,1024]{1,0:T(8,128)(2,1)S(1)} %get-tuple-element.18), channel_id=1, source_target_pairs={{0,4},{2,6},{4,0},{6,2},{9,13},{11,15},{13,9},{15,11},{1,8},{3,10}... | collective-permute-start | bytes 884744 | tf_op jit(solution)/shard_map/ppermute | solution.py:264
  24.6 0.2 collective-permute-start.1
  24.8 8.0 %collective-permute-done.refs_2_.refs_0_ = bf16[144,1024]{1,0:T(8,128)(2,1)S(1)} collective-permute-done((bf16[144,1024]{1,0:T(8,128)(2,1)S(1)}, bf16[144,1024]{1,0:T(8,128)(2,1)S(1)}, u32[]{:S(2)}, u32[]{:S(2)}) %collective-permute-start) | collective-permute-done | bytes 294944 | tf_op jit(solution)/shard_map/ppermute | solution.py:264
  32.8 0.7 collective-permute-start.2
  33.5 6.0 %collective-permute-done.1.refs_3_.refs_1_ = bf16[144,1024]{1,0:T(8,128)(2,1)S(1)} collective-permute-done((bf16[144,1024]{1,0:T(8,128)(2,1)S(1)}, bf16[144,1024]{1,0:T(8,128)(2,1)S(1)}, u32[]{:S(2)}, u32[]{:S(2)}) %collective-permute-start.1) | collective-permute-done | bytes 294944 | tf_op jit(solution)/shard_map/ppermute | solution.py:264
  39.5 0.7 collective-permute-start.3
  40.2 0.0 copy-done
  40.2 1.8 %collective-permute-start.10 = (bf16[1024,256]{1,0:T(8,128)(2,1)S(1)}, bf16[1024,256]{1,0:T(8,128)(2,1)S(1)}, u32[]{:S(2)}, u32[]{:S(2)}) collective-permute-start(bf16[1024,256]{1,0:T(8,128)(2,1)S(1)} %copy-done), channel_id=1, source_target_pairs={{0,2},{1,3},{2,0},{3,1},{4,6},{5,7},{6,4},{7,5},{8,10},{9,11},{10,... | collective-permute-start | bytes 1572872 | tf_op jit(solution)/shard_map/ppermute | solution.py:267
  42.0 0.2 shard_map.92.refs_0_
  42.2 0.0 collective-permute-done.5.refs_6_.refs_4_.refs_3_
  42.2 0.0 collective-permute-done.6.refs_7_.refs_5_.refs_4_
  42.2 0.7 shard_map.95.refs_0_
  43.0 2.1 %collective-permute-start.7 = (bf16[272,1024]{1,0:T(8,128)(2,1)S(1)}, bf16[272,1024]{1,0:T(8,128)(2,1)S(1)}, u32[]{:S(2)}, u32[]{:S(2)}) collective-permute-start(bf16[272,1024]{1,0:T(8,128)(2,1)S(1)} %shard_map.95.refs_0_), channel_id=1, source_target_pairs={{0,1},{1,0},{2,3},{3,2},{4,5},{5,4},{6,7},{7,6},{8,9},{9,8},{10,11... | collective-permute-start | bytes 1671176 | tf_op jit(solution)/shard_map/ppermute | solution.py:270
  45.1 0.0 collective-permute-done.2.refs_2_
  45.1 0.0 collective-permute-done.3.refs_3_
  45.1 0.8 %shard_map.93 = (bf16[272,1024]{1,0:T(8,128)(2,1)S(1)}, bf16[272,1024]{1,0:T(8,128)(2,1)S(1)}) custom-call(bf16[144,1024]{1,0:T(8,128)(2,1)S(1)} %collective-permute-done.refs_2_.refs_0_, bf16[144,1024]{1,0:T(8,128)(2,1)S(1)} %collective-permute-done.1.refs_3_.refs_1_, bf16[144,1024]{1,0:T(8,128)(2,1)S(1)} %collective-permute-done.2.refs_2_, ...), custom_call_target="tpu_custom_call" | custom-call | flops 536870912 | bytes 5439488 | tf_op jit(solution)/shard_map/pallas_call | solution.py:33
  45.9 2.2 %collective-permute-start.8 = (bf16[272,1024]{1,0:T(8,128)(2,1)S(1)}, bf16[272,1024]{1,0:T(8,128)(2,1)S(1)}, u32[]{:S(2)}, u32[]{:S(2)}) collective-permute-start(bf16[272,1024]{1,0:T(8,128)(2,1)S(1)} %get-tuple-element.23.refs_1_), channel_id=1, source_target_pairs={{0,1},{1,0},{2,3},{3,2},{4,5},{5,4},{6,7},{7,6},{8,9},{9,8},{10,11... | collective-permute-start | bytes 1671176 | tf_op jit(solution)/shard_map/ppermute | solution.py:270
  48.1 0.1 collective-permute-start.11
  48.1 5.3 %collective-permute-done.10.refs_7_ = bf16[1024,256]{1,0:T(8,128)(2,1)S(1)} collective-permute-done((bf16[1024,256]{1,0:T(8,128)(2,1)S(1)}, bf16[1024,256]{1,0:T(8,128)(2,1)S(1)}, u32[]{:S(2)}, u32[]{:S(2)}) %collective-permute-start.10) | collective-permute-done | bytes 524320 | tf_op jit(solution)/shard_map/ppermute | solution.py:267
  53.4 1.5 %collective-permute-start.12 = (bf16[1024,256]{1,0:T(8,128)(2,1)S(1)}, bf16[1024,256]{1,0:T(8,128)(2,1)S(1)}, u32[]{:S(2)}, u32[]{:S(2)}) collective-permute-start(bf16[1024,256]{1,0:T(8,128)(2,1)S(1)} %collective-permute-done.10.refs_7_), channel_id=1, source_target_pairs={{0,1},{1,0},{2,3},{3,2},{4,5},{5,4},{6,7},{7,6},{8,9},{9,8},{10,11... | collective-permute-start | bytes 1572872 | tf_op jit(solution)/shard_map/ppermute | solution.py:270
  54.9 0.7 shard_map.94
  55.6 0.0 collective-permute-done.7.refs_2_
  55.6 0.0 collective-permute-done.8.refs_3_
  55.6 3.0 %shard_map.96 = bf16[256,512]{1,0:T(8,128)(2,1)S(1)} custom-call(bf16[256,512]{1,0:T(8,128)(2,1)S(1)} %get-tuple-element.22.q, bf16[272,1024]{1,0:T(8,128)(2,1)S(1)} %shard_map.95.refs_0_, bf16[272,1024]{1,0:T(8,128)(2,1)S(1)} %get-tuple-element.23.refs_1_, bf16[272,1024]{1,0:T(8,128)(2,1)S(1)} %collective-permute-done.7.refs_2_, ...), custom_call_target="tpu_custom_call" | custom-call | flops 1073741824 | bytes 2752512 | tf_op jit(solution)/shard_map/pallas_call | solution.py:33
  58.7 0.7 collective-permute-start.9
  59.4 3.0 %shard_map.98 = bf16[256,512]{1,0:T(8,128)(2,1)S(1)} custom-call(bf16[256,512]{1,0:T(8,128)(2,1)S(1)} %get-tuple-element.25.q, bf16[272,1024]{1,0:T(8,128)(2,1)S(1)} %shard_map.95.refs_0_, bf16[272,1024]{1,0:T(8,128)(2,1)S(1)} %get-tuple-element.23.refs_1_, bf16[272,1024]{1,0:T(8,128)(2,1)S(1)} %collective-permute-done.7.refs_2_, ...), custom_call_target="tpu_custom_call" | custom-call | flops 1073741824 | bytes 2752512 | tf_op jit(solution)/shard_map/pallas_call | solution.py:33
  62.4 0.9 %collective-permute-start.13 = (bf16[256,512]{1,0:T(8,128)(2,1)S(1)}, bf16[256,512]{1,0:T(8,128)(2,1)S(1)}, u32[]{:S(2)}, u32[]{:S(2)}) collective-permute-start(bf16[256,512]{1,0:T(8,128)(2,1)S(1)} %shard_map.98), channel_id=1, source_target_pairs={{4,0},{12,1},{6,2},{14,3},{0,4},{8,5},{2,6},{10,7},{5,8},{13,9},{7... | collective-permute-start | bytes 786440 | tf_op jit(solution)/shard_map/ppermute | solution.py:264
  63.3 0.0 collective-permute-done.11.refs_8_
  63.3 0.0 collective-permute-done.12.refs_9_
  63.4 0.0 collective-permute-done.9.refs_5_
  63.4 2.1 %shard_map.97 = (f32[256,1024]{1,0:T(8,128)S(1)}, bf16[512,1024]{1,0:T(8,128)(2,1)S(1)}) custom-call(bf16[256,1024]{1,0:T(8,128)(2,1)} %bitcast.4, s32[1,256]{1,0:T(1,128)} %refs_1_.3, s32[1,256]{1,0:T(1,128)} %refs_2_.3, bf16[64,1024]{1,0:T(8,128)(2,1)} %refs_3_.3, bf16[64,1024]{1,0:T(8,128)(2,1)} %refs_4_.3, ...), custom_call_target="tpu_custom_call" | custom-call | flops 268435456 | bytes 5244928 | tf_op jit(solution)/shard_map/pallas_call | solution.py:33
  65.5 8.6 %collective-permute-done.13.context = bf16[256,512]{1,0:T(8,128)(2,1)S(1)} collective-permute-done((bf16[256,512]{1,0:T(8,128)(2,1)S(1)}, bf16[256,512]{1,0:T(8,128)(2,1)S(1)}, u32[]{:S(2)}, u32[]{:S(2)}) %collective-permute-start.13) | collective-permute-done | bytes 262176 | tf_op jit(solution)/shard_map/ppermute | solution.py:264
  74.0 1.2 %shard_map.99 = bf16[256,1024]{1,0:T(8,128)(2,1)} custom-call(f32[256,1024]{1,0:T(8,128)S(1)} %get-tuple-element.24.base, bf16[256,512]{1,0:T(8,128)(2,1)S(1)} %collective-permute-done.13.context, bf16[512,1024]{1,0:T(8,128)(2,1)S(1)} %get-tuple-element.26.weight), custom_call_target="tpu_custom_call" | custom-call | flops 268435456 | bytes 2883584 | tf_op jit(solution)/shard_map/pallas_call | solution.py:33
Async XLA Ops:
  0.0 40.2 %copy-start = (bf16[1024,256]{1,0:T(8,128)(2,1)S(1)}, bf16[1024,256]{1,0:T(8,128)(2,1)}, u32[]{:S(2)}) copy-start(bf16[1024,256]{1,0:T(8,128)(2,1)} %refs_6_.1) | copy-start | bytes 1572868
  2.2 20.6 %collective-permute-start.4 = (bf16[256,1536]{1,0:T(8,128)(2,1)S(1)}, bf16[256,1536]{1,0:T(8,128)(2,1)S(1)}, u32[]{:S(2)}, u32[]{:S(2)}) collective-permute-start(bf16[256,1536]{1,0:T(8,128)(2,1)S(1)} %get-tuple-element.20.refs_4_.refs_2_.refs_1_), channel_id=1, source_target_pairs={{0,2},{1,3},{2,0},{3,1},{4,6},{5,7},{6,4},{7,5},{8,10},{9,11},{10,... | collective-permute-start | bytes 2359304 | tf_op jit(solution)/shard_map/ppermute | solution.py:267
  5.2 37.0 %collective-permute-start.5 = (bf16[256,1536]{1,0:T(8,128)(2,1)S(1)}, bf16[256,1536]{1,0:T(8,128)(2,1)S(1)}, u32[]{:S(2)}, u32[]{:S(2)}) collective-permute-start(bf16[256,1536]{1,0:T(8,128)(2,1)S(1)} %get-tuple-element.20.refs_4_.refs_2_.refs_1_), channel_id=1, source_target_pairs={{0,1},{1,0},{2,3},{3,2},{4,5},{5,4},{6,7},{7,6},{8,9},{9,8},{10,11... | collective-permute-start | bytes 2359304 | tf_op jit(solution)/shard_map/ppermute | solution.py:270
  22.8 19.5 %collective-permute-start.6 = (bf16[256,1536]{1,0:T(8,128)(2,1)S(1)}, bf16[256,1536]{1,0:T(8,128)(2,1)S(1)}, u32[]{:S(2)}, u32[]{:S(2)}) collective-permute-start(bf16[256,1536]{1,0:T(8,128)(2,1)S(1)} %collective-permute-done.4.refs_5_.refs_3_.refs_2_), channel_id=1, source_target_pairs={{0,1},{1,0},{2,3},{3,2},{4,5},{5,4},{6,7},{7,6},{8,9},{9,8},{10,11... | collective-permute-start | bytes 2359304 | tf_op jit(solution)/shard_map/ppermute | solution.py:270
  22.8 10.0 %collective-permute-start = (bf16[144,1024]{1,0:T(8,128)(2,1)S(1)}, bf16[144,1024]{1,0:T(8,128)(2,1)S(1)}, u32[]{:S(2)}, u32[]{:S(2)}) collective-permute-start(bf16[144,1024]{1,0:T(8,128)(2,1)S(1)} %get-tuple-element.18), channel_id=1, source_target_pairs={{0,4},{2,6},{4,0},{6,2},{9,13},{11,15},{13,9},{15,11},{1,8},{3,10}... | collective-permute-start | bytes 884744 | tf_op jit(solution)/shard_map/ppermute | solution.py:264
  24.6 14.9 %collective-permute-start.1 = (bf16[144,1024]{1,0:T(8,128)(2,1)S(1)}, bf16[144,1024]{1,0:T(8,128)(2,1)S(1)}, u32[]{:S(2)}, u32[]{:S(2)}) collective-permute-start(bf16[144,1024]{1,0:T(8,128)(2,1)S(1)} %get-tuple-element.19), channel_id=1, source_target_pairs={{0,4},{2,6},{4,0},{6,2},{9,13},{11,15},{13,9},{15,11},{1,8},{3,10}... | collective-permute-start | bytes 884744 | tf_op jit(solution)/shard_map/ppermute | solution.py:264
  32.8 12.3 %collective-permute-start.2 = (bf16[144,1024]{1,0:T(8,128)(2,1)S(1)}, bf16[144,1024]{1,0:T(8,128)(2,1)S(1)}, u32[]{:S(2)}, u32[]{:S(2)}) collective-permute-start(bf16[144,1024]{1,0:T(8,128)(2,1)S(1)} %collective-permute-done.refs_2_.refs_0_), channel_id=1, source_target_pairs={{1,5},{3,7},{5,1},{7,3},{8,12},{10,14},{12,8},{14,10},{17,21},{19,... | collective-permute-start | bytes 884744 | tf_op jit(solution)/shard_map/ppermute | solution.py:264
  39.5 5.6 %collective-permute-start.3 = (bf16[144,1024]{1,0:T(8,128)(2,1)S(1)}, bf16[144,1024]{1,0:T(8,128)(2,1)S(1)}, u32[]{:S(2)}, u32[]{:S(2)}) collective-permute-start(bf16[144,1024]{1,0:T(8,128)(2,1)S(1)} %collective-permute-done.1.refs_3_.refs_1_), channel_id=1, source_target_pairs={{1,5},{3,7},{5,1},{7,3},{8,12},{10,14},{12,8},{14,10},{17,21},{19,... | collective-permute-start | bytes 884744 | tf_op jit(solution)/shard_map/ppermute | solution.py:264
  40.2 13.2 %collective-permute-start.10 = (bf16[1024,256]{1,0:T(8,128)(2,1)S(1)}, bf16[1024,256]{1,0:T(8,128)(2,1)S(1)}, u32[]{:S(2)}, u32[]{:S(2)}) collective-permute-start(bf16[1024,256]{1,0:T(8,128)(2,1)S(1)} %copy-done), channel_id=1, source_target_pairs={{0,2},{1,3},{2,0},{3,1},{4,6},{5,7},{6,4},{7,5},{8,10},{9,11},{10,... | collective-permute-start | bytes 1572872 | tf_op jit(solution)/shard_map/ppermute | solution.py:267
  43.0 12.7 %collective-permute-start.7 = (bf16[272,1024]{1,0:T(8,128)(2,1)S(1)}, bf16[272,1024]{1,0:T(8,128)(2,1)S(1)}, u32[]{:S(2)}, u32[]{:S(2)}) collective-permute-start(bf16[272,1024]{1,0:T(8,128)(2,1)S(1)} %shard_map.95.refs_0_), channel_id=1, source_target_pairs={{0,1},{1,0},{2,3},{3,2},{4,5},{5,4},{6,7},{7,6},{8,9},{9,8},{10,11... | collective-permute-start | bytes 1671176 | tf_op jit(solution)/shard_map/ppermute | solution.py:270
  45.9 9.7 %collective-permute-start.8 = (bf16[272,1024]{1,0:T(8,128)(2,1)S(1)}, bf16[272,1024]{1,0:T(8,128)(2,1)S(1)}, u32[]{:S(2)}, u32[]{:S(2)}) collective-permute-start(bf16[272,1024]{1,0:T(8,128)(2,1)S(1)} %get-tuple-element.23.refs_1_), channel_id=1, source_target_pairs={{0,1},{1,0},{2,3},{3,2},{4,5},{5,4},{6,7},{7,6},{8,9},{9,8},{10,11... | collective-permute-start | bytes 1671176 | tf_op jit(solution)/shard_map/ppermute | solution.py:270
  48.1 15.3 %collective-permute-start.11 = (bf16[1024,256]{1,0:T(8,128)(2,1)S(1)}, bf16[1024,256]{1,0:T(8,128)(2,1)S(1)}, u32[]{:S(2)}, u32[]{:S(2)}) collective-permute-start(bf16[1024,256]{1,0:T(8,128)(2,1)S(1)} %copy-done), channel_id=1, source_target_pairs={{0,1},{1,0},{2,3},{3,2},{4,5},{5,4},{6,7},{7,6},{8,9},{9,8},{10,11... | collective-permute-start | bytes 1572872 | tf_op jit(solution)/shard_map/ppermute | solution.py:270
  53.4 9.9 %collective-permute-start.12 = (bf16[1024,256]{1,0:T(8,128)(2,1)S(1)}, bf16[1024,256]{1,0:T(8,128)(2,1)S(1)}, u32[]{:S(2)}, u32[]{:S(2)}) collective-permute-start(bf16[1024,256]{1,0:T(8,128)(2,1)S(1)} %collective-permute-done.10.refs_7_), channel_id=1, source_target_pairs={{0,1},{1,0},{2,3},{3,2},{4,5},{5,4},{6,7},{7,6},{8,9},{9,8},{10,11... | collective-permute-start | bytes 1572872 | tf_op jit(solution)/shard_map/ppermute | solution.py:270
  58.7 4.7 %collective-permute-start.9 = (bf16[256,512]{1,0:T(8,128)(2,1)S(1)}, bf16[256,512]{1,0:T(8,128)(2,1)S(1)}, u32[]{:S(2)}, u32[]{:S(2)}) collective-permute-start(bf16[256,512]{1,0:T(8,128)(2,1)S(1)} %shard_map.96), channel_id=1, source_target_pairs={{0,0},{8,1},{2,2},{10,3},{4,4},{12,5},{6,6},{14,7},{1,8},{9,9},{3,... | collective-permute-start | bytes 786440 | tf_op jit(solution)/shard_map/ppermute | solution.py:264
  62.4 11.6 %collective-permute-start.13 = (bf16[256,512]{1,0:T(8,128)(2,1)S(1)}, bf16[256,512]{1,0:T(8,128)(2,1)S(1)}, u32[]{:S(2)}, u32[]{:S(2)}) collective-permute-start(bf16[256,512]{1,0:T(8,128)(2,1)S(1)} %shard_map.98), channel_id=1, source_target_pairs={{4,0},{12,1},{6,2},{14,3},{0,4},{8,5},{2,6},{10,7},{5,8},{13,9},{7... | collective-permute-start | bytes 786440 | tf_op jit(solution)/shard_map/ppermute | solution.py:264

commit v4 on v3

--- a/solution.py
+++ b/solution.py
@@ -14,6 +14,7 @@
 VM = pl.BlockSpec(memory_space=pltpu.VMEM)
 PAD = 16
 CUTS = 2
+FIRST = 10
 
 
 HB = pl.BlockSpec(memory_space=pltpu.HBM)
@@ -28,13 +29,18 @@
     return lax.rem(z, half), lax.div(z, half) == core, order
 
 
-def call(kernel, outs, args, specs, flops, scratch=(), away=0):
+def cut(length):
+    first = length * FIRST // 16
+    return (0, first), (first, length)
+
+
+def call(kernel, outs, args, specs, flops, scratch=()):
     moved = sum(a.size * a.dtype.itemsize for a in (*args, *outs))
     return pl.pallas_call(
         kernel,
         out_shape=outs,
         in_specs=specs,
-        out_specs=[VM] * (len(outs) - away) + [HB] * away,
+        out_specs=[VM] * len(outs),
         scratch_shapes=scratch,
         compiler_params=pltpu.CompilerParams(vmem_limit_bytes=16 << 20),
         cost_estimate=pl.CostEstimate(flops=flops, bytes_accessed=moved, transcendentals=0),
@@ -54,17 +60,16 @@
 
 
 def embed_kernel(*refs):
-    inputs, weight, share, blocks = refs[:7], refs[7], refs[8], refs[9 : 9 + CUTS]
-    kept, refs = refs[9 + CUTS : 9 + 2 * CUTS], refs[9 + 2 * CUTS :]
-    local, sems = refs[:7], refs[7]
+    inputs, weight, share_q, share_kv, blocks = refs[:7], refs[7], refs[8], refs[9], refs[10 : 10 + CUTS]
+    local, sems = refs[10 + CUTS : 17 + CUTS], refs[17 + CUTS]
     copies = [pltpu.make_async_copy(a, b, sems.at[i]) for i, (a, b) in enumerate(zip(inputs, local))]
-    group, (place, _, _) = share.shape[1] // 3, here()
+    group, (place, _, _) = share_q.shape[1], here()
     for part in range(3):
         first = pl.multiple_of(part * (weight.shape[1] // 3) + place * group, group)
         copies.append(
             pltpu.make_async_copy(
                 weight.at[:, pl.ds(first, group)],
-                share.at[:, pl.ds(part * group, group)],
+                share_kv.at[:, pl.ds((part - 1) * group, group)] if part else share_q,
                 sems.at[7 + part],
             )
         )
@@ -79,13 +84,11 @@
     variance = jnp.mean(centered * centered, axis=-1, keepdims=True)
     normed = (centered * lax.rsqrt(variance + epsilon) * gain[...]).astype(jnp.bfloat16)
     labels = jnp.broadcast_to(segs[...].astype(jnp.float32), (PAD, length)).astype(jnp.bfloat16)
-    cut = length // CUTS
-    for i, block in enumerate(blocks):
-        block[:cut, :] = normed[i * cut : (i + 1) * cut]
-        block[cut:, :] = jnp.zeros((PAD, block.shape[1]), jnp.bfloat16)
-        block[cut:, :cut] = labels[:, i * cut : (i + 1) * cut]
-        copies.append(pltpu.make_async_copy(block, kept[i], sems.at[10 + i]))
-        copies[-1].start()
+    for block, (start, stop) in zip(blocks, cut(length)):
+        rows = stop - start
+        block[:rows, :] = normed[start:stop]
+        block[rows:, :] = jnp.zeros((PAD, block.shape[1]), jnp.bfloat16)
+        block[rows:, :length] = labels
     for copy in copies[7:]:
         copy.wait()
 
@@ -103,38 +106,28 @@
     return total.astype(jnp.bfloat16)
 
 
-def pick_kernel(*refs):
-    away, two, block, one, sems = refs[:CUTS], refs[CUTS : 2 * CUTS], refs[-CUTS - 2], refs[-CUTS - 1 : -1], refs[-1]
-    copies = [pltpu.make_async_copy(a, b, sems.at[i]) for i, (a, b) in enumerate(zip(away, one))]
-    for copy in copies:
-        copy.start()
-    for copy in copies:
-        copy.wait()
-    pick(one, two, block)
-
-
-def pick(one, two, block):
+def pick_kernel(one, two, out):
     _, own, _ = here()
-    length = block.shape[0] - PAD
-    cut = length // CUTS
-    block[length:, :] = jnp.zeros((PAD, block.shape[1]), jnp.bfloat16)
-    for i, (a, b) in enumerate(zip(one, two)):
-        part = jnp.where(own, a[...], b[...])
-        block[i * cut : (i + 1) * cut, :] = part[:cut]
-        block[length:, i * cut : (i + 1) * cut] = part[cut:, :cut]
-
-
-def keys_kernel(pieces, tile, *refs):
-    if len(refs) == 2 + pieces:
-        block, weights, kv_out = refs[0], refs[1:-1], refs[-1]
-    else:
-        weights, (block, kv_out) = refs[2 * CUTS : 2 * CUTS + pieces], refs[2 * CUTS + pieces :]
-        pick(refs[:CUTS], refs[CUTS : 2 * CUTS], block)
-    length, third = block.shape[0] - PAD, weights[0].shape[1] // 3
+    out[...] = jnp.where(own, one[...], two[...])
+
+
+def keys_kernel(pieces, ways, tile, *refs):
+    _, own, _ = here()
+    weights, (block, kv_out) = refs[-2 - pieces : -2], refs[-2:]
+    at = 0
+    for count, (start, stop) in zip(ways, cut(block.shape[0] - PAD)):
+        part = refs[at][...]
+        if count == 2:
+            part = jnp.where(own, part, refs[at + 1][...])
+        block[start:stop, :] = part[: stop - start]
+        if start == 0:
+            block[block.shape[0] - PAD :, :] = part[stop:]
+        at += count
+    length, third = block.shape[0] - PAD, weights[0].shape[1] // 2
     kv_out[length:, :] = jnp.zeros((PAD, 2 * third), jnp.bfloat16)
     kv_out[length:, :length] = block[length:, :length]
     for first in range(0, 2 * third, tile):
-        columns = slice(third + first, third + first + tile)
+        columns = slice(first, first + tile)
         kv_out[:length, first : first + tile] = matched(block, weights, columns)
 
 
@@ -286,52 +279,46 @@
     )
     kept = [pltpu.with_memory_space_constraint(a, pltpu.HBM) for a in (*inputs, qkv_weight)]
     local = [pltpu.VMEM(a.shape, a.dtype) for a in inputs]
-    share, *made = call(
+    share_q, share_kv, *block = call(
         embed_kernel,
         [
-            shape((depth, 3 * group), jnp.bfloat16),
-            *[shape((length // CUTS + PAD, model), jnp.bfloat16)] * (2 * CUTS),
+            shape((depth, group), jnp.bfloat16),
+            shape((depth, 2 * group), jnp.bfloat16),
+            *[shape((b - a + PAD, model), jnp.bfloat16) for a, b in cut(length)],
         ],
         kept,
         [HB] * 8,
         4 * length * row_table.shape[0] * model,
-        scratch=local + [pltpu.SemaphoreType.DMA((10 + CUTS,))],
-        away=CUTS,
-    )
-    block, parked = made[:CUTS], made[CUTS:]
-    weights = gather(share)
+        scratch=local + [pltpu.SemaphoreType.DMA((10,))],
+    )
+    kv_weights, q_weights = gather(share_kv), gather(share_q)
     out_weights = gather(out_weight)
     first = send_cuts(block, moves(around(1 % half, True), spread(0)))
     whole = shape((length + PAD, model), jnp.bfloat16)
-    (picked,) = call(
-        pick_kernel,
-        [whole],
-        (*parked, *first),
-        [HB] * CUTS + [VM] * CUTS,
-        0,
-        scratch=[pltpu.VMEM(a.shape, a.dtype) for a in block] + [pltpu.SemaphoreType.DMA((CUTS,))],
-    )
-    blocks = [(picked,), (*first, *send_cuts(first, around(1, False)))]
+    picked = call(pick_kernel, [shape(block[0].shape, jnp.bfloat16)], (block[0], first[0]), [VM] * 2, 0)
+    relayed = send_cuts(first, around(1, False))
+    blocks = [[picked, *zip(block[1:], first[1:])], list(zip(first, relayed))]
     for j in range(2, half):
         held = [jnp.where(own, a, b) for a, b in zip(block, first)]
         held = send_cuts(held, around(j, True) + around(j, False))
-        blocks.append((*held, *held))
+        blocks.append([[h] for h in held])
     tile = min(group, 256)
     slots, keys = [], []
-    for j, ways in enumerate(blocks):
-        *slot, kv = call(
-            functools.partial(keys_kernel, lanes, tile),
-            [whole] * (j > 0) + [shape((length + PAD, 2 * group), jnp.bfloat16)],
-            (*ways, *weights),
-            [VM] * (len(ways) + lanes),
+    for ways in blocks:
+        ways, parts = tuple(len(w) for w in ways), [p for w in ways for p in w]
+        slot, kv = call(
+            functools.partial(keys_kernel, lanes, ways, tile),
+            [whole, shape((length + PAD, 2 * group), jnp.bfloat16)],
+            (*parts, *kv_weights),
+            [VM] * (len(parts) + lanes),
             4 * length * model * group,
         )
-        slots += slot or [picked]
+        slots.append(slot)
         keys.append(kv)
     queries = call(
         functools.partial(queries_kernel, half, lanes, tile, 1.0 / head**0.5),
         [shape((length, group), jnp.bfloat16)] * half,
-        (*slots, *weights),
+        (*slots, *q_weights),
         [VM] * (half + lanes),
         2 * half * length * model * group,
     )

time: 75.5 us -> 67.7 us (0.90)
  waiting for transfers between devices: 45.5 us -> 32.4 us
  starting transfers between devices: 15.6 us -> 21.3 us
    ppermute x6, waiting for transfers between devices: 22.6 us -> 15.3 us  [send(): return lax.ppermute(value, ('ctx', 'fsdp'), pairs)]
    ppermute x2 -> x3, waiting for transfers between devices: 22.8 us -> 16.5 us  [along(): lax.ppermute(value, 'fsdp', [(i, (i + 2 * by) % lanes) for i in range(lan...]
    ppermute x6 -> x8, starting transfers between devices: 5.85 us -> 9.86 us  [partner(): return lax.ppermute(value, 'fsdp', [(i, i ^ 1) for i in range(lanes)])]
    ppermute x6, starting transfers between devices: 4.96 us -> 6.28 us  [send(): return lax.ppermute(value, ('ctx', 'fsdp'), pairs)]
    ppermute x2 -> x3, starting transfers between devices: 4.83 us -> 5.18 us  [along(): lax.ppermute(value, 'fsdp', [(i, (i + 2 * by) % lanes) for i in range(lan...]
  transfers between devices with their start and end apart: 14 -> 17, of which waited for: 5 -> 5; matrix products, arithmetic and copies ran while one was open for 0% -> 0% of each run, Pallas kernels for 14% -> 15%
where the time goes in v4:
time: 67.7 us; the launch traced here: 67.6 us
  waiting for transfers between devices  32.4 us (48%)
  starting transfers between devices  21.3 us (31%)
  Pallas kernels  13.7 us (20%)
    ppermute x3, waiting for transfers between devices, along(): lax.ppermute(value, 'fsdp', [(i, (i + 2 * by) % lanes) for i in range(lan...  16.5 us
    ppermute x6, waiting for transfers between devices, send(): return lax.ppermute(value, ('ctx', 'fsdp'), pairs)  15.3 us
    pallas_call x9, Pallas kernels, call(): pl.pallas_call(kernel, out_shape=outs, in_specs=specs, out_specs=[VM] * l...  13.7 us
    ppermute x8, starting transfers between devices, partner(): return lax.ppermute(value, 'fsdp', [(i, i ^ 1) for i in range(lanes)])  9.86 us
    ppermute x6, starting transfers between devices, send(): return lax.ppermute(value, ('ctx', 'fsdp'), pairs)  6.28 us
    ppermute x3, starting transfers between devices, along(): lax.ppermute(value, 'fsdp', [(i, (i + 2 * by) % lanes) for i in range(lan...  5.18 us
  transfers between devices with their start and end apart: 17, of which 5 were waited for; matrix products, arithmetic and copies ran while one was open for 0% of the time, Pallas kernels for 15%

profile of v4, /device:TPU:0, one launch (start us, length us, event | category | flops | bytes accessed | tf_op | source)
XLA Modules:
  0.0 67.6 jit_solution(9473497305845886218)
XLA Ops:
  0.0 0.0 copy-start
  0.0 2.0 %shard_map.91 = (bf16[256,512]{1,0:T(8,128)(2,1)S(1)}, bf16[256,1024]{1,0:T(8,128)(2,1)S(1)}, bf16[176,1024]{1,0:T(8,128)(2,1)S(1)}, bf16[112,1024]{1,0:T(8,128)(2,1)S(1)}) custom-call(bf16[256,1024]{1,0:T(8,128)(2,1)} %bitcast.3, s32[1,256]{1,0:T(1,128)} %refs_1_.3, s32[1,256]{1,0:T(1,128)} %refs_2_.3, bf16[64,1024]{1,0:T(8,128)(2,1)} %refs_3_.3, ...), custom_call_target="tpu_custom_call" | custom-call | flops 67108864 | bytes 3742720 | tf_op jit(solution)/shard_map/pallas_call | solution.py:39
  2.1 3.0 %collective-permute-start.2 = (bf16[256,1024]{1,0:T(8,128)(2,1)S(1)}, bf16[256,1024]{1,0:T(8,128)(2,1)S(1)}, u32[]{:S(2)}, u32[]{:S(2)}) collective-permute-start(bf16[256,1024]{1,0:T(8,128)(2,1)S(1)} %get-tuple-element.19.refs_3_.refs_4_), channel_id=1, source_target_pairs={{0,2},{1,3},{2,0},{3,1},{4,6},{5,7},{6,4},{7,5},{8,10},{9,11},{10,... | collective-permute-start | bytes 1572872 | tf_op jit(solution)/shard_map/ppermute | solution.py:260
  5.1 1.6 %collective-permute-start = (bf16[176,1024]{1,0:T(8,128)(2,1)S(1)}, bf16[176,1024]{1,0:T(8,128)(2,1)S(1)}, u32[]{:S(2)}, u32[]{:S(2)}) collective-permute-start(bf16[176,1024]{1,0:T(8,128)(2,1)S(1)} %get-tuple-element.17.one), channel_id=1, source_target_pairs={{0,4},{2,6},{4,0},{6,2},{9,13},{11,15},{13,9},{15,11},{1,8},{3,10}... | collective-permute-start | bytes 1081352 | tf_op jit(solution)/shard_map/ppermute | solution.py:257
  6.7 1.1 %collective-permute-start.3 = (bf16[256,1024]{1,0:T(8,128)(2,1)S(1)}, bf16[256,1024]{1,0:T(8,128)(2,1)S(1)}, u32[]{:S(2)}, u32[]{:S(2)}) collective-permute-start(bf16[256,1024]{1,0:T(8,128)(2,1)S(1)} %get-tuple-element.19.refs_3_.refs_4_), channel_id=1, source_target_pairs={{0,1},{1,0},{2,3},{3,2},{4,5},{5,4},{6,7},{7,6},{8,9},{9,8},{10,11... | collective-permute-start | bytes 1572872 | tf_op jit(solution)/shard_map/ppermute | solution.py:263
  7.8 9.2 %collective-permute-done.2.refs_4_.refs_5_ = bf16[256,1024]{1,0:T(8,128)(2,1)S(1)} collective-permute-done((bf16[256,1024]{1,0:T(8,128)(2,1)S(1)}, bf16[256,1024]{1,0:T(8,128)(2,1)S(1)}, u32[]{:S(2)}, u32[]{:S(2)}) %collective-permute-start.2) | collective-permute-done | bytes 524320 | tf_op jit(solution)/shard_map/ppermute | solution.py:260
  17.0 0.0 collective-permute-start.4
  17.0 1.8 %collective-permute-start.1 = (bf16[112,1024]{1,0:T(8,128)(2,1)S(1)}, bf16[112,1024]{1,0:T(8,128)(2,1)S(1)}, u32[]{:S(2)}, u32[]{:S(2)}) collective-permute-start(bf16[112,1024]{1,0:T(8,128)(2,1)S(1)} %get-tuple-element.18.refs_1_), channel_id=1, source_target_pairs={{0,4},{2,6},{4,0},{6,2},{9,13},{11,15},{13,9},{15,11},{1,8},{3,10}... | collective-permute-start | bytes 688136 | tf_op jit(solution)/shard_map/ppermute | solution.py:257
  18.8 0.0 collective-permute-done.two.refs_0_
  18.8 0.7 collective-permute-start.5
  19.5 6.6 %collective-permute-done.1.refs_2_ = bf16[112,1024]{1,0:T(8,128)(2,1)S(1)} collective-permute-done((bf16[112,1024]{1,0:T(8,128)(2,1)S(1)}, bf16[112,1024]{1,0:T(8,128)(2,1)S(1)}, u32[]{:S(2)}, u32[]{:S(2)}) %collective-permute-start.1) | collective-permute-done | bytes 229408 | tf_op jit(solution)/shard_map/ppermute | solution.py:257
  26.1 0.7 collective-permute-start.6
  26.8 1.8 %collective-permute-start.7 = (bf16[256,512]{1,0:T(8,128)(2,1)S(1)}, bf16[256,512]{1,0:T(8,128)(2,1)S(1)}, u32[]{:S(2)}, u32[]{:S(2)}) collective-permute-start(bf16[256,512]{1,0:T(8,128)(2,1)S(1)} %get-tuple-element.22.refs_2_), channel_id=1, source_target_pairs={{0,2},{1,3},{2,0},{3,1},{4,6},{5,7},{6,4},{7,5},{8,10},{9,11},{10,... | collective-permute-start | bytes 786440 | tf_op jit(solution)/shard_map/ppermute | solution.py:260
  28.6 0.0 collective-permute-done.6.refs_3_
  28.6 0.0 copy-done
  28.6 0.4 collective-permute-start.13
  29.0 0.0 collective-permute-done.3.refs_5_.refs_6_
  29.0 0.0 collective-permute-done.5.refs_1_
  29.0 0.0 collective-permute-done.4.refs_6_.refs_7_
  29.0 0.7 %shard_map.94 = (bf16[272,1024]{1,0:T(8,128)(2,1)S(1)}, bf16[272,1024]{1,0:T(8,128)(2,1)S(1)}) custom-call(bf16[176,1024]{1,0:T(8,128)(2,1)S(1)} %collective-permute-done.two.refs_0_, bf16[176,1024]{1,0:T(8,128)(2,1)S(1)} %collective-permute-done.5.refs_1_, bf16[112,1024]{1,0:T(8,128)(2,1)S(1)} %collective-permute-done.1.refs_2_, ...), custom_call_target="tpu_custom_call" | custom-call | flops 536870912 | bytes 4390912 | tf_op jit(solution)/shard_map/pallas_call | solution.py:39
  29.7 5.3 %collective-permute-start.11 = (bf16[272,1024]{1,0:T(8,128)(2,1)S(1)}, bf16[272,1024]{1,0:T(8,128)(2,1)S(1)}, u32[]{:S(2)}, u32[]{:S(2)}) collective-permute-start(bf16[272,1024]{1,0:T(8,128)(2,1)S(1)} %get-tuple-element.25.refs_1_), channel_id=1, source_target_pairs={{0,1},{1,0},{2,3},{3,2},{4,5},{5,4},{6,7},{7,6},{8,9},{9,8},{10,11... | collective-permute-start | bytes 1671176 | tf_op jit(solution)/shard_map/ppermute | solution.py:263
  35.0 0.8 %shard_map.93 = (bf16[272,1024]{1,0:T(8,128)(2,1)S(1)}, bf16[272,1024]{1,0:T(8,128)(2,1)S(1)}) custom-call(bf16[176,1024]{1,0:T(8,128)(2,1)S(1)} %shard_map.92.refs_0_, bf16[112,1024]{1,0:T(8,128)(2,1)S(1)} %get-tuple-element.18.refs_1_, bf16[112,1024]{1,0:T(8,128)(2,1)S(1)} %collective-permute-done.1.refs_2_, ...), custom_call_target="tpu_custom_call" | custom-call | flops 536870912 | bytes 4030464 | tf_op jit(solution)/shard_map/pallas_call | solution.py:39
  35.8 0.1 collective-permute-start.10
  35.9 0.5 collective-permute-start.8
  36.4 0.0 collective-permute-done.7.refs_3_
  36.4 1.3 %collective-permute-start.9 = (bf16[256,512]{1,0:T(8,128)(2,1)S(1)}, bf16[256,512]{1,0:T(8,128)(2,1)S(1)}, u32[]{:S(2)}, u32[]{:S(2)}) collective-permute-start(bf16[256,512]{1,0:T(8,128)(2,1)S(1)} %collective-permute-done.7.refs_3_), channel_id=1, source_target_pairs={{0,1},{1,0},{2,3},{3,2},{4,5},{5,4},{6,7},{7,6},{8,9},{9,8},{10,11... | collective-permute-start | bytes 786440 | tf_op jit(solution)/shard_map/ppermute | solution.py:263
  37.7 0.5 collective-permute-done.8.refs_4_
  38.2 0.1 collective-permute-start.14
  38.3 7.3 %collective-permute-done.13.refs_7_ = bf16[1024,256]{1,0:T(8,128)(2,1)S(1)} collective-permute-done((bf16[1024,256]{1,0:T(8,128)(2,1)S(1)}, bf16[1024,256]{1,0:T(8,128)(2,1)S(1)}, u32[]{:S(2)}, u32[]{:S(2)}) %collective-permute-start.13) | collective-permute-done | bytes 524320 | tf_op jit(solution)/shard_map/ppermute | solution.py:260
  45.7 1.4 %collective-permute-start.15 = (bf16[1024,256]{1,0:T(8,128)(2,1)S(1)}, bf16[1024,256]{1,0:T(8,128)(2,1)S(1)}, u32[]{:S(2)}, u32[]{:S(2)}) collective-permute-start(bf16[1024,256]{1,0:T(8,128)(2,1)S(1)} %collective-permute-done.13.refs_7_), channel_id=1, source_target_pairs={{0,1},{1,0},{2,3},{3,2},{4,5},{5,4},{6,7},{7,6},{8,9},{9,8},{10,11... | collective-permute-start | bytes 1572872 | tf_op jit(solution)/shard_map/ppermute | solution.py:263
  47.1 0.0 collective-permute-done.9.refs_5_
  47.1 0.7 %shard_map.95 = (bf16[256,512]{1,0:T(8,128)(2,1)S(1)}, bf16[256,512]{1,0:T(8,128)(2,1)S(1)}) custom-call(bf16[272,1024]{1,0:T(8,128)(2,1)S(1)} %get-tuple-element.20.refs_0_, bf16[272,1024]{1,0:T(8,128)(2,1)S(1)} %get-tuple-element.21.refs_1_, bf16[256,512]{1,0:T(8,128)(2,1)S(1)} %get-tuple-element.22.refs_2_, ...), custom_call_target="tpu_custom_call" | custom-call | flops 536870912 | bytes 2686976 | tf_op jit(solution)/shard_map/pallas_call | solution.py:39
  47.8 0.0 collective-permute-done.11.refs_3_
  47.8 0.0 collective-permute-done.10.refs_2_
  47.8 3.0 %shard_map.96 = bf16[256,512]{1,0:T(8,128)(2,1)S(1)} custom-call(bf16[256,512]{1,0:T(8,128)(2,1)S(1)} %get-tuple-element.23.q, bf16[272,1024]{1,0:T(8,128)(2,1)S(1)} %get-tuple-element.24.refs_0_, bf16[272,1024]{1,0:T(8,128)(2,1)S(1)} %get-tuple-element.25.refs_1_, bf16[272,1024]{1,0:T(8,128)(2,1)S(1)} %collective-permute-done.10.refs_2_, ...), custom_call_target="tpu_custom_call" | custom-call | flops 1073741824 | bytes 2752512 | tf_op jit(solution)/shard_map/pallas_call | solution.py:39
  50.9 0.7 %collective-permute-start.12 = (bf16[256,512]{1,0:T(8,128)(2,1)S(1)}, bf16[256,512]{1,0:T(8,128)(2,1)S(1)}, u32[]{:S(2)}, u32[]{:S(2)}) collective-permute-start(bf16[256,512]{1,0:T(8,128)(2,1)S(1)} %shard_map.96), channel_id=1, source_target_pairs={{0,0},{8,1},{2,2},{10,3},{4,4},{12,5},{6,6},{14,7},{1,8},{9,9},{3,... | collective-permute-start | bytes 786440 | tf_op jit(solution)/shard_map/ppermute | solution.py:257
  51.5 3.0 %shard_map.98 = bf16[256,512]{1,0:T(8,128)(2,1)S(1)} custom-call(bf16[256,512]{1,0:T(8,128)(2,1)S(1)} %get-tuple-element.27.q, bf16[272,1024]{1,0:T(8,128)(2,1)S(1)} %get-tuple-element.24.refs_0_, bf16[272,1024]{1,0:T(8,128)(2,1)S(1)} %get-tuple-element.25.refs_1_, bf16[272,1024]{1,0:T(8,128)(2,1)S(1)} %collective-permute-done.10.refs_2_, ...), custom_call_target="tpu_custom_call" | custom-call | flops 1073741824 | bytes 2752512 | tf_op jit(solution)/shard_map/pallas_call | solution.py:39
  54.6 0.9 %collective-permute-start.16 = (bf16[256,512]{1,0:T(8,128)(2,1)S(1)}, bf16[256,512]{1,0:T(8,128)(2,1)S(1)}, u32[]{:S(2)}, u32[]{:S(2)}) collective-permute-start(bf16[256,512]{1,0:T(8,128)(2,1)S(1)} %shard_map.98), channel_id=1, source_target_pairs={{4,0},{12,1},{6,2},{14,3},{0,4},{8,5},{2,6},{10,7},{5,8},{13,9},{7... | collective-permute-start | bytes 786440 | tf_op jit(solution)/shard_map/ppermute | solution.py:257
  55.5 0.0 collective-permute-done.14.refs_8_
  55.5 0.0 collective-permute-done.15.refs_9_
  55.5 0.0 collective-permute-done.12.refs_5_
  55.5 2.1 %shard_map.97 = (f32[256,1024]{1,0:T(8,128)S(1)}, bf16[512,1024]{1,0:T(8,128)(2,1)S(1)}) custom-call(bf16[256,1024]{1,0:T(8,128)(2,1)} %bitcast.4, s32[1,256]{1,0:T(1,128)} %refs_1_.3, s32[1,256]{1,0:T(1,128)} %refs_2_.3, bf16[64,1024]{1,0:T(8,128)(2,1)} %refs_3_.3, bf16[64,1024]{1,0:T(8,128)(2,1)} %refs_4_.3, ...), custom_call_target="tpu_custom_call" | custom-call | flops 268435456 | bytes 5244928 | tf_op jit(solution)/shard_map/pallas_call | solution.py:39
  57.6 8.8 %collective-permute-done.16.context = bf16[256,512]{1,0:T(8,128)(2,1)S(1)} collective-permute-done((bf16[256,512]{1,0:T(8,128)(2,1)S(1)}, bf16[256,512]{1,0:T(8,128)(2,1)S(1)}, u32[]{:S(2)}, u32[]{:S(2)}) %collective-permute-start.16) | collective-permute-done | bytes 262176 | tf_op jit(solution)/shard_map/ppermute | solution.py:257
  66.3 1.2 %shard_map.99 = bf16[256,1024]{1,0:T(8,128)(2,1)} custom-call(f32[256,1024]{1,0:T(8,128)S(1)} %get-tuple-element.26.base, bf16[256,512]{1,0:T(8,128)(2,1)S(1)} %collective-permute-done.16.context, bf16[512,1024]{1,0:T(8,128)(2,1)S(1)} %get-tuple-element.28.weight), custom_call_target="tpu_custom_call" | custom-call | flops 268435456 | bytes 2883584 | tf_op jit(solution)/shard_map/pallas_call | solution.py:39
  (1 shorter events, 0.0 us)
Async XLA Ops:
  0.0 28.6 %copy-start = (bf16[1024,256]{1,0:T(8,128)(2,1)S(1)}, bf16[1024,256]{1,0:T(8,128)(2,1)}, u32[]{:S(2)}) copy-start(bf16[1024,256]{1,0:T(8,128)(2,1)} %refs_6_.1) | copy-start | bytes 1572868
  2.1 15.0 %collective-permute-start.2 = (bf16[256,1024]{1,0:T(8,128)(2,1)S(1)}, bf16[256,1024]{1,0:T(8,128)(2,1)S(1)}, u32[]{:S(2)}, u32[]{:S(2)}) collective-permute-start(bf16[256,1024]{1,0:T(8,128)(2,1)S(1)} %get-tuple-element.19.refs_3_.refs_4_), channel_id=1, source_target_pairs={{0,2},{1,3},{2,0},{3,1},{4,6},{5,7},{6,4},{7,5},{8,10},{9,11},{10,... | collective-permute-start | bytes 1572872 | tf_op jit(solution)/shard_map/ppermute | solution.py:260
  5.1 13.8 %collective-permute-start = (bf16[176,1024]{1,0:T(8,128)(2,1)S(1)}, bf16[176,1024]{1,0:T(8,128)(2,1)S(1)}, u32[]{:S(2)}, u32[]{:S(2)}) collective-permute-start(bf16[176,1024]{1,0:T(8,128)(2,1)S(1)} %get-tuple-element.17.one), channel_id=1, source_target_pairs={{0,4},{2,6},{4,0},{6,2},{9,13},{11,15},{13,9},{15,11},{1,8},{3,10}... | collective-permute-start | bytes 1081352 | tf_op jit(solution)/shard_map/ppermute | solution.py:257
  6.7 22.3 %collective-permute-start.3 = (bf16[256,1024]{1,0:T(8,128)(2,1)S(1)}, bf16[256,1024]{1,0:T(8,128)(2,1)S(1)}, u32[]{:S(2)}, u32[]{:S(2)}) collective-permute-start(bf16[256,1024]{1,0:T(8,128)(2,1)S(1)} %get-tuple-element.19.refs_3_.refs_4_), channel_id=1, source_target_pairs={{0,1},{1,0},{2,3},{3,2},{4,5},{5,4},{6,7},{7,6},{8,9},{9,8},{10,11... | collective-permute-start | bytes 1572872 | tf_op jit(solution)/shard_map/ppermute | solution.py:263
  17.0 12.0 %collective-permute-start.4 = (bf16[256,1024]{1,0:T(8,128)(2,1)S(1)}, bf16[256,1024]{1,0:T(8,128)(2,1)S(1)}, u32[]{:S(2)}, u32[]{:S(2)}) collective-permute-start(bf16[256,1024]{1,0:T(8,128)(2,1)S(1)} %collective-permute-done.2.refs_4_.refs_5_), channel_id=1, source_target_pairs={{0,1},{1,0},{2,3},{3,2},{4,5},{5,4},{6,7},{7,6},{8,9},{9,8},{10,11... | collective-permute-start | bytes 1572872 | tf_op jit(solution)/shard_map/ppermute | solution.py:263
  17.0 9.1 %collective-permute-start.1 = (bf16[112,1024]{1,0:T(8,128)(2,1)S(1)}, bf16[112,1024]{1,0:T(8,128)(2,1)S(1)}, u32[]{:S(2)}, u32[]{:S(2)}) collective-permute-start(bf16[112,1024]{1,0:T(8,128)(2,1)S(1)} %get-tuple-element.18.refs_1_), channel_id=1, source_target_pairs={{0,4},{2,6},{4,0},{6,2},{9,13},{11,15},{13,9},{15,11},{1,8},{3,10}... | collective-permute-start | bytes 688136 | tf_op jit(solution)/shard_map/ppermute | solution.py:257
  18.8 10.2 %collective-permute-start.5 = (bf16[176,1024]{1,0:T(8,128)(2,1)S(1)}, bf16[176,1024]{1,0:T(8,128)(2,1)S(1)}, u32[]{:S(2)}, u32[]{:S(2)}) collective-permute-start(bf16[176,1024]{1,0:T(8,128)(2,1)S(1)} %collective-permute-done.two.refs_0_), channel_id=1, source_target_pairs={{1,5},{3,7},{5,1},{7,3},{8,12},{10,14},{12,8},{14,10},{17,21},{19,... | collective-permute-start | bytes 1081352 | tf_op jit(solution)/shard_map/ppermute | solution.py:257
  26.1 2.5 %collective-permute-start.6 = (bf16[112,1024]{1,0:T(8,128)(2,1)S(1)}, bf16[112,1024]{1,0:T(8,128)(2,1)S(1)}, u32[]{:S(2)}, u32[]{:S(2)}) collective-permute-start(bf16[112,1024]{1,0:T(8,128)(2,1)S(1)} %collective-permute-done.1.refs_2_), channel_id=1, source_target_pairs={{1,5},{3,7},{5,1},{7,3},{8,12},{10,14},{12,8},{14,10},{17,21},{19,... | collective-permute-start | bytes 688136 | tf_op jit(solution)/shard_map/ppermute | solution.py:257
  26.8 9.6 %collective-permute-start.7 = (bf16[256,512]{1,0:T(8,128)(2,1)S(1)}, bf16[256,512]{1,0:T(8,128)(2,1)S(1)}, u32[]{:S(2)}, u32[]{:S(2)}) collective-permute-start(bf16[256,512]{1,0:T(8,128)(2,1)S(1)} %get-tuple-element.22.refs_2_), channel_id=1, source_target_pairs={{0,2},{1,3},{2,0},{3,1},{4,6},{5,7},{6,4},{7,5},{8,10},{9,11},{10,... | collective-permute-start | bytes 786440 | tf_op jit(solution)/shard_map/ppermute | solution.py:260
  28.6 17.0 %collective-permute-start.13 = (bf16[1024,256]{1,0:T(8,128)(2,1)S(1)}, bf16[1024,256]{1,0:T(8,128)(2,1)S(1)}, u32[]{:S(2)}, u32[]{:S(2)}) collective-permute-start(bf16[1024,256]{1,0:T(8,128)(2,1)S(1)} %copy-done), channel_id=1, source_target_pairs={{0,2},{1,3},{2,0},{3,1},{4,6},{5,7},{6,4},{7,5},{8,10},{9,11},{10,... | collective-permute-start | bytes 1572872 | tf_op jit(solution)/shard_map/ppermute | solution.py:260
  29.7 18.0 %collective-permute-start.11 = (bf16[272,1024]{1,0:T(8,128)(2,1)S(1)}, bf16[272,1024]{1,0:T(8,128)(2,1)S(1)}, u32[]{:S(2)}, u32[]{:S(2)}) collective-permute-start(bf16[272,1024]{1,0:T(8,128)(2,1)S(1)} %get-tuple-element.25.refs_1_), channel_id=1, source_target_pairs={{0,1},{1,0},{2,3},{3,2},{4,5},{5,4},{6,7},{7,6},{8,9},{9,8},{10,11... | collective-permute-start | bytes 1671176 | tf_op jit(solution)/shard_map/ppermute | solution.py:263
  35.8 12.0 %collective-permute-start.10 = (bf16[272,1024]{1,0:T(8,128)(2,1)S(1)}, bf16[272,1024]{1,0:T(8,128)(2,1)S(1)}, u32[]{:S(2)}, u32[]{:S(2)}) collective-permute-start(bf16[272,1024]{1,0:T(8,128)(2,1)S(1)} %get-tuple-element.24.refs_0_), channel_id=1, source_target_pairs={{0,1},{1,0},{2,3},{3,2},{4,5},{5,4},{6,7},{7,6},{8,9},{9,8},{10,11... | collective-permute-start | bytes 1671176 | tf_op jit(solution)/shard_map/ppermute | solution.py:263
  35.9 2.3 %collective-permute-start.8 = (bf16[256,512]{1,0:T(8,128)(2,1)S(1)}, bf16[256,512]{1,0:T(8,128)(2,1)S(1)}, u32[]{:S(2)}, u32[]{:S(2)}) collective-permute-start(bf16[256,512]{1,0:T(8,128)(2,1)S(1)} %get-tuple-element.22.refs_2_), channel_id=1, source_target_pairs={{0,1},{1,0},{2,3},{3,2},{4,5},{5,4},{6,7},{7,6},{8,9},{9,8},{10,11... | collective-permute-start | bytes 786440 | tf_op jit(solution)/shard_map/ppermute | solution.py:263
  36.4 10.7 %collective-permute-start.9 = (bf16[256,512]{1,0:T(8,128)(2,1)S(1)}, bf16[256,512]{1,0:T(8,128)(2,1)S(1)}, u32[]{:S(2)}, u32[]{:S(2)}) collective-permute-start(bf16[256,512]{1,0:T(8,128)(2,1)S(1)} %collective-permute-done.7.refs_3_), channel_id=1, source_target_pairs={{0,1},{1,0},{2,3},{3,2},{4,5},{5,4},{6,7},{7,6},{8,9},{9,8},{10,11... | collective-permute-start | bytes 786440 | tf_op jit(solution)/shard_map/ppermute | solution.py:263
  38.2 17.3 %collective-permute-start.14 = (bf16[1024,256]{1,0:T(8,128)(2,1)S(1)}, bf16[1024,256]{1,0:T(8,128)(2,1)S(1)}, u32[]{:S(2)}, u32[]{:S(2)}) collective-permute-start(bf16[1024,256]{1,0:T(8,128)(2,1)S(1)} %copy-done), channel_id=1, source_target_pairs={{0,1},{1,0},{2,3},{3,2},{4,5},{5,4},{6,7},{7,6},{8,9},{9,8},{10,11... | collective-permute-start | bytes 1572872 | tf_op jit(solution)/shard_map/ppermute | solution.py:263
  45.7 9.8 %collective-permute-start.15 = (bf16[1024,256]{1,0:T(8,128)(2,1)S(1)}, bf16[1024,256]{1,0:T(8,128)(2,1)S(1)}, u32[]{:S(2)}, u32[]{:S(2)}) collective-permute-start(bf16[1024,256]{1,0:T(8,128)(2,1)S(1)} %collective-permute-done.13.refs_7_), channel_id=1, source_target_pairs={{0,1},{1,0},{2,3},{3,2},{4,5},{5,4},{6,7},{7,6},{8,9},{9,8},{10,11... | collective-permute-start | bytes 1572872 | tf_op jit(solution)/shard_map/ppermute | solution.py:263
  50.9 4.6 %collective-permute-start.12 = (bf16[256,512]{1,0:T(8,128)(2,1)S(1)}, bf16[256,512]{1,0:T(8,128)(2,1)S(1)}, u32[]{:S(2)}, u32[]{:S(2)}) collective-permute-start(bf16[256,512]{1,0:T(8,128)(2,1)S(1)} %shard_map.96), channel_id=1, source_target_pairs={{0,0},{8,1},{2,2},{10,3},{4,4},{12,5},{6,6},{14,7},{1,8},{9,9},{3,... | collective-permute-start | bytes 786440 | tf_op jit(solution)/shard_map/ppermute | solution.py:257
  54.6 11.7 %collective-permute-start.16 = (bf16[256,512]{1,0:T(8,128)(2,1)S(1)}, bf16[256,512]{1,0:T(8,128)(2,1)S(1)}, u32[]{:S(2)}, u32[]{:S(2)}) collective-permute-start(bf16[256,512]{1,0:T(8,128)(2,1)S(1)} %shard_map.98), channel_id=1, source_target_pairs={{4,0},{12,1},{6,2},{14,3},{0,4},{8,5},{2,6},{10,7},{5,8},{13,9},{7... | collective-permute-start | bytes 786440 | tf_op jit(solution)/shard_map/ppermute | solution.py:257

commit v5 on v4

--- a/solution.py
+++ b/solution.py
@@ -139,28 +139,36 @@
             out[:, columns] = matched(block, weights, columns) * jnp.bfloat16(scale)
 
 
-def attend_kernel(slots, slot, head, q, *refs):
-    keys, (out, hot, gate) = refs[: 2 * slots], refs[2 * slots :]
+def attend_kernel(count, head, resume, finish, q, owner, *refs):
+    keys, refs = refs[:count], refs[count:]
+    before, refs = (refs[:3], refs[3:]) if resume else (None, refs)
+    outs, (hot, gate) = refs[:-2], refs[-2:]
     length, third = q.shape
     level = lax.broadcasted_iota(jnp.int32, (128, length), 0).astype(jnp.float32)
+
+    def match(ref):
+        return ref[length : length + 1, :length].astype(jnp.float32) == level
+
+    hot[...] = jnp.where(match(owner), 1.0, 0.0).T.astype(jnp.bfloat16)
     for j, ref in enumerate(keys):
-        match = ref[length : length + 1, :length].astype(jnp.float32) == level
         gate[pl.ds(j * length, length), :] = (
-            jnp.where(match, 0.0, floor_score).T.astype(jnp.bfloat16)
+            jnp.where(match(ref), 0.0, floor_score).T.astype(jnp.bfloat16)
         )
-        if j == slot:
-            hot[...] = jnp.where(match, 1.0, 0.0).T.astype(jnp.bfloat16)
-    lane = lax.broadcasted_iota(jnp.int32, (length, 2 * head), 1)
+    span = 2 * head
+    lane = lax.broadcasted_iota(jnp.int32, (length, span), 1)
     nt = (((1,), (1,)), ((), ()))
-    ones = jnp.ones((length, 2 * head), jnp.bfloat16)
+    ones = jnp.ones((length, span), jnp.bfloat16)
 
     def pair(index, carry):
-        lanes = pl.ds(pl.multiple_of(index * 2 * head, 2 * head), 2 * head)
-        values = pl.ds(pl.multiple_of(third + index * 2 * head, 2 * head), 2 * head)
+        lanes = pl.ds(pl.multiple_of(index * span, span), span)
+        values = pl.ds(pl.multiple_of(third + index * span, span), span)
         both = q[:, lanes]
-        mixed = []
-        for low in (True, False):
-            mask = (lane < head) if low else (lane >= head)
+        if resume:
+            held = [ref[:, lanes] for ref in before[:2]]
+        results = []
+        for which, low in enumerate((0, head)):
+            own = pl.ds(pl.multiple_of((2 * index + which) * span, span), span)
+            mask = (lane >= low) & (lane < low + head)
             one = jnp.concatenate([jnp.where(mask, both, jnp.zeros_like(both)), hot[...]], axis=1)
             scores = [
                 lax.dot_general(
@@ -174,19 +182,33 @@
             highest = functools.reduce(
                 jnp.maximum, [jnp.max(s, axis=-1, keepdims=True) for s in scores]
             )
+            highest = jnp.broadcast_to(highest, (length, span))
+            if resume:
+                earlier = before[2][:, own]
+                highest = jnp.maximum(highest, earlier)
+            wide = jnp.concatenate([highest] * (length // span), axis=1)
             product = sum(
                 jnp.dot(
-                    jnp.exp(s - highest).astype(jnp.bfloat16),
+                    jnp.exp(s - wide).astype(jnp.bfloat16),
                     jnp.concatenate([ref[:length, values], ones], axis=1),
                     preferred_element_type=jnp.float32,
                 )
                 for s, ref in zip(scores, keys)
             )
-            mixed.append(product[:, : 2 * head] / product[:, 2 * head :])
-        out[:, lanes] = jnp.where(lane < head, mixed[0], mixed[1]).astype(jnp.bfloat16)
+            mixed, total = product[:, :span], product[:, span:]
+            if resume:
+                factor = jnp.exp(earlier - highest)
+                mixed, total = mixed + held[0] * factor, total + held[1] * factor
+            if finish:
+                results.append((mixed / total,))
+            else:
+                results.append((mixed, total))
+                outs[2][:, own] = highest
+        for out, one, two in zip(outs, *results):
+            out[:, lanes] = jnp.where(lane < head, one, two).astype(out.dtype)
         return carry
 
-    lax.fori_loop(0, third // (2 * head), pair, 0, unroll=True)
+    lax.fori_loop(0, third // span, pair, 0, unroll=True)
 
 
 def first_kernel(slots, pieces, *refs):
@@ -323,20 +345,29 @@
         2 * half * length * model * group,
     )
     keys += [partner(kv) for kv in keys]
+    context = shape((length, group), jnp.bfloat16)
+
+    def attend(slot, blocks, held, outs):
+        return call(
+            functools.partial(attend_kernel, len(blocks), head, len(held) > 0, len(outs) == 1),
+            outs,
+            (queries[slot], keys[slot], *blocks, *held),
+            [VM] * (2 + len(blocks) + len(held)),
+            8 * length * len(blocks) * length * group,
+            scratch=[
+                pltpu.VMEM((length, 128), jnp.bfloat16),
+                pltpu.VMEM((len(blocks) * length, 128), jnp.bfloat16),
+            ],
+        )
+
+    late = [keys[half - 1], keys[-1]]
+    state = shape((length, group), jnp.float32)
+    wide = shape((length, 2 * group), jnp.float32)
+    held = attend(0, keys[: half - 1] + keys[half:-1], [], [state, state, wide])
     contexts = []
     for j in range(half):
-        (context,) = call(
-            functools.partial(attend_kernel, half, j, head),
-            [shape((length, group), jnp.bfloat16)],
-            (queries[j], *keys),
-            [VM] * (1 + 2 * half),
-            8 * length * half * length * 2 * group,
-            scratch=[
-                pltpu.VMEM((length, 128), jnp.bfloat16),
-                pltpu.VMEM((2 * half * length, 128), jnp.bfloat16),
-            ],
-        )
-        contexts.append(send(context, [(b, a) for a, b in spread(j)]))
+        (mixed,) = attend(j, keys if j else late, () if j else held, [context])
+        contexts.append(send(mixed, [(b, a) for a, b in spread(j)]))
     base, kept_rows = call(
         functools.partial(first_kernel, half, lanes),
         [shape((length, model), jnp.float32), shape((group, model), jnp.bfloat16)],

time: 67.7 us -> 69.7 us (1.030)
  waiting for transfers between devices: 32.4 us -> 37 us
  starting transfers between devices: 21.3 us -> 17.9 us
    ppermute x3, waiting for transfers between devices: 16.5 us -> 21 us  [along(): lax.ppermute(value, 'fsdp', [(i, (i + 2 * by) % lanes) for i in range(lan...]
    ppermute x8, starting transfers between devices: 9.86 us -> 6.45 us  [partner(): return lax.ppermute(value, 'fsdp', [(i, i ^ 1) for i in range(lanes)])]
    pallas_call x9 -> x10, Pallas kernels: 13.7 us -> 14.2 us  [call(): pl.pallas_call(kernel, out_shape=outs, in_specs=specs, out_specs=[VM] * l...]
  transfers between devices with their start and end apart: 17 -> 17, of which waited for: 5 -> 5; matrix products, arithmetic and copies ran while one was open for 0% -> 0% of each run, Pallas kernels for 15% -> 16%
where the time goes in v5:
time: 69.7 us; the launch traced here: 69.3 us
  waiting for transfers between devices  37 us (53%)
  starting transfers between devices  17.9 us (26%)
  Pallas kernels  14.2 us (20%)
    ppermute x3, waiting for transfers between devices, along(): lax.ppermute(value, 'fsdp', [(i, (i + 2 * by) % lanes) for i in range(lan...  21 us
    ppermute x6, waiting for transfers between devices, send(): return lax.ppermute(value, ('ctx', 'fsdp'), pairs)  15.3 us
    pallas_call x10, Pallas kernels, call(): pl.pallas_call(kernel, out_shape=outs, in_specs=specs, out_specs=[VM] * l...  14.2 us
    ppermute x8, starting transfers between devices, partner(): return lax.ppermute(value, 'fsdp', [(i, i ^ 1) for i in range(lanes)])  6.45 us
    ppermute x6, starting transfers between devices, send(): return lax.ppermute(value, ('ctx', 'fsdp'), pairs)  6.28 us
    ppermute x3, starting transfers between devices, along(): lax.ppermute(value, 'fsdp', [(i, (i + 2 * by) % lanes) for i in range(lan...  5.18 us
  transfers between devices with their start and end apart: 17, of which 5 were waited for; matrix products, arithmetic and copies ran while one was open for 0% of the time, Pallas kernels for 16%

profile of v5, /device:TPU:0, one launch (start us, length us, event | category | flops | bytes accessed | tf_op | source)
XLA Modules:
  0.0 69.3 jit_solution(544010088620981174)
XLA Ops:
  0.0 0.0 copy-start
  0.0 2.0 %shard_map.91 = (bf16[256,512]{1,0:T(8,128)(2,1)S(1)}, bf16[256,1024]{1,0:T(8,128)(2,1)S(1)}, bf16[176,1024]{1,0:T(8,128)(2,1)S(1)}, bf16[112,1024]{1,0:T(8,128)(2,1)S(1)}) custom-call(bf16[256,1024]{1,0:T(8,128)(2,1)} %bitcast.3, s32[1,256]{1,0:T(1,128)} %refs_1_.3, s32[1,256]{1,0:T(1,128)} %refs_2_.3, bf16[64,1024]{1,0:T(8,128)(2,1)} %refs_3_.3, ...), custom_call_target="tpu_custom_call" | custom-call | flops 67108864 | bytes 3742720 | tf_op jit(solution)/shard_map/pallas_call | solution.py:39
  2.1 3.0 %collective-permute-start.2 = (bf16[256,1024]{1,0:T(8,128)(2,1)S(1)}, bf16[256,1024]{1,0:T(8,128)(2,1)S(1)}, u32[]{:S(2)}, u32[]{:S(2)}) collective-permute-start(bf16[256,1024]{1,0:T(8,128)(2,1)S(1)} %get-tuple-element.22.refs_3_.refs_4_), channel_id=1, source_target_pairs={{0,2},{1,3},{2,0},{3,1},{4,6},{5,7},{6,4},{7,5},{8,10},{9,11},{10,... | collective-permute-start | bytes 1572872 | tf_op jit(solution)/shard_map/ppermute | solution.py:282
  5.1 1.6 %collective-permute-start = (bf16[176,1024]{1,0:T(8,128)(2,1)S(1)}, bf16[176,1024]{1,0:T(8,128)(2,1)S(1)}, u32[]{:S(2)}, u32[]{:S(2)}) collective-permute-start(bf16[176,1024]{1,0:T(8,128)(2,1)S(1)} %get-tuple-element.20.one), channel_id=1, source_target_pairs={{0,4},{2,6},{4,0},{6,2},{9,13},{11,15},{13,9},{15,11},{1,8},{3,10}... | collective-permute-start | bytes 1081352 | tf_op jit(solution)/shard_map/ppermute | solution.py:279
  6.7 1.1 %collective-permute-start.3 = (bf16[256,1024]{1,0:T(8,128)(2,1)S(1)}, bf16[256,1024]{1,0:T(8,128)(2,1)S(1)}, u32[]{:S(2)}, u32[]{:S(2)}) collective-permute-start(bf16[256,1024]{1,0:T(8,128)(2,1)S(1)} %get-tuple-element.22.refs_3_.refs_4_), channel_id=1, source_target_pairs={{0,1},{1,0},{2,3},{3,2},{4,5},{5,4},{6,7},{7,6},{8,9},{9,8},{10,11... | collective-permute-start | bytes 1572872 | tf_op jit(solution)/shard_map/ppermute | solution.py:285
  7.8 9.2 %collective-permute-done.2.refs_4_.refs_5_ = bf16[256,1024]{1,0:T(8,128)(2,1)S(1)} collective-permute-done((bf16[256,1024]{1,0:T(8,128)(2,1)S(1)}, bf16[256,1024]{1,0:T(8,128)(2,1)S(1)}, u32[]{:S(2)}, u32[]{:S(2)}) %collective-permute-start.2) | collective-permute-done | bytes 524320 | tf_op jit(solution)/shard_map/ppermute | solution.py:282
  17.0 0.0 collective-permute-start.4
  17.0 1.8 %collective-permute-start.1 = (bf16[112,1024]{1,0:T(8,128)(2,1)S(1)}, bf16[112,1024]{1,0:T(8,128)(2,1)S(1)}, u32[]{:S(2)}, u32[]{:S(2)}) collective-permute-start(bf16[112,1024]{1,0:T(8,128)(2,1)S(1)} %get-tuple-element.21.refs_1_), channel_id=1, source_target_pairs={{0,4},{2,6},{4,0},{6,2},{9,13},{11,15},{13,9},{15,11},{1,8},{3,10}... | collective-permute-start | bytes 688136 | tf_op jit(solution)/shard_map/ppermute | solution.py:279
  18.8 0.0 collective-permute-done.two.refs_0_
  18.8 0.7 collective-permute-start.5
  19.5 6.6 %collective-permute-done.1.refs_2_ = bf16[112,1024]{1,0:T(8,128)(2,1)S(1)} collective-permute-done((bf16[112,1024]{1,0:T(8,128)(2,1)S(1)}, bf16[112,1024]{1,0:T(8,128)(2,1)S(1)}, u32[]{:S(2)}, u32[]{:S(2)}) %collective-permute-start.1) | collective-permute-done | bytes 229408 | tf_op jit(solution)/shard_map/ppermute | solution.py:279
  26.1 0.7 collective-permute-start.6
  26.8 0.0 copy-done
  26.8 1.8 %collective-permute-start.13 = (bf16[1024,256]{1,0:T(8,128)(2,1)S(1)}, bf16[1024,256]{1,0:T(8,128)(2,1)S(1)}, u32[]{:S(2)}, u32[]{:S(2)}) collective-permute-start(bf16[1024,256]{1,0:T(8,128)(2,1)S(1)} %copy-done), channel_id=1, source_target_pairs={{0,2},{1,3},{2,0},{3,1},{4,6},{5,7},{6,4},{7,5},{8,10},{9,11},{10,... | collective-permute-start | bytes 1572872 | tf_op jit(solution)/shard_map/ppermute | solution.py:282
  28.6 0.0 collective-permute-done.3.refs_5_.refs_6_
  28.6 0.4 collective-permute-start.7
  29.0 0.0 collective-permute-done.4.refs_6_.refs_7_
  29.0 0.7 %shard_map.93 = (bf16[272,1024]{1,0:T(8,128)(2,1)S(1)}, bf16[272,1024]{1,0:T(8,128)(2,1)S(1)}) custom-call(bf16[176,1024]{1,0:T(8,128)(2,1)S(1)} %shard_map.92.refs_0_, bf16[112,1024]{1,0:T(8,128)(2,1)S(1)} %get-tuple-element.21.refs_1_, bf16[112,1024]{1,0:T(8,128)(2,1)S(1)} %collective-permute-done.1.refs_2_, ...), custom_call_target="tpu_custom_call" | custom-call | flops 536870912 | bytes 4030464 | tf_op jit(solution)/shard_map/pallas_call | solution.py:39
  29.7 2.1 %collective-permute-start.11 = (bf16[272,1024]{1,0:T(8,128)(2,1)S(1)}, bf16[272,1024]{1,0:T(8,128)(2,1)S(1)}, u32[]{:S(2)}, u32[]{:S(2)}) collective-permute-start(bf16[272,1024]{1,0:T(8,128)(2,1)S(1)} %get-tuple-element.27.owner.refs_0_), channel_id=1, source_target_pairs={{0,1},{1,0},{2,3},{3,2},{4,5},{5,4},{6,7},{7,6},{8,9},{9,8},{10,11... | collective-permute-start | bytes 1671176 | tf_op jit(solution)/shard_map/ppermute | solution.py:285
  31.8 0.0 collective-permute-done.6.refs_3_
  31.8 0.0 collective-permute-done.5.refs_1_
  31.8 0.7 %shard_map.94 = (bf16[272,1024]{1,0:T(8,128)(2,1)S(1)}, bf16[272,1024]{1,0:T(8,128)(2,1)S(1)}) custom-call(bf16[176,1024]{1,0:T(8,128)(2,1)S(1)} %collective-permute-done.two.refs_0_, bf16[176,1024]{1,0:T(8,128)(2,1)S(1)} %collective-permute-done.5.refs_1_, bf16[112,1024]{1,0:T(8,128)(2,1)S(1)} %collective-permute-done.1.refs_2_, ...), custom_call_target="tpu_custom_call" | custom-call | flops 536870912 | bytes 4390912 | tf_op jit(solution)/shard_map/pallas_call | solution.py:39
  32.6 1.3 %collective-permute-start.10 = (bf16[272,1024]{1,0:T(8,128)(2,1)S(1)}, bf16[272,1024]{1,0:T(8,128)(2,1)S(1)}, u32[]{:S(2)}, u32[]{:S(2)}) collective-permute-start(bf16[272,1024]{1,0:T(8,128)(2,1)S(1)} %get-tuple-element.28.refs_0_.owner.refs_1_), channel_id=1, source_target_pairs={{0,1},{1,0},{2,3},{3,2},{4,5},{5,4},{6,7},{7,6},{8,9},{9,8},{10,11... | collective-permute-start | bytes 1671176 | tf_op jit(solution)/shard_map/ppermute | solution.py:285
  33.8 0.1 collective-permute-start.8
  33.9 11.8 %collective-permute-done.7.refs_3_ = bf16[256,512]{1,0:T(8,128)(2,1)S(1)} collective-permute-done((bf16[256,512]{1,0:T(8,128)(2,1)S(1)}, bf16[256,512]{1,0:T(8,128)(2,1)S(1)}, u32[]{:S(2)}, u32[]{:S(2)}) %collective-permute-start.7) | collective-permute-done | bytes 262176 | tf_op jit(solution)/shard_map/ppermute | solution.py:282
  45.7 1.4 %collective-permute-start.9 = (bf16[256,512]{1,0:T(8,128)(2,1)S(1)}, bf16[256,512]{1,0:T(8,128)(2,1)S(1)}, u32[]{:S(2)}, u32[]{:S(2)}) collective-permute-start(bf16[256,512]{1,0:T(8,128)(2,1)S(1)} %collective-permute-done.7.refs_3_), channel_id=1, source_target_pairs={{0,1},{1,0},{2,3},{3,2},{4,5},{5,4},{6,7},{7,6},{8,9},{9,8},{10,11... | collective-permute-start | bytes 786440 | tf_op jit(solution)/shard_map/ppermute | solution.py:285
  47.1 0.0 collective-permute-done.8.refs_4_
  47.1 0.0 collective-permute-start.14
  47.1 0.0 collective-permute-done.13.refs_7_
  47.1 0.5 collective-permute-start.15
  47.6 0.6 collective-permute-done.9.refs_5_
  48.2 0.7 %shard_map.95 = (bf16[256,512]{1,0:T(8,128)(2,1)S(1)}, bf16[256,512]{1,0:T(8,128)(2,1)S(1)}) custom-call(bf16[272,1024]{1,0:T(8,128)(2,1)S(1)} %get-tuple-element.23.refs_0_, bf16[272,1024]{1,0:T(8,128)(2,1)S(1)} %get-tuple-element.24.refs_1_, bf16[256,512]{1,0:T(8,128)(2,1)S(1)} %get-tuple-element.25.refs_2_, ...), custom_call_target="tpu_custom_call" | custom-call | flops 536870912 | bytes 2686976 | tf_op jit(solution)/shard_map/pallas_call | solution.py:39
  49.0 0.0 collective-permute-done.11.refs_1_.refs_2_
  49.0 1.7 %shard_map.96 = (f32[256,512]{1,0:T(8,128)S(1)}, f32[256,512]{1,0:T(8,128)S(1)}, f32[256,1024]{1,0:T(8,128)S(1)}) custom-call(bf16[256,512]{1,0:T(8,128)(2,1)S(1)} %get-tuple-element.26.q, bf16[272,1024]{1,0:T(8,128)(2,1)S(1)} %get-tuple-element.27.owner.refs_0_, bf16[272,1024]{1,0:T(8,128)(2,1)S(1)} %get-tuple-element.27.owner.refs_0_, ...), custom_call_target="tpu_custom_call" | custom-call | flops 536870912 | bytes 4030464 | tf_op jit(solution)/shard_map/pallas_call | solution.py:39
  50.7 0.0 collective-permute-done.10.refs_1_.refs_3_
  50.7 1.8 %shard_map.97 = bf16[256,512]{1,0:T(8,128)(2,1)S(1)} custom-call(bf16[256,512]{1,0:T(8,128)(2,1)S(1)} %get-tuple-element.26.q, bf16[272,1024]{1,0:T(8,128)(2,1)S(1)} %get-tuple-element.27.owner.refs_0_, bf16[272,1024]{1,0:T(8,128)(2,1)S(1)} %get-tuple-element.28.refs_0_.owner.refs_1_, bf16[272,1024]{1,0:T(8,128)(2,1)S(1)} %collective-permute-done.10.refs_1_.refs_3_, ...), custom_call_target="tpu_custom_call" | custom-call | flops 536870912 | bytes 4292608 | tf_op jit(solution)/shard_map/pallas_call | solution.py:39
  52.6 0.7 collective-permute-start.12
  53.3 3.0 %shard_map.99 = bf16[256,512]{1,0:T(8,128)(2,1)S(1)} custom-call(bf16[256,512]{1,0:T(8,128)(2,1)S(1)} %get-tuple-element.33.q, bf16[272,1024]{1,0:T(8,128)(2,1)S(1)} %get-tuple-element.28.refs_0_.owner.refs_1_, bf16[272,1024]{1,0:T(8,128)(2,1)S(1)} %get-tuple-element.27.owner.refs_0_, bf16[272,1024]{1,0:T(8,128)(2,1)S(1)} %get-tuple-element.28.refs_0_.owner.refs_1_, ...), custom_call_target="tpu_custom_call" | custom-call | flops 1073741824 | bytes 3309568 | tf_op jit(solution)/shard_map/pallas_call | solution.py:39
  56.3 0.9 %collective-permute-start.16 = (bf16[256,512]{1,0:T(8,128)(2,1)S(1)}, bf16[256,512]{1,0:T(8,128)(2,1)S(1)}, u32[]{:S(2)}, u32[]{:S(2)}) collective-permute-start(bf16[256,512]{1,0:T(8,128)(2,1)S(1)} %shard_map.99), channel_id=1, source_target_pairs={{4,0},{12,1},{6,2},{14,3},{0,4},{8,5},{2,6},{10,7},{5,8},{13,9},{7... | collective-permute-start | bytes 786440 | tf_op jit(solution)/shard_map/ppermute | solution.py:279
  57.2 0.0 collective-permute-done.14.refs_8_
  57.2 0.0 collective-permute-done.15.refs_9_
  57.2 0.0 collective-permute-done.12.refs_5_
  57.2 2.1 %shard_map.98 = (f32[256,1024]{1,0:T(8,128)S(1)}, bf16[512,1024]{1,0:T(8,128)(2,1)S(1)}) custom-call(bf16[256,1024]{1,0:T(8,128)(2,1)} %bitcast.4, s32[1,256]{1,0:T(1,128)} %refs_1_.3, s32[1,256]{1,0:T(1,128)} %refs_2_.3, bf16[64,1024]{1,0:T(8,128)(2,1)} %refs_3_.3, bf16[64,1024]{1,0:T(8,128)(2,1)} %refs_4_.3, ...), custom_call_target="tpu_custom_call" | custom-call | flops 268435456 | bytes 5244928 | tf_op jit(solution)/shard_map/pallas_call | solution.py:39
  59.3 8.8 %collective-permute-done.16.context = bf16[256,512]{1,0:T(8,128)(2,1)S(1)} collective-permute-done((bf16[256,512]{1,0:T(8,128)(2,1)S(1)}, bf16[256,512]{1,0:T(8,128)(2,1)S(1)}, u32[]{:S(2)}, u32[]{:S(2)}) %collective-permute-start.16) | collective-permute-done | bytes 262176 | tf_op jit(solution)/shard_map/ppermute | solution.py:279
  68.0 1.2 %shard_map.100 = bf16[256,1024]{1,0:T(8,128)(2,1)} custom-call(f32[256,1024]{1,0:T(8,128)S(1)} %get-tuple-element.32.base, bf16[256,512]{1,0:T(8,128)(2,1)S(1)} %collective-permute-done.16.context, bf16[512,1024]{1,0:T(8,128)(2,1)S(1)} %get-tuple-element.34.weight), custom_call_target="tpu_custom_call" | custom-call | flops 268435456 | bytes 2883584 | tf_op jit(solution)/shard_map/pallas_call | solution.py:39
  (1 shorter events, 0.0 us)
Async XLA Ops:
  0.0 26.8 %copy-start = (bf16[1024,256]{1,0:T(8,128)(2,1)S(1)}, bf16[1024,256]{1,0:T(8,128)(2,1)}, u32[]{:S(2)}) copy-start(bf16[1024,256]{1,0:T(8,128)(2,1)} %refs_6_.1) | copy-start | bytes 1572868
  2.1 15.0 %collective-permute-start.2 = (bf16[256,1024]{1,0:T(8,128)(2,1)S(1)}, bf16[256,1024]{1,0:T(8,128)(2,1)S(1)}, u32[]{:S(2)}, u32[]{:S(2)}) collective-permute-start(bf16[256,1024]{1,0:T(8,128)(2,1)S(1)} %get-tuple-element.22.refs_3_.refs_4_), channel_id=1, source_target_pairs={{0,2},{1,3},{2,0},{3,1},{4,6},{5,7},{6,4},{7,5},{8,10},{9,11},{10,... | collective-permute-start | bytes 1572872 | tf_op jit(solution)/shard_map/ppermute | solution.py:282
  5.1 13.8 %collective-permute-start = (bf16[176,1024]{1,0:T(8,128)(2,1)S(1)}, bf16[176,1024]{1,0:T(8,128)(2,1)S(1)}, u32[]{:S(2)}, u32[]{:S(2)}) collective-permute-start(bf16[176,1024]{1,0:T(8,128)(2,1)S(1)} %get-tuple-element.20.one), channel_id=1, source_target_pairs={{0,4},{2,6},{4,0},{6,2},{9,13},{11,15},{13,9},{15,11},{1,8},{3,10}... | collective-permute-start | bytes 1081352 | tf_op jit(solution)/shard_map/ppermute | solution.py:279
  6.7 22.0 %collective-permute-start.3 = (bf16[256,1024]{1,0:T(8,128)(2,1)S(1)}, bf16[256,1024]{1,0:T(8,128)(2,1)S(1)}, u32[]{:S(2)}, u32[]{:S(2)}) collective-permute-start(bf16[256,1024]{1,0:T(8,128)(2,1)S(1)} %get-tuple-element.22.refs_3_.refs_4_), channel_id=1, source_target_pairs={{0,1},{1,0},{2,3},{3,2},{4,5},{5,4},{6,7},{7,6},{8,9},{9,8},{10,11... | collective-permute-start | bytes 1572872 | tf_op jit(solution)/shard_map/ppermute | solution.py:285
  17.0 12.0 %collective-permute-start.4 = (bf16[256,1024]{1,0:T(8,128)(2,1)S(1)}, bf16[256,1024]{1,0:T(8,128)(2,1)S(1)}, u32[]{:S(2)}, u32[]{:S(2)}) collective-permute-start(bf16[256,1024]{1,0:T(8,128)(2,1)S(1)} %collective-permute-done.2.refs_4_.refs_5_), channel_id=1, source_target_pairs={{0,1},{1,0},{2,3},{3,2},{4,5},{5,4},{6,7},{7,6},{8,9},{9,8},{10,11... | collective-permute-start | bytes 1572872 | tf_op jit(solution)/shard_map/ppermute | solution.py:285
  17.0 9.1 %collective-permute-start.1 = (bf16[112,1024]{1,0:T(8,128)(2,1)S(1)}, bf16[112,1024]{1,0:T(8,128)(2,1)S(1)}, u32[]{:S(2)}, u32[]{:S(2)}) collective-permute-start(bf16[112,1024]{1,0:T(8,128)(2,1)S(1)} %get-tuple-element.21.refs_1_), channel_id=1, source_target_pairs={{0,4},{2,6},{4,0},{6,2},{9,13},{11,15},{13,9},{15,11},{1,8},{3,10}... | collective-permute-start | bytes 688136 | tf_op jit(solution)/shard_map/ppermute | solution.py:279
  18.8 13.0 %collective-permute-start.5 = (bf16[176,1024]{1,0:T(8,128)(2,1)S(1)}, bf16[176,1024]{1,0:T(8,128)(2,1)S(1)}, u32[]{:S(2)}, u32[]{:S(2)}) collective-permute-start(bf16[176,1024]{1,0:T(8,128)(2,1)S(1)} %collective-permute-done.two.refs_0_), channel_id=1, source_target_pairs={{1,5},{3,7},{5,1},{7,3},{8,12},{10,14},{12,8},{14,10},{17,21},{19,... | collective-permute-start | bytes 1081352 | tf_op jit(solution)/shard_map/ppermute | solution.py:279
  26.1 5.7 %collective-permute-start.6 = (bf16[112,1024]{1,0:T(8,128)(2,1)S(1)}, bf16[112,1024]{1,0:T(8,128)(2,1)S(1)}, u32[]{:S(2)}, u32[]{:S(2)}) collective-permute-start(bf16[112,1024]{1,0:T(8,128)(2,1)S(1)} %collective-permute-done.1.refs_2_), channel_id=1, source_target_pairs={{1,5},{3,7},{5,1},{7,3},{8,12},{10,14},{12,8},{14,10},{17,21},{19,... | collective-permute-start | bytes 688136 | tf_op jit(solution)/shard_map/ppermute | solution.py:279
  26.8 20.3 %collective-permute-start.13 = (bf16[1024,256]{1,0:T(8,128)(2,1)S(1)}, bf16[1024,256]{1,0:T(8,128)(2,1)S(1)}, u32[]{:S(2)}, u32[]{:S(2)}) collective-permute-start(bf16[1024,256]{1,0:T(8,128)(2,1)S(1)} %copy-done), channel_id=1, source_target_pairs={{0,2},{1,3},{2,0},{3,1},{4,6},{5,7},{6,4},{7,5},{8,10},{9,11},{10,... | collective-permute-start | bytes 1572872 | tf_op jit(solution)/shard_map/ppermute | solution.py:282
  28.6 17.0 %collective-permute-start.7 = (bf16[256,512]{1,0:T(8,128)(2,1)S(1)}, bf16[256,512]{1,0:T(8,128)(2,1)S(1)}, u32[]{:S(2)}, u32[]{:S(2)}) collective-permute-start(bf16[256,512]{1,0:T(8,128)(2,1)S(1)} %get-tuple-element.25.refs_2_), channel_id=1, source_target_pairs={{0,2},{1,3},{2,0},{3,1},{4,6},{5,7},{6,4},{7,5},{8,10},{9,11},{10,... | collective-permute-start | bytes 786440 | tf_op jit(solution)/shard_map/ppermute | solution.py:282
  29.7 19.2 %collective-permute-start.11 = (bf16[272,1024]{1,0:T(8,128)(2,1)S(1)}, bf16[272,1024]{1,0:T(8,128)(2,1)S(1)}, u32[]{:S(2)}, u32[]{:S(2)}) collective-permute-start(bf16[272,1024]{1,0:T(8,128)(2,1)S(1)} %get-tuple-element.27.owner.refs_0_), channel_id=1, source_target_pairs={{0,1},{1,0},{2,3},{3,2},{4,5},{5,4},{6,7},{7,6},{8,9},{9,8},{10,11... | collective-permute-start | bytes 1671176 | tf_op jit(solution)/shard_map/ppermute | solution.py:285
  32.6 18.2 %collective-permute-start.10 = (bf16[272,1024]{1,0:T(8,128)(2,1)S(1)}, bf16[272,1024]{1,0:T(8,128)(2,1)S(1)}, u32[]{:S(2)}, u32[]{:S(2)}) collective-permute-start(bf16[272,1024]{1,0:T(8,128)(2,1)S(1)} %get-tuple-element.28.refs_0_.owner.refs_1_), channel_id=1, source_target_pairs={{0,1},{1,0},{2,3},{3,2},{4,5},{5,4},{6,7},{7,6},{8,9},{9,8},{10,11... | collective-permute-start | bytes 1671176 | tf_op jit(solution)/shard_map/ppermute | solution.py:285
  33.8 13.3 %collective-permute-start.8 = (bf16[256,512]{1,0:T(8,128)(2,1)S(1)}, bf16[256,512]{1,0:T(8,128)(2,1)S(1)}, u32[]{:S(2)}, u32[]{:S(2)}) collective-permute-start(bf16[256,512]{1,0:T(8,128)(2,1)S(1)} %get-tuple-element.25.refs_2_), channel_id=1, source_target_pairs={{0,1},{1,0},{2,3},{3,2},{4,5},{5,4},{6,7},{7,6},{8,9},{9,8},{10,11... | collective-permute-start | bytes 786440 | tf_op jit(solution)/shard_map/ppermute | solution.py:285
  45.7 2.6 %collective-permute-start.9 = (bf16[256,512]{1,0:T(8,128)(2,1)S(1)}, bf16[256,512]{1,0:T(8,128)(2,1)S(1)}, u32[]{:S(2)}, u32[]{:S(2)}) collective-permute-start(bf16[256,512]{1,0:T(8,128)(2,1)S(1)} %collective-permute-done.7.refs_3_), channel_id=1, source_target_pairs={{0,1},{1,0},{2,3},{3,2},{4,5},{5,4},{6,7},{7,6},{8,9},{9,8},{10,11... | collective-permute-start | bytes 786440 | tf_op jit(solution)/shard_map/ppermute | solution.py:285
  47.1 10.1 %collective-permute-start.14 = (bf16[1024,256]{1,0:T(8,128)(2,1)S(1)}, bf16[1024,256]{1,0:T(8,128)(2,1)S(1)}, u32[]{:S(2)}, u32[]{:S(2)}) collective-permute-start(bf16[1024,256]{1,0:T(8,128)(2,1)S(1)} %copy-done), channel_id=1, source_target_pairs={{0,1},{1,0},{2,3},{3,2},{4,5},{5,4},{6,7},{7,6},{8,9},{9,8},{10,11... | collective-permute-start | bytes 1572872 | tf_op jit(solution)/shard_map/ppermute | solution.py:285
  47.1 10.1 %collective-permute-start.15 = (bf16[1024,256]{1,0:T(8,128)(2,1)S(1)}, bf16[1024,256]{1,0:T(8,128)(2,1)S(1)}, u32[]{:S(2)}, u32[]{:S(2)}) collective-permute-start(bf16[1024,256]{1,0:T(8,128)(2,1)S(1)} %collective-permute-done.13.refs_7_), channel_id=1, source_target_pairs={{0,1},{1,0},{2,3},{3,2},{4,5},{5,4},{6,7},{7,6},{8,9},{9,8},{10,11... | collective-permute-start | bytes 1572872 | tf_op jit(solution)/shard_map/ppermute | solution.py:285
  52.6 4.6 %collective-permute-start.12 = (bf16[256,512]{1,0:T(8,128)(2,1)S(1)}, bf16[256,512]{1,0:T(8,128)(2,1)S(1)}, u32[]{:S(2)}, u32[]{:S(2)}) collective-permute-start(bf16[256,512]{1,0:T(8,128)(2,1)S(1)} %shard_map.97), channel_id=1, source_target_pairs={{0,0},{8,1},{2,2},{10,3},{4,4},{12,5},{6,6},{14,7},{1,8},{9,9},{3,... | collective-permute-start | bytes 786440 | tf_op jit(solution)/shard_map/ppermute | solution.py:279
  56.3 11.7 %collective-permute-start.16 = (bf16[256,512]{1,0:T(8,128)(2,1)S(1)}, bf16[256,512]{1,0:T(8,128)(2,1)S(1)}, u32[]{:S(2)}, u32[]{:S(2)}) collective-permute-start(bf16[256,512]{1,0:T(8,128)(2,1)S(1)} %shard_map.99), channel_id=1, source_target_pairs={{4,0},{12,1},{6,2},{14,3},{0,4},{8,5},{2,6},{10,7},{5,8},{13,9},{7... | collective-permute-start | bytes 786440 | tf_op jit(solution)/shard_map/ppermute | solution.py:279
